TPU v7x, 256 devices: a whole 4x4x8 slice. The times are simulated.
256 devices in a mesh: member: 16 (over y, x_hi, core), dp: 16 (over z, x_lo).
Axes of the slice: x: 4 (x_hi: 2, x_lo: 2; x = x_hi * 2 + x_lo), y: 4, z: 8, core: 2. Of those that a mesh axis runs over, the one named last changes fastest.
Arguments:
- teacher_tokens: bfloat16 [2752, 1536], P('dp'), may hold values from -100 to 100
- teacher_qkv: bfloat16 [16, 1536, 4608], P('member', None, 'dp'), may hold values from -0.15625 to 0.15625
- student_tokens: bfloat16 [2752, 1024], P('dp'), may hold values from -6 to 6
- student_gain: float32 [1024], replicated, may hold values from 0.1 to 1.9
- w_up: bfloat16 [1024, 4096], P(None, 'member'), may hold values from -0.1875 to 0.1875
- w_down: bfloat16 [1024, 4096], P(None, 'member'), may hold values from -0.09375 to 0.09375
- w_head: bfloat16 [1024, 1536], P(None, 'member'), may hold values from -0.1875 to 0.1875
Outputs:
- grad_up: float32 [1024, 4096], P('dp', 'member')
- grad_down: float32 [1024, 4096], P('dp', 'member')
- grad_head: float32 [1024, 1536], P('dp', 'member')
All inputs are finite; a program needn't handle non-finite values.
Results may differ from a plain program's by a relative error of at most 0.0055.
Values may be sent and summed in bfloat16 or wider, within the bound.
No kernel may reach another device: no remote copies, remote signals or barrier semaphores. Data moves between devices by JAX's collectives and lax.ppermute only.
A program may use at most 192 MiB of HBM per device.

v0:
```python
from functools import partial
import math

import jax
import jax.numpy as jnp
from jax import lax
from jax.sharding import PartitionSpec as P

VALID = 1370
IMAGES = 2


def body(teacher_tokens, teacher_qkv, student_tokens, student_gain, w_up, w_down, w_head):
    tok_rows = teacher_tokens.shape[0]
    feat_width = teacher_tokens.shape[1]
    head_count = feat_width // 64
    own_columns = teacher_qkv[0]
    query_slots = lax.axis_index("dp") * tok_rows + jnp.arange(tok_rows, dtype=jnp.int32)
    query_image = query_slots % IMAGES
    real_query = query_slots // IMAGES < VALID
    projected = jnp.dot(
        teacher_tokens,
        lax.all_gather(own_columns, "dp", axis=1, tiled=True),
        preferred_element_type=jnp.float32,
    ).astype(jnp.bfloat16)
    queries = projected[:, :feat_width].reshape(tok_rows, head_count, 64)
    keys_local = projected[:, feat_width : 2 * feat_width]
    values_local = projected[:, 2 * feat_width :]
    row_max = jnp.full((head_count, tok_rows), -1e30, jnp.float32)
    weighted = jnp.zeros((tok_rows, head_count, 64), jnp.float32)
    key_heads = lax.all_gather(keys_local, "dp", axis=0, tiled=True).reshape(-1, head_count, 64)
    value_heads = lax.all_gather(values_local, "dp", axis=0, tiled=True).reshape(-1, head_count, 64)
    key_slots = jnp.arange(key_heads.shape[0], dtype=jnp.int32)
    allowed = (query_image[:, None] == (key_slots % IMAGES)[None, :]) & (
        key_slots // IMAGES < VALID
    )[None, :]
    scores = (
        jnp.einsum("qhd,khd->hqk", queries, key_heads, preferred_element_type=jnp.float32) * 0.125
    )
    scores = jnp.where(allowed[None], scores, -1e30)
    new_max = jnp.maximum(row_max, jnp.max(scores, axis=-1))
    factor = jnp.exp(row_max - new_max)
    expsc = jnp.where(allowed[None], jnp.exp(scores - new_max[:, :, None]), 0.0)
    denom_sum = jnp.sum(expsc, axis=-1)
    update = jnp.einsum(
        "hqk,khd->qhd", expsc.astype(jnp.bfloat16), value_heads, preferred_element_type=jnp.float32
    )
    weighted = weighted * factor.T[:, :, None] + update
    row_max, denom_sum, weighted = (new_max, denom_sum, weighted)
    context = (weighted / denom_sum.T[:, :, None]).reshape(tok_rows, feat_width)
    member_slot = lax.axis_index("member")
    share_width = feat_width // lax.axis_size("member")
    summed = lax.psum(context, "member")
    row_mean = jnp.mean(summed, axis=-1, keepdims=True)
    mean_square = jnp.mean(summed * summed, axis=-1, keepdims=True)
    full_target = (summed - row_mean) * lax.rsqrt(mean_square - row_mean * row_mean + 1e-06)
    target = lax.dynamic_slice_in_dim(full_target, member_slot * share_width, share_width, 1)
    inputs = student_tokens.astype(jnp.float32)
    in_mean = jnp.mean(inputs, axis=-1, keepdims=True)
    in_var = jnp.mean((inputs - in_mean) ** 2, axis=-1, keepdims=True)
    normed = ((inputs - in_mean) * lax.rsqrt(in_var + 1e-06) * student_gain).astype(jnp.bfloat16)
    pre = jnp.dot(normed, w_up, preferred_element_type=jnp.float32)
    gelu_tanh = partial(jax.nn.gelu, approximate=True)
    hidden = gelu_tanh(pre).astype(jnp.bfloat16)
    branch_part = lax.dot_general(
        hidden, w_down, (((1,), (1,)), ((), ())), preferred_element_type=jnp.float32
    )
    student_out = (inputs + lax.psum(branch_part, "member")).astype(jnp.bfloat16)
    pred = jnp.dot(student_out, w_head, preferred_element_type=jnp.float32)
    pred_grad = jnp.where(
        real_query[:, None], (pred - target) / math.sqrt(IMAGES * VALID), 0.0
    ).astype(jnp.bfloat16)
    grad_head = lax.dot_general(
        student_out, pred_grad, (((0,), (0,)), ((), ())), preferred_element_type=jnp.float32
    )
    out_part = lax.dot_general(
        pred_grad, w_head, (((1,), (1,)), ((), ())), preferred_element_type=jnp.float32
    )
    out_grad = lax.psum(out_part, "member").astype(jnp.bfloat16)
    grad_down = lax.dot_general(
        out_grad, hidden, (((0,), (0,)), ((), ())), preferred_element_type=jnp.float32
    )
    hidden_grad = jnp.dot(out_grad, w_down, preferred_element_type=jnp.float32)
    _, pullback = jax.vjp(gelu_tanh, pre)
    pre_grad = pullback(hidden_grad)[0].astype(jnp.bfloat16)
    grad_up = lax.dot_general(
        normed, pre_grad, (((0,), (0,)), ((), ())), preferred_element_type=jnp.float32
    )
    grad_up, grad_down, grad_head = (
        lax.psum_scatter(grad_up, "dp", scatter_dimension=0, tiled=True),
        lax.psum_scatter(grad_down, "dp", scatter_dimension=0, tiled=True),
        lax.psum_scatter(grad_head, "dp", scatter_dimension=0, tiled=True),
    )
    return (grad_up, grad_down, grad_head)


def solution(mesh):
    in_specs = (
        P("dp", None),
        P("member", None, "dp"),
        P("dp", None),
        P(),
        P(None, "member"),
        P(None, "member"),
        P(None, "member"),
    )
    out_specs = (P("dp", "member"), P("dp", "member"), P("dp", "member"))
    return jax.shard_map(body, mesh=mesh, in_specs=in_specs, out_specs=out_specs, check_vma=False)
```

profile of v0, /device:TPU:8, one launch (start us, length us, event | category | flops | bytes accessed | tf_op | source)
XLA Modules:
  0.0 1197.4 jit_solution(361960012682249767)
XLA Ops:
  7.3 0.7 all-gather.7.cloned.1.call-update
  8.0 303.0 %all-gather.7.cloned.1.call-done = bf16[1,1536,4608]{1,2,0:T(8,128)(2,1)} async-done(((bf16[1,1536,288]{1,2,0:T(8,128)(2,1)}), bf16[1,1536,4608]{1,2,0:T(8,128)(2,1)}) %all-gather.7.cloned.1.call-update) | async-done | bytes 14155792 | tf_op jit(solution)/shard_map/all_gather | solution.py:23
  311.0 9.7 fusion.8
  320.7 1.2 slice_bitcast_fusion.1
  322.0 0.7 all-gather.9.cloned.1.call-update
  322.8 0.1 convert_reduce_fusion
  322.9 0.2 fusion.19
  323.2 0.3 fusion.71
  323.5 1.2 fusion.69
  324.7 0.4 compare_and_fusion
  325.1 0.3 copy.18
  325.4 186.0 %all-gather.11.cloned.1.call-done = bf16[16,172,1536]{2,1,0:T(8,128)(2,1)} async-done(((bf16[1,172,1536]{2,1,0:T(8,128)(2,1)}), bf16[16,172,1536]{2,1,0:T(8,128)(2,1)}) %all-gather.11.cloned.1.call-update) | async-done | bytes 8454160 | tf_op jit(solution)/shard_map/all_gather | solution.py:32
  511.4 17.4 %copy.20 = bf16[16,172,1536]{1,0,2:T(8,128)(2,1)} copy(bf16[16,172,1536]{2,1,0:T(8,128)(2,1)} %all-gather.11.cloned.1.call-done) | data formatting | bytes 16908288 | tf_op jit(solution)/shard_map/all_gather | solution.py:32
  528.8 22.6 %reshape.154 = bf16[2752,24,64]{0,2,1:T(8,128)(2,1)} reshape(bf16[16,172,1536]{1,0,2:T(8,128)(2,1)} %copy.20) | data formatting | bytes 16908288 | tf_op jit(solution)/shard_map/reshape | solution.py:32
  551.4 150.4 %all-gather.9.cloned.1.call-done = bf16[16,172,1536]{2,1,0:T(8,128)(2,1)} async-done(((bf16[1,172,1536]{2,1,0:T(8,128)(2,1)}), bf16[16,172,1536]{2,1,0:T(8,128)(2,1)}) %all-gather.9.cloned.1.call-update) | async-done | bytes 8454160 | tf_op jit(solution)/shard_map/all_gather | solution.py:31
  701.8 17.4 %copy.19 = bf16[16,172,1536]{1,0,2:T(8,128)(2,1)} copy(bf16[16,172,1536]{2,1,0:T(8,128)(2,1)} %all-gather.9.cloned.1.call-done) | data formatting | bytes 16908288 | tf_op jit(solution)/shard_map/all_gather | solution.py:31
  719.2 22.6 %reshape.153 = bf16[2752,24,64]{0,2,1:T(8,128)(2,1)} reshape(bf16[16,172,1536]{1,0,2:T(8,128)(2,1)} %copy.19) | data formatting | bytes 16908288 | tf_op jit(solution)/shard_map/reshape | solution.py:31
  741.8 21.7 %fusion = (f32[24,172]{1,0:T(8,128)S(1)}, f32[24,172,2752]{2,1,0:T(8,128)}) fusion(pred[172,2752]{1,0:T(8,128)(4,1)S(1)} %compare_and_fusion, bf16[172,24,64]{0,2,1:T(8,128)(2,1)S(1)} %bitcast.35, bf16[2752,24,64]{0,2,1:T(8,128)(2,1)} %reshape.153), kind=kOutput, calls=%fused_computation.2 | convolution fusion | flops 1488189440 | bytes 54913408 | tf_op jit(solution)/shard_map/qhd,khd->hqk/dot_general | solution.py:38
  763.5 22.9 %fusion.1 = f32[24,172]{1,0:T(8,128)S(1)} fusion(f32[24,172,2752]{2,1,0:T(8,128)} %get-tuple-element.15, f32[24,172]{1,0:T(8,128)S(1)} %get-tuple-element.11, pred[172,2752]{1,0:T(8,128)(4,1)S(1)} %compare_and_fusion), kind=kLoop, calls=%fused_computation.3 | loop fusion | flops 56797152 | bytes 45947392 | tf_op jit(solution)/shard_map/reduce_sum | solution.py:44
  786.4 20.8 %fusion.11 = f32[172,24,64]{0,2,1:T(8,128)S(1)} fusion(bf16[2752,24,64]{0,2,1:T(8,128)(2,1)} %reshape.154, f32[24,172,2752]{2,1,0:T(8,128)} %get-tuple-element.15, f32[24,172]{1,0:T(8,128)S(1)} %get-tuple-element.11, pred[172,2752]{1,0:T(8,128)(4,1)S(1)} %compare_and_fusion, f32[172,24]{0,1:T(8,128)S(1)} %bitcast.37, f32[172,24]{0,1:T(8,128)S(1)} %get-tuple-element.10), kind=kOutput, calls=%fused_computation.12 | convolution fusion | flops 1511442432 | bytes 55474816 | tf_op jit(solution)/shard_map/hqk,khd->qhd/dot_general | solution.py:45
  807.3 1.5 copy.21
  808.8 144.0 %all-reduce.4.cloned.1.call-done = (f32[172,1536]{1,0:T(8,128)}, f32[172,1024]{1,0:T(8,128)}) async-done(((f32[172,1536]{1,0:T(8,128)}, f32[172,1024]{1,0:T(8,128)}), (f32[172,1536]{1,0:T(8,128)}, f32[172,1024]{1,0:T(8,128)})) %all-reduce.4.cloned.1.call-update) | async-done | bytes 1761296 | tf_op jit(solution)/shard_map/psum | solution.py:53
  952.9 1.5 fusion.73
  954.3 1.4 fusion.16
  955.8 0.2 fusion.74
  956.0 2.3 fusion.66
  958.3 0.0 reduce-scatter.4.cloned.1.call-start
  958.4 77.2 %all-reduce.5 = bf16[172,1024]{1,0:T(8,128)(2,1)S(1)} all-reduce(f32[172,1024]{1,0:T(8,128)S(1)} %fusion.74), channel_id=1, replica_groups=mesh['member'=16,'dp'=16] {'member'}, use_global_device_ids=true, to_apply=%region_8.9 | all-reduce | flops 176128 | bytes 1056768 | tf_op jit(solution)/shard_map/psum | solution.py:79
  1035.6 2.8 fusion.37
  1038.4 1.4 fusion.30
  1039.8 76.7 %reduce-scatter.4.cloned.1.call-done = f32[64,256]{1,0:T(8,128)} async-done(((f32[1024,256]{1,0:T(8,128)}), f32[64,256]{1,0:T(8,128)}) %reduce-scatter.4.cloned.1.call-update) | async-done | bytes 65552 | tf_op jit(solution)/shard_map/reduce_scatter | solution.py:90
  1116.6 74.0 %reduce-scatter.6.cloned.1.call-done = f32[64,256]{1,0:T(8,128)} async-done(((f32[1024,256]{1,0:T(8,128)}), f32[64,256]{1,0:T(8,128)}) %reduce-scatter.6.cloned.1.call-update) | async-done | bytes 65552 | tf_op jit(solution)/shard_map/reduce_scatter | solution.py:91
  (34 shorter events, 0.5 us)
Async XLA Ops:
  7.2 303.8 %copy-start = (bf16[172,1536]{1,0:T(8,128)(2,1)S(1)}, bf16[172,1536]{1,0:T(8,128)(2,1)}, u32[]{:S(2)}) copy-start(bf16[172,1536]{1,0:T(8,128)(2,1)} %param.7) | copy-start | bytes 1585156
  7.2 315.6 %copy-start.2 = (bf16[172,1024]{1,0:T(8,128)(2,1)S(1)}, bf16[172,1024]{1,0:T(8,128)(2,1)}, u32[]{:S(2)}) copy-start(bf16[172,1024]{1,0:T(8,128)(2,1)} %param.9) | copy-start | bytes 1056772
  7.2 316.0 %copy-start.5 = (bf16[1024,256]{1,0:T(8,128)(2,1)S(1)}, bf16[1024,256]{1,0:T(8,128)(2,1)}, u32[]{:S(2)}) copy-start(bf16[1024,256]{1,0:T(8,128)(2,1)} %param.11) | copy-start | bytes 1572868
  7.2 316.0 %copy-start.6 = (f32[1024]{0:T(1024)S(1)}, f32[1024]{0:T(1024)}, u32[]{:S(2)}) copy-start(f32[1024]{0:T(1024)} %param.10) | copy-start | bytes 12292
  7.2 316.3 %copy-start.4 = (bf16[1024,256]{1,0:T(8,128)(2,1)S(1)}, bf16[1024,256]{1,0:T(8,128)(2,1)}, u32[]{:S(2)}) copy-start(bf16[1024,256]{1,0:T(8,128)(2,1)} %param.12) | copy-start | bytes 1572868
  7.2 303.8 %all-gather.7.cloned.1.call-start = ((), (), s32[]{:S(2)}) async-start(), calls=%async_computation.6 | async-start | bytes 15040512 | tf_op jit(solution)/shard_map/all_gather | solution.py:23
  8.0 503.5 %all-gather.11.cloned.1.call-start = ((), (), s32[]{:S(2)}) async-start(), calls=%async_computation.8 | async-start | bytes 9191424 | tf_op jit(solution)/shard_map/all_gather | solution.py:32
  321.9 379.9 %all-gather.9.cloned.1.call-start = ((), (), s32[]{:S(2)}) async-start(), calls=%async_computation.7 | async-start | bytes 9191424 | tf_op jit(solution)/shard_map/all_gather | solution.py:31
  322.7 630.2 %all-reduce.4.cloned.1.call-start = ((), (), s32[]{:S(2)}) async-start(), calls=%async_computation.9 | async-start | bytes 3604480 | tf_op jit(solution)/shard_map/psum | solution.py:53
  786.4 167.9 %copy-start.3 = (bf16[1024,96]{0,1:T(8,128)(2,1)S(1)}, bf16[1024,96]{0,1:T(8,128)(2,1)}, u32[]{:S(2)}) copy-start(bf16[1024,96]{0,1:T(8,128)(2,1)} %param.13) | copy-start | bytes 589828
  786.4 404.2 %copy-start.1 = (bf16[172,1536]{1,0:T(8,128)(2,1)S(1)}, bf16[172,1536]{1,0:T(8,128)(2,1)}, u32[]{:S(2)}) copy-start(bf16[172,1536]{1,0:T(8,128)(2,1)} %param.7) | copy-start | bytes 1585156
  808.8 231.1 %reduce-scatter.8.cloned.1.call-start = ((), (), s32[]{:S(2)}) async-start(), calls=%async_computation.5 | async-start | bytes 557056 | tf_op jit(solution)/shard_map/reduce_scatter | solution.py:92
  958.3 158.2 %reduce-scatter.4.cloned.1.call-start = ((), (), s32[]{:S(2)}) async-start(), calls=%async_computation.3 | async-start | bytes 1114112 | tf_op jit(solution)/shard_map/reduce_scatter | solution.py:90
  1038.4 152.2 %reduce-scatter.6.cloned.1.call-start = ((), (), s32[]{:S(2)}) async-start(), calls=%async_computation.4 | async-start | bytes 1114112 | tf_op jit(solution)/shard_map/reduce_scatter | solution.py:91
Sparse Core Ops, SparseCore 0:
  9.8 301.1 all-gather.6
  322.0 189.3 all-gather.10
  513.2 188.5 all-gather.8
  808.9 143.9 all-reduce.3
  958.4 79.0 reduce-scatter.7
  1040.5 75.9 reduce-scatter.3
  1119.6 70.9 reduce-scatter.5
where the time goes:
time: 1200 us
  waiting for transfers between devices  936 us (78%)
  local copies, waits for them, and re-layouts  83 us (7%)
  blocking collectives  77.2 us (6%)
  matrix products  61.8 us (5%)
  other arithmetic  25.2 us (2%)
  between operations  14.3 us (1%)
    all_gather x1, waiting for transfers between devices, body(): lax.all_gather(own_columns, 'dp', axis=1, tiled=True)  303 us
    all_gather x1, waiting for transfers between devices, body(): lax.all_gather(values_local, 'dp', axis=0, tiled=True)  186 us
    all_gather x1, waiting for transfers between devices, body(): lax.all_gather(keys_local, 'dp', axis=0, tiled=True)  150 us
    psum x1, waiting for transfers between devices, body(): summed = lax.psum(context, 'member')  144 us
    psum x1, blocking collectives, body(): out_grad = lax.psum(out_part, 'member').astype(jnp.bfloat16)  77.2 us
    reduce_scatter x1, waiting for transfers between devices, body(): lax.psum_scatter(grad_up, 'dp', scatter_dimension=0, tiled=True)  76.7 us
    reduce_scatter x1, waiting for transfers between devices, body(): lax.psum_scatter(grad_down, 'dp', scatter_dimension=0, tiled=True)  74 us
  transfers between devices with their start and end apart: 7, of which 6 were waited for; matrix products, arithmetic and copies ran while one was open for 4% of the time, Pallas kernels for 0%

commit v1 on v0

v1 whole, which is shorter than its diff:
```python
from functools import partial
import math

import jax
import jax.numpy as jnp
from jax import lax
from jax.experimental import pallas as pl
from jax.experimental.pallas import tpu as pltpu
from jax.sharding import Mesh, PartitionSpec as P

VALID = 1370
IMAGES = 2
BF = jnp.bfloat16
F32 = jnp.float32
MEM = ("y", "xh", "c")
G = ("y", "xh")
DP = ("z", "xl")
GROUP = (0, 2, 1, 3, 5, 7, 4, 6)
AT = tuple(GROUP.index(j) for j in range(8))
SWAP = [(0, 1), (1, 0)]
CHUNK = 86
ROWS = 88


def teacher_kernel(s_ref, xa0, xa1, xa2, xa3, xb0, xb1, xb2, xb3, m_own, m_oth, h_own, h_oth, out_ref, xs, wt, p_sc, vx):
    y, xl, rot, c, z = s_ref[0], s_ref[1], s_ref[2], s_ref[3], s_ref[4]
    half = 8 * ROWS
    total = 2 * half
    for d, (a, b) in enumerate(((xa0, xb0), (xa1, xb1), (xa2, xb2), (xa3, xb3))):
        col = pl.multiple_of(lax.rem(y + d, 4) * 384, 384)
        xs[0:half, pl.ds(col, 384)] = a[...]
        xs[half:total, pl.ds(col, 384)] = b[...]
    wt[pl.ds(pl.multiple_of(xl * 384, 384), 192), :] = m_own[...]
    wt[pl.ds(pl.multiple_of((1 - xl) * 384, 384), 192), :] = m_oth[...]
    wt[pl.ds(pl.multiple_of(192 + xl * 96, 96), 96), :] = h_own[...]
    wt[pl.ds(pl.multiple_of(192 + (1 - xl) * 96, 96), 96), :] = h_oth[...]
    blk = 176

    def project(i, carry):
        r0 = pl.multiple_of(i * blk, blk)
        out = lax.dot_general(xs[pl.ds(r0, blk), :], wt[...], (((1,), (1,)), ((), ())), preferred_element_type=F32).astype(BF)
        for t in range(9):
            p_sc[t, pl.ds(r0, blk), :] = out[:, 64 * t : 64 * t + 64]
        return carry

    lax.fori_loop(0, total // blk, project, 0)
    q0 = 3 * rot
    k0 = 3 * lax.rem(rot + 2, 3)
    v0 = 3 * lax.rem(rot + 1, 3)
    row = lax.broadcasted_iota(jnp.int32, (total, 1), 0)
    second = row >= half
    r = lax.rem(row, ROWS)
    zz = lax.rem(row // ROWS, 8)
    parity = jnp.where(second, 1 - c, c)
    real = r < jnp.where((zz == 7) & (parity == 1), VALID - 15 * CHUNK, CHUNK)
    realf = real.astype(F32)
    lane = lax.broadcasted_iota(jnp.int32, (total, 64), 1)
    ones = jnp.where(lane == 0, realf, 0.0).astype(BF)
    for h in range(3):
        vals = p_sc[v0 + h].astype(F32) * realf
        vx[h, :, 0:64] = vals.astype(BF)
        vx[h, :, 64:128] = ones

    def attend(i, carry):
        r0 = pl.multiple_of(i * blk, blk)
        for h in range(3):
            q = p_sc[q0 + h, pl.ds(r0, blk), :] * jnp.asarray(0.125, BF)
            s = lax.dot_general(q, p_sc[k0 + h], (((1,), (1,)), ((), ())), preferred_element_type=F32)
            m = jnp.max(s, axis=1, keepdims=True)
            p = jnp.exp(s - m).astype(BF)
            o = jnp.dot(p, vx[h], preferred_element_type=F32)
            out_ref[pl.ds(r0, blk), 64 * h : 64 * h + 64] = o[:, 0:64] / o[:, 64:65]
        return carry

    lax.fori_loop(0, total // blk, attend, 0)


def teacher(scalars, xa, xb, m_own, m_oth, h_own, h_oth):
    total = 16 * ROWS
    vm = pl.BlockSpec(memory_space=pltpu.VMEM)
    return pl.pallas_call(
        teacher_kernel,
        out_shape=jax.ShapeDtypeStruct((total, 192), F32),
        in_specs=[pl.BlockSpec(memory_space=pltpu.SMEM)] + [vm] * 12,
        out_specs=vm,
        scratch_shapes=[
            pltpu.VMEM((total, 1536), BF),
            pltpu.VMEM((576, 1536), BF),
            pltpu.VMEM((9, total, 64), BF),
            pltpu.VMEM((3, total, 128), BF),
        ],
        compiler_params=pltpu.CompilerParams(vmem_limit_bytes=50 * 2**20),
        cost_estimate=pl.CostEstimate(flops=6_000_000_000, bytes_accessed=12_000_000, transcendentals=6_000_000),
        name="teacher",
    )(scalars, *xa, *xb, m_own, m_oth, h_own, h_oth)


def swap(x, axis):
    return lax.ppermute(x, axis, SWAP)


def spread(x, axis, n):
    return lax.all_to_all(jnp.broadcast_to(x[None], (n,) + x.shape), axis, 0, 0, tiled=True)


def body(teacher_tokens, teacher_qkv, student_tokens, student_gain, w_up, w_down, w_head):
    y, xh, c, z, xl = (lax.axis_index(a) for a in ("y", "xh", "c", "z", "xl"))
    g = 2 * y + xh

    wt = teacher_qkv[0].T
    main = jnp.where(xl == 0, wt[:192], wt[96:])
    part = jnp.where(xl == 0, wt[192:], wt[:96])
    to_main = [(2 * k + e, 2 * AT[(3 * k + 2 * e) % 8] + e) for k in range(8) for e in range(2)]
    to_part = [(2 * k + e, 2 * AT[(3 * k + 1) % 8] + e) for k in range(8) for e in range(2)]
    m_own = lax.ppermute(main, DP, to_main)
    h_own = lax.ppermute(part, DP, to_part)
    m_oth = swap(m_own, "xl")
    h_oth = swap(h_own, "xl")

    tt = lax.dynamic_slice_in_dim(teacher_tokens, y * 384, 384, 1).reshape(CHUNK, IMAGES, 384)
    rows = jnp.arange(ROWS)[:, None]
    reals = jnp.where((z == 7) & (xl == 1), VALID - 15 * CHUNK, CHUNK)

    def padded(v):
        v = jnp.pad(v, ((0, ROWS - CHUNK), (0, 0)))
        return jnp.where(rows < reals, v, v[79:80])

    mine = padded(jnp.where(xl == 0, tt[:, 0], tt[:, 1]))
    other = padded(jnp.where(xl == 0, tt[:, 1], tt[:, 0]))
    got = lax.ppermute(other, ("c", "xl"), [(0, 1), (3, 2)])
    piece = jnp.where(c == xl, mine, got)
    xa0 = spread(piece, "z", 8).reshape(8 * ROWS, 384)
    xa1 = lax.ppermute(xa0, "y", [(k, (k - 1) % 4) for k in range(4)])
    xa3 = lax.ppermute(xa0, "y", [(k, (k + 1) % 4) for k in range(4)])
    top = lax.ppermute(xa1[: 4 * ROWS], "y", [(k, (k - 1) % 4) for k in range(4)])
    low = lax.ppermute(xa3[4 * ROWS :], "y", [(k, (k + 1) % 4) for k in range(4)])
    xa2 = jnp.concatenate([top, low])
    xa = (xa0, xa1, xa2, xa3)
    xb = tuple(swap(v, "c") for v in xa)

    def arranged(v):
        v = jnp.pad(v, ((0, (ROWS - CHUNK) * IMAGES), (0, 0))).reshape(11, 8, IMAGES, -1)
        return v.transpose(2, 1, 0, 3).reshape(IMAGES, ROWS, -1)

    st_own = arranged(student_tokens)
    st_nb = swap(jnp.where(c == 0, st_own[0], st_own[1]), "xl")
    st_nb2 = swap(st_nb, "c")
    st_oth = jnp.where(c == 0, jnp.stack([st_nb, st_nb2]), jnp.stack([st_nb2, st_nb]))
    st = jnp.where(xl == 0, jnp.stack([st_own, st_oth]), jnp.stack([st_oth, st_own]))
    inputs = st.reshape(4 * ROWS, -1).astype(F32)
    in_mean = jnp.mean(inputs, axis=-1, keepdims=True)
    in_var = jnp.mean((inputs - in_mean) ** 2, axis=-1, keepdims=True)
    normed = ((inputs - in_mean) * lax.rsqrt(in_var + 1e-06) * student_gain).astype(BF)
    up = lax.dynamic_slice_in_dim(w_up, xl * 128, 128, 1)
    down = lax.dynamic_slice_in_dim(w_down, xl * 128, 128, 1)
    pre = jnp.dot(normed, up, preferred_element_type=F32)
    gelu_tanh = partial(jax.nn.gelu, approximate=True)
    hidden = gelu_tanh(pre).astype(BF)
    branch = lax.dot_general(hidden, down, (((1,), (1,)), ((), ())), preferred_element_type=F32)
    branch = branch.reshape(2, 2, ROWS, -1)
    keep = lax.dynamic_index_in_dim(branch, c, 0, False) + swap(lax.dynamic_index_in_dim(branch, 1 - c, 0, False), "c")
    sent = swap(lax.dynamic_index_in_dim(keep, 1 - xl, 0, False).astype(BF), "xl")
    keep = (lax.dynamic_index_in_dim(keep, xl, 0, False) + sent.astype(F32)).astype(BF)
    keep = lax.all_to_all(keep.reshape(8, 11, -1), G, 0, 0, tiled=True)
    own_in = lax.dynamic_slice(st.reshape(2, 2, 8, 11, -1), (c, xl, g, 0, 0), (1, 1, 1, 11, st.shape[-1]))[0, 0, 0]
    student_out = (own_in.astype(F32) + jnp.sum(keep.astype(F32), axis=0)).astype(BF)

    def regroup(v):
        nb = swap(v, "xl")
        pair = jnp.where(xl == 0, jnp.stack([v, nb]), jnp.stack([nb, v]))
        far = swap(pair, "c")
        return jnp.where(c == 0, jnp.stack([pair, far]), jnp.stack([far, pair]))

    so_all = regroup(spread(student_out, G, 8).reshape(ROWS, -1)).reshape(4 * ROWS, -1)

    wh = w_head.T
    wh, anchor = lax.optimization_barrier((wh, xa2))
    wh2 = swap(wh, "xh")
    pair = jnp.where(xh == 0, jnp.stack([wh, wh2]), jnp.stack([wh2, wh]))
    w_y = [
        pair,
        lax.ppermute(pair, "y", [(k, (k - 1) % 4) for k in range(4)]),
        lax.ppermute(pair, "y", [(k, (k + 2) % 4) for k in range(4)]),
        lax.ppermute(pair, "y", [(k, (k + 1) % 4) for k in range(4)]),
    ]
    w_y = jnp.stack(w_y)
    w_far = swap(w_y, "c")
    w_all = jnp.where(c == 0, jnp.stack([w_y, w_far], axis=2), jnp.stack([w_far, w_y], axis=2))
    w_all = jnp.concatenate([lax.dynamic_index_in_dim(w_all, (k - y) % 4, 0, True) for k in range(4)])
    w_all = w_all.reshape(1536, -1)
    pred = lax.dot_general(student_out, w_all, (((1,), (1,)), ((), ())), preferred_element_type=F32)

    group = jnp.take(jnp.asarray(GROUP, jnp.int32), z)
    scalars = jnp.stack([y, xl, group % 3, c, z]).astype(jnp.int32)
    xa = (xa[0], xa[1], anchor, xa[3])
    context = teacher(scalars, xa, xb, m_own, m_oth, h_own, h_oth)
    context = context.reshape(2, 8 * ROWS, 192)
    both = context[0] + swap(context[1], "c")
    both = both.astype(BF).reshape(8, 11, 8, 192).transpose(2, 0, 1, 3)
    got = lax.all_to_all(both, G, 0, 0, tiled=True)
    sums = jnp.sum(got.astype(F32), axis=0)
    sums = lax.all_to_all(sums, "z", 0, 0, tiled=True)
    summed = jnp.concatenate([sums[AT[j]] for j in range(8)], axis=-1)

    row_mean = jnp.mean(summed, axis=-1, keepdims=True)
    mean_square = jnp.mean(summed * summed, axis=-1, keepdims=True)
    target = (summed - row_mean) * lax.rsqrt(mean_square - row_mean * row_mean + 1e-06)
    r = 8 * jnp.arange(11)[:, None] + g
    real = (r < CHUNK) & (172 * z + CHUNK * c + r < VALID)
    pred_grad = jnp.where(real, (pred - target) / math.sqrt(IMAGES * VALID), 0.0).astype(BF)
    out_grad = jnp.dot(pred_grad, w_all, preferred_element_type=F32).astype(BF)

    cols = pred_grad.reshape(11, 8, 192).transpose(1, 0, 2)
    load = jnp.concatenate([jnp.broadcast_to(out_grad[None], (8,) + out_grad.shape), cols], axis=-1)
    load = lax.all_to_all(load, G, 0, 0, tiled=True).reshape(ROWS, -1)
    load = regroup(load).reshape(4 * ROWS, -1)
    og = load[:, :1024]
    pg = load[:, 1024:]
    pg = jnp.where(c == 0, pg[:, :96], pg[:, 96:])
    pg = jnp.where(xl == 0, pg[:, :48], pg[:, 48:])

    dims = (((0,), (0,)), ((), ()))
    grad_head = lax.dot_general(pg, so_all, dims, preferred_element_type=F32)
    grad_down = lax.dot_general(hidden, og, dims, preferred_element_type=F32)
    hidden_grad = jnp.dot(og, down, preferred_element_type=F32)
    _, pullback = jax.vjp(gelu_tanh, pre)
    pre_grad = pullback(hidden_grad)[0].astype(BF)
    grad_up = lax.dot_general(pre_grad, normed, dims, preferred_element_type=F32)
    grads = jnp.concatenate([grad_up, grad_down, grad_head]).astype(BF)
    grads = grads.reshape(-1, 8, 128).transpose(1, 0, 2)
    grads = lax.all_to_all(grads, "z", 0, 0, tiled=True)
    grads = jnp.sum(grads.astype(F32), axis=0)
    stay = jnp.where(xl == 0, grads[:, :64], grads[:, 64:])
    come = swap(jnp.where(xl == 0, grads[:, 64:], grads[:, :64]), "xl")

    def joined(lo, hi):
        a, b = stay[lo:hi], come[lo:hi]
        return jnp.where(xl == 0, jnp.concatenate([a, b]), jnp.concatenate([b, a])).T

    return joined(0, 128), joined(128, 256), joined(256, 304)


def solution(mesh):
    fine = Mesh(mesh.devices.reshape(4, 2, 2, 8, 2), ("y", "xh", "c", "z", "xl"))
    in_specs = (
        P(DP, None),
        P(MEM, None, DP),
        P(DP, None),
        P(),
        P(None, MEM),
        P(None, MEM),
        P(None, MEM),
    )
    out_specs = (P(DP, MEM), P(DP, MEM), P(DP, MEM))
    return jax.shard_map(body, mesh=fine, in_specs=in_specs, out_specs=out_specs, check_vma=False)
```

time: 1200 us -> 251 us (0.21)
  waiting for transfers between devices: 936 us -> 73.9 us
  starting transfers between devices: 0.28 us -> 67.6 us
  local copies, waits for them, and re-layouts: 83 us -> 24.3 us
  blocking collectives: 77.2 us -> 22.9 us
  matrix products: 61.8 us -> 7.53 us
  Pallas kernels: 0 us -> 24.3 us
  between operations: 14.3 us -> 2.2 us
    all_gather x3 -> x0, waiting for transfers between devices: 639 us -> none  [the longest x1 303 us: body(): lax.all_gather(own_columns, 'dp', axis=1, tiled=True)]
    reduce_scatter x3 -> x0, waiting for transfers between devices: 151 us -> none  [the longest x1 76.7 us: body(): lax.psum_scatter(grad_up, 'dp', scatter_dimension=0, tiled=True)]
    psum x1 -> x0, waiting for transfers between devices: 144 us -> none  [body(): summed = lax.psum(context, 'member')]
    psum x1 -> x0, blocking collectives: 77.2 us -> none  [body(): out_grad = lax.psum(out_part, 'member').astype(jnp.bfloat16)]
    dot_general x10 -> x7, matrix products: 61.8 us -> 7.53 us  [the longest x1 2.54 us: body(): lax.dot_general(pre_grad, normed, dims, preferred_element_type=F32)]
    reshape x3 -> x8, local copies, waits for them, and re-layouts: 46.7 us -> 2.19 us  [the longest x1 0.81 us: body(): both = both.astype(BF).reshape(8, 11, 8, 192).transpose(2, 0, 1, 3)]
    all_to_all x0 -> x6, waiting for transfers between devices: none -> 43.2 us  [the longest x2 17.3 us: spread(): lax.all_to_all(jnp.broadcast_to(x[None], (n,) + x.shape), axis, 0, 0, til...]
    all_gather x2 -> x0, local copies, waits for them, and re-layouts: 34.8 us -> none  [the longest x1 17.4 us: body(): lax.all_gather(values_local, 'dp', axis=0, tiled=True)]
  transfers between devices with their start and end apart: 7 -> 34, of which waited for: 6 -> 11; matrix products, arithmetic and copies ran while one was open for 4% -> 18% of each run, Pallas kernels for 0% -> 10%
where the time goes in v1:
time: 251 us; the launch traced here: 248 us
  waiting for transfers between devices  73.9 us (29%)
  starting transfers between devices  67.6 us (27%)
  other arithmetic  24.8 us (10%)
  local copies, waits for them, and re-layouts  24.3 us (10%)
  Pallas kernels  24.3 us (10%)
  blocking collectives  22.9 us (9%)
  matrix products  7.53 us (3%)
    pallas_call x1, Pallas kernels, teacher(): pl.pallas_call(teacher_kernel, out_shape=jax.ShapeDtypeStruct((total, 192...  24.3 us
    all_to_all x1, blocking collectives, body(): grads = lax.all_to_all(grads, 'z', 0, 0, tiled=True)  22.9 us
    all_to_all x2, waiting for transfers between devices, spread(): lax.all_to_all(jnp.broadcast_to(x[None], (n,) + x.shape), axis, 0, 0, til...  17.3 us
    ppermute x18, waiting for transfers between devices, swap(): return lax.ppermute(x, axis, SWAP)  14.9 us
    all_to_all x2, starting transfers between devices, spread(): lax.all_to_all(jnp.broadcast_to(x[None], (n,) + x.shape), axis, 0, 0, til...  12.5 us
    all_to_all x1, waiting for transfers between devices, body(): sums = lax.all_to_all(sums, 'z', 0, 0, tiled=True)  8.96 us
    ppermute x18, starting transfers between devices, swap(): return lax.ppermute(x, axis, SWAP)  8.9 us
    ppermute x1, waiting for transfers between devices, body(): lax.ppermute(xa3[4 * ROWS:], 'y', [(k, (k + 1) % 4) for k in range(4)])  8.15 us
  transfers between devices with their start and end apart: 34, of which 11 were waited for; matrix products, arithmetic and copies ran while one was open for 18% of the time, Pallas kernels for 10%

profile of v1, /device:TPU:8, one launch (start us, length us, event | category | flops | bytes accessed | tf_op | source)
XLA Modules:
  0.0 247.5 jit_solution(3060217049933365362)
XLA Ops:
  2.3 3.4 %collective-permute-start.4 = (bf16[88,384]{1,0:T(8,128)(2,1)S(1)}, bf16[88,384]{1,0:T(8,128)(2,1)S(1)}, u32[]{:S(2)}, u32[]{:S(2)}) collective-permute-start(bf16[88,384]{1,0:T(8,128)(2,1)S(1)} %pad_select_fusion), channel_id=1, source_target_pairs={{0,1},{17,16},{2,3},{19,18},{4,5},{21,20},{6,7},{23,22},{8,9},{25,... | collective-permute-start | bytes 202760 | tf_op jit(solution)/shard_map/ppermute | solution.py:130
  7.8 5.2 %collective-permute-start.20 = (bf16[96,1536]{1,0:T(8,128)(2,1)}, bf16[96,1536]{1,0:T(8,128)(2,1)S(1)}, u32[]{:S(2)}, u32[]{:S(2)}) collective-permute-start(bf16[96,1536]{1,0:T(8,128)(2,1)} %slice_select_fusion.1), channel_id=1, source_target_pairs={{0,4},{1,5},{2,12},{3,13},{4,10},{5,11},{6,2},{7,3},{8,8},{9,9},{1... | collective-permute-start | bytes 884744 | tf_op jit(solution)/shard_map/ppermute | solution.py:116
  14.5 7.4 %all-to-all-start.1 = ((bf16[8,88,384]{2,1,0:T(8,128)(2,1)}), bf16[8,88,384]{2,1,0:T(8,128)(2,1)S(1)}, u32[]{:S(2)}, u32[]{:S(2)}) async-start(bf16[8,88,384]{2,1,0:T(8,128)(2,1)} %broadcast_in_dim.75), calls=%async_computation.1 | async-start | bytes 1081344 | tf_op jit(solution)/shard_map/all_to_all | solution.py:103
  24.1 16.3 %all-to-all-done.1 = bf16[8,88,384]{2,1,0:T(8,128)(2,1)S(1)} async-done(((bf16[8,88,384]{2,1,0:T(8,128)(2,1)}), bf16[8,88,384]{2,1,0:T(8,128)(2,1)S(1)}, u32[]{:S(2)}, u32[]{:S(2)}) %all-to-all-start.1) | async-done | bytes 540704 | tf_op jit(solution)/shard_map/all_to_all | solution.py:103
  47.0 7.7 %collective-permute-done.5.xa1 = bf16[704,384]{1,0:T(8,128)(2,1)S(1)} collective-permute-done((bf16[704,384]{1,0:T(8,128)(2,1)S(1)}, bf16[704,384]{1,0:T(8,128)(2,1)S(1)}, u32[]{:S(2)}, u32[]{:S(2)}) %collective-permute-start.5) | collective-permute-done | bytes 540704 | tf_op jit(solution)/shard_map/ppermute | solution.py:133
  56.6 5.9 %collective-permute-start.18 = (bf16[192,1536]{1,0:T(8,128)(2,1)}, bf16[192,1536]{1,0:T(8,128)(2,1)}, u32[]{:S(2)}, u32[]{:S(2)}) collective-permute-start(bf16[192,1536]{1,0:T(8,128)(2,1)} %slice_select_fusion), channel_id=1, source_target_pairs={{0,0},{1,3},{2,6},{3,9},{4,14},{5,1},{6,4},{7,7},{8,12},{9,15},{10... | collective-permute-start | bytes 1769480 | tf_op jit(solution)/shard_map/ppermute | solution.py:115
  63.8 8.2 %collective-permute-done.8 = bf16[352,384]{1,0:T(8,128)(2,1)S(1)} collective-permute-done((bf16[352,384]{1,0:T(8,128)(2,1)S(1)}, bf16[352,384]{1,0:T(8,128)(2,1)S(1)}, u32[]{:S(2)}, u32[]{:S(2)}) %collective-permute-start.8) | collective-permute-done | bytes 270368 | tf_op jit(solution)/shard_map/ppermute | solution.py:136
  72.0 2.8 %collective-permute-start.9 = (bf16[96,1024]{1,0:T(8,128)(2,1)}, bf16[96,1024]{1,0:T(8,128)(2,1)}, u32[]{:S(2)}, u32[]{:S(2)}) collective-permute-start(bf16[96,1024]{1,0:T(8,128)(2,1)} %bitcast.14), channel_id=1, source_target_pairs={{0,32},{32,0},{1,33},{33,1},{2,34},{34,2},{3,35},{35,3},{4,36},{36... | collective-permute-start | bytes 589832 | tf_op jit(solution)/shard_map/ppermute | solution.py:99
  75.9 5.8 %collective-permute-done.9 = bf16[96,1024]{1,0:T(8,128)(2,1)} collective-permute-done((bf16[96,1024]{1,0:T(8,128)(2,1)}, bf16[96,1024]{1,0:T(8,128)(2,1)}, u32[]{:S(2)}, u32[]{:S(2)}) %collective-permute-start.9) | collective-permute-done | bytes 196640 | tf_op jit(solution)/shard_map/ppermute | solution.py:99
  83.7 1.7 stack.164
  85.4 2.0 copy.102
  87.4 1.7 stack.165
  89.1 2.0 copy.103
  93.4 2.1 maximum_select_fusion.7
  95.4 2.8 %collective-permute-start.10 = (bf16[2,96,1024]{2,1,0:T(8,128)(2,1)}, bf16[2,96,1024]{2,1,0:T(8,128)(2,1)}, u32[]{:S(2)}, u32[]{:S(2)}) collective-permute-start(bf16[2,96,1024]{2,1,0:T(8,128)(2,1)} %maximum_select_fusion.7), channel_id=1, source_target_pairs={{0,192},{64,0},{128,64},{192,128},{1,193},{65,1},{129,65},{193,129... | collective-permute-start | bytes 1179656 | tf_op jit(solution)/shard_map/ppermute | solution.py:182
  98.7 2.5 %collective-permute-start.12 = (bf16[2,96,1024]{2,1,0:T(8,128)(2,1)}, bf16[2,96,1024]{2,1,0:T(8,128)(2,1)}, u32[]{:S(2)}, u32[]{:S(2)}) collective-permute-start(bf16[2,96,1024]{2,1,0:T(8,128)(2,1)} %maximum_select_fusion.7), channel_id=1, source_target_pairs={{0,64},{64,128},{128,192},{192,0},{1,65},{65,129},{129,193},{193,1... | collective-permute-start | bytes 1179656 | tf_op jit(solution)/shard_map/ppermute | solution.py:184
  101.2 24.3 %teacher.1 = f32[1408,192]{1,0:T(8,128)} custom-call(s32[5]{0:T(128)S(1)} %stack.197.s_ref, bf16[704,384]{1,0:T(8,128)(2,1)S(1)} %bitcast.136, bf16[704,384]{1,0:T(8,128)(2,1)S(1)} %collective-permute-done.5.xa1, bf16[704,384]{1,0:T(8,128)(2,1)S(1)} %constant_dynamic-update-slice_fusion.xa2, bf16[704,384]{1,0:T(8,128)(2,1)S(1)} %collective-permute-done.7.xa3, ...), custom_call_target="tpu_custom_call" | custom-call | flops 6000000000 | bytes 12000000 | tf_op jit(solution)/shard_map/teacher/pallas_call | solution.py:81
  128.3 2.7 %fusion.77 = (bf16[4,2,1,96,1024]{4,3,2,1,0:T(8,128)(2,1)S(1)}, bf16[4,2,96,1024]{3,2,1,0:T(8,128)(2,1)}) fusion(bf16[1,2,96,1024]{3,2,1,0:T(8,128)(2,1)} %bitcast.22, bf16[1,2,96,1024]{3,2,1,0:T(8,128)(2,1)} %bitcast.21, bf16[1,2,96,1024]{3,2,1,0:T(8,128)(2,1)} %bitcast.20, bf16[1,2,96,1024]{3,2,1,0:T(8,128)(2,1)S(1)} %maximum_select_fusion.6), kind=kLoop, calls=%fused_computation.152 | loop fusion | flops 2359296 | bytes 4718592 | tf_op jit(solution)/shard_map/stack | solution.py:188
  134.9 6.9 %all-to-all-start = ((bf16[8,11,1024]{2,1,0:T(8,128)(2,1)}), bf16[8,11,1024]{2,1,0:T(8,128)(2,1)}, u32[]{:S(2)}, u32[]{:S(2)}) async-start(bf16[8,11,1024]{2,1,0:T(8,128)(2,1)} %reshape.490), calls=%async_computation | async-start | bytes 524288 | tf_op jit(solution)/shard_map/all_to_all | solution.py:164
  145.2 3.9 %all-to-all-done = bf16[8,11,1024]{2,1,0:T(8,128)(2,1)} async-done(((bf16[8,11,1024]{2,1,0:T(8,128)(2,1)}), bf16[8,11,1024]{2,1,0:T(8,128)(2,1)}, u32[]{:S(2)}, u32[]{:S(2)}) %all-to-all-start) | async-done | bytes 180256 | tf_op jit(solution)/shard_map/all_to_all | solution.py:164
  149.1 5.1 %all-to-all-start.2 = ((bf16[8,8,11,192]{3,1,2,0:T(8,128)(2,1)}), bf16[8,8,11,192]{3,1,2,0:T(8,128)(2,1)S(1)}, u32[]{:S(2)}, u32[]{:S(2)}) async-start(bf16[8,8,11,192]{3,1,2,0:T(8,128)(2,1)} %bitcast.129), calls=%async_computation.2 | async-start | bytes 720896 | tf_op jit(solution)/shard_map/all_to_all | solution.py:200
  155.5 6.3 %all-to-all-done.2 = bf16[8,8,11,192]{3,1,2,0:T(8,128)(2,1)S(1)} async-done(((bf16[8,8,11,192]{3,1,2,0:T(8,128)(2,1)}), bf16[8,8,11,192]{3,1,2,0:T(8,128)(2,1)S(1)}, u32[]{:S(2)}, u32[]{:S(2)}) %all-to-all-start.2) | async-done | bytes 270368 | tf_op jit(solution)/shard_map/all_to_all | solution.py:200
  162.6 3.4 %all-to-all-start.3 = ((f32[8,11,192]{2,1,0:T(8,128)}), f32[8,11,192]{2,1,0:T(8,128)S(1)}, u32[]{:S(2)}, u32[]{:S(2)}) async-start(f32[8,11,192]{2,1,0:T(8,128)} %copy.113), calls=%async_computation.3 | async-start | bytes 262144 | tf_op jit(solution)/shard_map/all_to_all | solution.py:202
  165.9 9.0 %all-to-all-done.3 = f32[8,11,192]{2,1,0:T(8,128)S(1)} async-done(((f32[8,11,192]{2,1,0:T(8,128)}), f32[8,11,192]{2,1,0:T(8,128)S(1)}, u32[]{:S(2)}, u32[]{:S(2)}) %all-to-all-start.3) | async-done | bytes 67616 | tf_op jit(solution)/shard_map/all_to_all | solution.py:202
  175.7 5.1 %all-to-all-start.5 = ((bf16[8,11,1024]{2,1,0:T(8,128)(2,1)}), bf16[8,11,1024]{2,1,0:T(8,128)(2,1)S(1)}, u32[]{:S(2)}, u32[]{:S(2)}) async-start(bf16[8,11,1024]{2,1,0:T(8,128)(2,1)} %broadcast_in_dim.79), calls=%async_computation.5 | async-start | bytes 524288 | tf_op jit(solution)/shard_map/all_to_all | solution.py:103
  181.3 2.1 maximum_select_fusion
  187.8 6.3 %all-to-all-start.4 = ((bf16[8,11,1216]{2,1,0:T(8,128)(2,1)}), bf16[8,11,1216]{2,1,0:T(8,128)(2,1)S(1)}, u32[]{:S(2)}, u32[]{:S(2)}) async-start(bf16[8,11,1216]{2,1,0:T(8,128)(2,1)} %pad_maximum_fusion.2), calls=%async_computation.4 | async-start | bytes 655360 | tf_op jit(solution)/shard_map/all_to_all | solution.py:215
  195.6 6.7 %all-to-all-done.4 = bf16[8,11,1216]{2,1,0:T(8,128)(2,1)S(1)} async-done(((bf16[8,11,1216]{2,1,0:T(8,128)(2,1)}), bf16[8,11,1216]{2,1,0:T(8,128)(2,1)S(1)}, u32[]{:S(2)}, u32[]{:S(2)}) %all-to-all-start.4) | async-done | bytes 214048 | tf_op jit(solution)/shard_map/all_to_all | solution.py:215
  204.2 4.3 %collective-permute-done.23 = bf16[88,1216]{1,0:T(8,128)(2,1)S(1)} collective-permute-done((bf16[88,1216]{1,0:T(8,128)(2,1)S(1)}, bf16[88,1216]{1,0:T(8,128)(2,1)S(1)}, u32[]{:S(2)}, u32[]{:S(2)}) %collective-permute-start.23) | collective-permute-done | bytes 214048 | tf_op jit(solution)/shard_map/ppermute | solution.py:99
  212.3 2.5 %convolution_convert_fusion.1 = bf16[128,8,128]{2,0,1:T(8,128)(2,1)} fusion(f32[352,128]{1,0:T(8,128)S(1)} %copy-done.9, bf16[1024,256]{1,0:T(8,128)(2,1)} %param.13, s32[]{:T(128)S(6)} %select_n.330, bf16[352,1216]{1,0:T(8,128)(2,1)S(1)} %bitcast.144, bf16[352,1024]{1,0:T(8,128)(2,1)S(1)} %copy-done.5), kind=kOutput, calls=%fused_computation.14 | convolution fusion | flops 185581568 | bytes 2146308 | tf_op jit(solution)/shard_map/dot_general | solution.py:228
  216.1 22.9 %all_to_all.35 = bf16[8,304,128]{2,1,0:T(8,128)(2,1)S(1)} all-to-all(bf16[8,304,128]{2,1,0:T(8,128)(2,1)S(1)} %maximum_bitcast_fusion), channel_id=1, replica_groups=mesh['y'=4,'xh'=2,'c'=2,'z'=8,'xl'=2] {'z'}, dimensions={0} | all-to-all | bytes 1245184 | tf_op jit(solution)/shard_map/all_to_all | solution.py:231
  240.6 4.8 %collective-permute-done.27 = f32[304,64]{1,0:T(8,128)S(1)} collective-permute-done((f32[304,64]{1,0:T(8,128)S(1)}, f32[304,64]{1,0:T(8,128)S(1)}, u32[]{:S(2)}, u32[]{:S(2)}) %collective-permute-start.27) | collective-permute-done | bytes 77856 | tf_op jit(solution)/shard_map/ppermute | solution.py:99
  (184 shorter events, 51.5 us)
Async XLA Ops:
  2.3 11.2 %collective-permute-start.4 = (bf16[88,384]{1,0:T(8,128)(2,1)S(1)}, bf16[88,384]{1,0:T(8,128)(2,1)S(1)}, u32[]{:S(2)}, u32[]{:S(2)}) collective-permute-start(bf16[88,384]{1,0:T(8,128)(2,1)S(1)} %pad_select_fusion), channel_id=1, source_target_pairs={{0,1},{17,16},{2,3},{19,18},{4,5},{21,20},{6,7},{23,22},{8,9},{25,... | collective-permute-start | bytes 202760 | tf_op jit(solution)/shard_map/ppermute | solution.py:130
  6.9 6.5 %collective-permute-start = (bf16[88,1024]{1,0:T(8,128)(2,1)S(1)}, bf16[88,1024]{1,0:T(8,128)(2,1)S(1)}, u32[]{:S(2)}, u32[]{:S(2)}) collective-permute-start(bf16[88,1024]{1,0:T(8,128)(2,1)S(1)} %select_n.320), channel_id=1, source_target_pairs={{0,1},{1,0},{2,3},{3,2},{4,5},{5,4},{6,7},{7,6},{8,9},{9,8},{10,11... | collective-permute-start | bytes 540680 | tf_op jit(solution)/shard_map/ppermute | solution.py:99
  7.8 55.9 %collective-permute-start.20 = (bf16[96,1536]{1,0:T(8,128)(2,1)}, bf16[96,1536]{1,0:T(8,128)(2,1)S(1)}, u32[]{:S(2)}, u32[]{:S(2)}) collective-permute-start(bf16[96,1536]{1,0:T(8,128)(2,1)} %slice_select_fusion.1), channel_id=1, source_target_pairs={{0,4},{1,5},{2,12},{3,13},{4,10},{5,11},{6,2},{7,3},{8,8},{9,9},{1... | collective-permute-start | bytes 884744 | tf_op jit(solution)/shard_map/ppermute | solution.py:116
  13.4 8.4 %collective-permute-start.1 = (bf16[88,1024]{1,0:T(8,128)(2,1)S(1)}, bf16[88,1024]{1,0:T(8,128)(2,1)S(1)}, u32[]{:S(2)}, u32[]{:S(2)}) collective-permute-start(bf16[88,1024]{1,0:T(8,128)(2,1)S(1)} %collective-permute-done), channel_id=1, source_target_pairs={{0,16},{16,0},{1,17},{17,1},{2,18},{18,2},{3,19},{19,3},{4,20},{20... | collective-permute-start | bytes 540680 | tf_op jit(solution)/shard_map/ppermute | solution.py:99
  14.5 25.9 %all-to-all-start.1 = ((bf16[8,88,384]{2,1,0:T(8,128)(2,1)}), bf16[8,88,384]{2,1,0:T(8,128)(2,1)S(1)}, u32[]{:S(2)}, u32[]{:S(2)}) async-start(bf16[8,88,384]{2,1,0:T(8,128)(2,1)} %broadcast_in_dim.75), calls=%async_computation.1 | async-start | bytes 1081344 | tf_op jit(solution)/shard_map/all_to_all | solution.py:103
  40.4 14.2 %collective-permute-start.5 = (bf16[704,384]{1,0:T(8,128)(2,1)S(1)}, bf16[704,384]{1,0:T(8,128)(2,1)S(1)}, u32[]{:S(2)}, u32[]{:S(2)}) collective-permute-start(bf16[704,384]{1,0:T(8,128)(2,1)S(1)} %bitcast.133), channel_id=1, source_target_pairs={{0,192},{64,0},{128,64},{192,128},{1,193},{65,1},{129,65},{193,129... | collective-permute-start | bytes 1622024 | tf_op jit(solution)/shard_map/ppermute | solution.py:133
  44.4 18.2 %collective-permute-start.7 = (bf16[704,384]{1,0:T(8,128)(2,1)S(1)}, bf16[704,384]{1,0:T(8,128)(2,1)S(1)}, u32[]{:S(2)}, u32[]{:S(2)}) collective-permute-start(bf16[704,384]{1,0:T(8,128)(2,1)S(1)} %bitcast.134), channel_id=1, source_target_pairs={{0,64},{64,128},{128,192},{192,0},{1,65},{65,129},{129,193},{193,1... | collective-permute-start | bytes 1622024 | tf_op jit(solution)/shard_map/ppermute | solution.py:134
  47.0 28.9 %collective-permute-start.2 = (f32[2,88,1024]{2,1,0:T(8,128)}, f32[2,88,1024]{2,1,0:T(8,128)}, u32[]{:S(2)}, u32[]{:S(2)}) collective-permute-start(f32[2,88,1024]{2,1,0:T(8,128)} %dynamic-slice_bitcast_fusion), channel_id=1, source_target_pairs={{0,16},{16,0},{1,17},{17,1},{2,18},{18,2},{3,19},{19,3},{4,20},{20... | collective-permute-start | bytes 2162696 | tf_op jit(solution)/shard_map/ppermute | solution.py:99
  54.7 9.0 %collective-permute-start.6 = (bf16[352,384]{1,0:T(8,128)(2,1)S(1)}, bf16[352,384]{1,0:T(8,128)(2,1)S(1)}, u32[]{:S(2)}, u32[]{:S(2)}) collective-permute-start(bf16[352,384]{1,0:T(8,128)(2,1)S(1)} %slice.166), channel_id=1, source_target_pairs={{0,192},{64,0},{128,64},{192,128},{1,193},{65,1},{129,65},{193,129... | collective-permute-start | bytes 811016 | tf_op jit(solution)/shard_map/ppermute | solution.py:135
  56.6 18.2 %collective-permute-start.18 = (bf16[192,1536]{1,0:T(8,128)(2,1)}, bf16[192,1536]{1,0:T(8,128)(2,1)}, u32[]{:S(2)}, u32[]{:S(2)}) collective-permute-start(bf16[192,1536]{1,0:T(8,128)(2,1)} %slice_select_fusion), channel_id=1, source_target_pairs={{0,0},{1,3},{2,6},{3,9},{4,14},{5,1},{6,4},{7,7},{8,12},{9,15},{10... | collective-permute-start | bytes 1769480 | tf_op jit(solution)/shard_map/ppermute | solution.py:115
  62.6 9.3 %collective-permute-start.8 = (bf16[352,384]{1,0:T(8,128)(2,1)S(1)}, bf16[352,384]{1,0:T(8,128)(2,1)S(1)}, u32[]{:S(2)}, u32[]{:S(2)}) collective-permute-start(bf16[352,384]{1,0:T(8,128)(2,1)S(1)} %slice.167), channel_id=1, source_target_pairs={{0,64},{64,128},{128,192},{192,0},{1,65},{65,129},{129,193},{193,1... | collective-permute-start | bytes 811016 | tf_op jit(solution)/shard_map/ppermute | solution.py:136
  63.7 11.6 %collective-permute-start.21 = (bf16[96,1536]{1,0:T(8,128)(2,1)S(1)}, bf16[96,1536]{1,0:T(8,128)(2,1)}, u32[]{:S(2)}, u32[]{:S(2)}) collective-permute-start(bf16[96,1536]{1,0:T(8,128)(2,1)S(1)} %collective-permute-done.20.h_own), channel_id=1, source_target_pairs={{0,1},{1,0},{2,3},{3,2},{4,5},{5,4},{6,7},{7,6},{8,9},{9,8},{10,11... | collective-permute-start | bytes 884744 | tf_op jit(solution)/shard_map/ppermute | solution.py:99
  72.0 9.7 %collective-permute-start.9 = (bf16[96,1024]{1,0:T(8,128)(2,1)}, bf16[96,1024]{1,0:T(8,128)(2,1)}, u32[]{:S(2)}, u32[]{:S(2)}) collective-permute-start(bf16[96,1024]{1,0:T(8,128)(2,1)} %bitcast.14), channel_id=1, source_target_pairs={{0,32},{32,0},{1,33},{33,1},{2,34},{34,2},{3,35},{35,3},{4,36},{36... | collective-permute-start | bytes 589832 | tf_op jit(solution)/shard_map/ppermute | solution.py:99
  74.8 20.6 %collective-permute-start.19 = (bf16[192,1536]{1,0:T(8,128)(2,1)}, bf16[192,1536]{1,0:T(8,128)(2,1)}, u32[]{:S(2)}, u32[]{:S(2)}) collective-permute-start(bf16[192,1536]{1,0:T(8,128)(2,1)} %collective-permute-done.18.m_own), channel_id=1, source_target_pairs={{0,1},{1,0},{2,3},{3,2},{4,5},{5,4},{6,7},{7,6},{8,9},{9,8},{10,11... | collective-permute-start | bytes 1769480 | tf_op jit(solution)/shard_map/ppermute | solution.py:99
  75.3 20.1 %collective-permute-start.14 = (bf16[704,384]{1,0:T(8,128)(2,1)S(1)}, bf16[704,384]{1,0:T(8,128)(2,1)S(1)}, u32[]{:S(2)}, u32[]{:S(2)}) collective-permute-start(bf16[704,384]{1,0:T(8,128)(2,1)S(1)} %bitcast.135), channel_id=1, source_target_pairs={{0,16},{16,0},{1,17},{17,1},{2,18},{18,2},{3,19},{19,3},{4,20},{20... | collective-permute-start | bytes 1622024 | tf_op jit(solution)/shard_map/ppermute | solution.py:99
  75.3 22.9 %collective-permute-start.15 = (bf16[704,384]{1,0:T(8,128)(2,1)S(1)}, bf16[704,384]{1,0:T(8,128)(2,1)}, u32[]{:S(2)}, u32[]{:S(2)}) collective-permute-start(bf16[704,384]{1,0:T(8,128)(2,1)S(1)} %collective-permute-done.5.xa1), channel_id=1, source_target_pairs={{0,16},{16,0},{1,17},{17,1},{2,18},{18,2},{3,19},{19,3},{4,20},{20... | collective-permute-start | bytes 1622024 | tf_op jit(solution)/shard_map/ppermute | solution.py:99
  75.8 22.8 %collective-permute-start.17 = (bf16[704,384]{1,0:T(8,128)(2,1)S(1)}, bf16[704,384]{1,0:T(8,128)(2,1)}, u32[]{:S(2)}, u32[]{:S(2)}) collective-permute-start(bf16[704,384]{1,0:T(8,128)(2,1)S(1)} %collective-permute-done.7.xa3), channel_id=1, source_target_pairs={{0,16},{16,0},{1,17},{17,1},{2,18},{18,2},{3,19},{19,3},{4,20},{20... | collective-permute-start | bytes 1622024 | tf_op jit(solution)/shard_map/ppermute | solution.py:99
  81.7 19.5 %collective-permute-start.16 = (bf16[704,384]{1,0:T(8,128)(2,1)S(1)}, bf16[704,384]{1,0:T(8,128)(2,1)}, u32[]{:S(2)}, u32[]{:S(2)}) collective-permute-start(bf16[704,384]{1,0:T(8,128)(2,1)S(1)} %constant_dynamic-update-slice_fusion.xa2), channel_id=1, source_target_pairs={{0,16},{16,0},{1,17},{17,1},{2,18},{18,2},{3,19},{19,3},{4,20},{20... | collective-permute-start | bytes 1622024 | tf_op jit(solution)/shard_map/ppermute | solution.py:99
  95.4 37.7 %collective-permute-start.3 = (bf16[88,1024]{1,0:T(8,128)(2,1)}, bf16[88,1024]{1,0:T(8,128)(2,1)}, u32[]{:S(2)}, u32[]{:S(2)}) collective-permute-start(bf16[88,1024]{1,0:T(8,128)(2,1)} %fusion.28), channel_id=1, source_target_pairs={{0,1},{1,0},{2,3},{3,2},{4,5},{5,4},{6,7},{7,6},{8,9},{9,8},{10,11... | collective-permute-start | bytes 540680 | tf_op jit(solution)/shard_map/ppermute | solution.py:99
  95.4 32.8 %collective-permute-start.10 = (bf16[2,96,1024]{2,1,0:T(8,128)(2,1)}, bf16[2,96,1024]{2,1,0:T(8,128)(2,1)}, u32[]{:S(2)}, u32[]{:S(2)}) collective-permute-start(bf16[2,96,1024]{2,1,0:T(8,128)(2,1)} %maximum_select_fusion.7), channel_id=1, source_target_pairs={{0,192},{64,0},{128,64},{192,128},{1,193},{65,1},{129,65},{193,129... | collective-permute-start | bytes 1179656 | tf_op jit(solution)/shard_map/ppermute | solution.py:182
  98.2 30.0 %collective-permute-start.11 = (bf16[2,96,1024]{2,1,0:T(8,128)(2,1)}, bf16[2,96,1024]{2,1,0:T(8,128)(2,1)}, u32[]{:S(2)}, u32[]{:S(2)}) collective-permute-start(bf16[2,96,1024]{2,1,0:T(8,128)(2,1)} %maximum_select_fusion.7), channel_id=1, source_target_pairs={{0,128},{64,192},{128,0},{192,64},{1,129},{65,193},{129,1},{193,65... | collective-permute-start | bytes 1179656 | tf_op jit(solution)/shard_map/ppermute | solution.py:183
  98.7 29.6 %collective-permute-start.12 = (bf16[2,96,1024]{2,1,0:T(8,128)(2,1)}, bf16[2,96,1024]{2,1,0:T(8,128)(2,1)}, u32[]{:S(2)}, u32[]{:S(2)}) collective-permute-start(bf16[2,96,1024]{2,1,0:T(8,128)(2,1)} %maximum_select_fusion.7), channel_id=1, source_target_pairs={{0,64},{64,128},{128,192},{192,0},{1,65},{65,129},{129,193},{193,1... | collective-permute-start | bytes 1179656 | tf_op jit(solution)/shard_map/ppermute | solution.py:184
  126.8 15.0 %collective-permute-start.22 = (f32[704,192]{0,1:T(8,128)S(1)}, f32[704,192]{0,1:T(8,128)}, u32[]{:S(2)}, u32[]{:S(2)}) collective-permute-start(f32[704,192]{0,1:T(8,128)S(1)} %copy.110), channel_id=1, source_target_pairs={{0,16},{16,0},{1,17},{17,1},{2,18},{18,2},{3,19},{19,3},{4,20},{20... | collective-permute-start | bytes 1622024 | tf_op jit(solution)/shard_map/ppermute | solution.py:99
  131.0 50.2 %collective-permute-start.13 = (bf16[4,2,96,1024]{3,2,1,0:T(8,128)(2,1)}, bf16[4,2,96,1024]{3,2,1,0:T(8,128)(2,1)}, u32[]{:S(2)}, u32[]{:S(2)}) collective-permute-start(bf16[4,2,96,1024]{3,2,1,0:T(8,128)(2,1)} %get-tuple-element.51), channel_id=1, source_target_pairs={{0,16},{16,0},{1,17},{17,1},{2,18},{18,2},{3,19},{19,3},{4,20},{20... | collective-permute-start | bytes 4718600 | tf_op jit(solution)/shard_map/ppermute | solution.py:99
  134.9 14.2 %all-to-all-start = ((bf16[8,11,1024]{2,1,0:T(8,128)(2,1)}), bf16[8,11,1024]{2,1,0:T(8,128)(2,1)}, u32[]{:S(2)}, u32[]{:S(2)}) async-start(bf16[8,11,1024]{2,1,0:T(8,128)(2,1)} %reshape.490), calls=%async_computation | async-start | bytes 524288 | tf_op jit(solution)/shard_map/all_to_all | solution.py:164
  149.1 12.7 %all-to-all-start.2 = ((bf16[8,8,11,192]{3,1,2,0:T(8,128)(2,1)}), bf16[8,8,11,192]{3,1,2,0:T(8,128)(2,1)S(1)}, u32[]{:S(2)}, u32[]{:S(2)}) async-start(bf16[8,8,11,192]{3,1,2,0:T(8,128)(2,1)} %bitcast.129), calls=%async_computation.2 | async-start | bytes 720896 | tf_op jit(solution)/shard_map/all_to_all | solution.py:200
  162.6 12.4 %all-to-all-start.3 = ((f32[8,11,192]{2,1,0:T(8,128)}), f32[8,11,192]{2,1,0:T(8,128)S(1)}, u32[]{:S(2)}, u32[]{:S(2)}) async-start(f32[8,11,192]{2,1,0:T(8,128)} %copy.113), calls=%async_computation.3 | async-start | bytes 262144 | tf_op jit(solution)/shard_map/all_to_all | solution.py:202
  175.7 12.2 %all-to-all-start.5 = ((bf16[8,11,1024]{2,1,0:T(8,128)(2,1)}), bf16[8,11,1024]{2,1,0:T(8,128)(2,1)S(1)}, u32[]{:S(2)}, u32[]{:S(2)}) async-start(bf16[8,11,1024]{2,1,0:T(8,128)(2,1)} %broadcast_in_dim.79), calls=%async_computation.5 | async-start | bytes 524288 | tf_op jit(solution)/shard_map/all_to_all | solution.py:103
  187.8 14.5 %all-to-all-start.4 = ((bf16[8,11,1216]{2,1,0:T(8,128)(2,1)}), bf16[8,11,1216]{2,1,0:T(8,128)(2,1)S(1)}, u32[]{:S(2)}, u32[]{:S(2)}) async-start(bf16[8,11,1216]{2,1,0:T(8,128)(2,1)} %pad_maximum_fusion.2), calls=%async_computation.4 | async-start | bytes 655360 | tf_op jit(solution)/shard_map/all_to_all | solution.py:215
  194.2 9.8 %collective-permute-start.25 = (bf16[88,1024]{1,0:T(8,128)(2,1)S(1)}, bf16[88,1024]{1,0:T(8,128)(2,1)S(1)}, u32[]{:S(2)}, u32[]{:S(2)}) collective-permute-start(bf16[88,1024]{1,0:T(8,128)(2,1)S(1)} %reshape.497), channel_id=1, source_target_pairs={{0,1},{1,0},{2,3},{3,2},{4,5},{5,4},{6,7},{7,6},{8,9},{9,8},{10,11... | collective-permute-start | bytes 540680 | tf_op jit(solution)/shard_map/ppermute | solution.py:99
  202.5 6.1 %collective-permute-start.23 = (bf16[88,1216]{1,0:T(8,128)(2,1)S(1)}, bf16[88,1216]{1,0:T(8,128)(2,1)S(1)}, u32[]{:S(2)}, u32[]{:S(2)}) collective-permute-start(bf16[88,1216]{1,0:T(8,128)(2,1)S(1)} %reshape.496), channel_id=1, source_target_pairs={{0,1},{1,0},{2,3},{3,2},{4,5},{5,4},{6,7},{7,6},{8,9},{9,8},{10,11... | collective-permute-start | bytes 642056 | tf_op jit(solution)/shard_map/ppermute | solution.py:99
  239.3 6.1 %collective-permute-start.27 = (f32[304,64]{1,0:T(8,128)S(1)}, f32[304,64]{1,0:T(8,128)S(1)}, u32[]{:S(2)}, u32[]{:S(2)}) collective-permute-start(f32[304,64]{1,0:T(8,128)S(1)} %get-tuple-element.57), channel_id=1, source_target_pairs={{0,1},{1,0},{2,3},{3,2},{4,5},{5,4},{6,7},{7,6},{8,9},{9,8},{10,11... | collective-permute-start | bytes 233480 | tf_op jit(solution)/shard_map/ppermute | solution.py:99
  (23 other events, 106.5 us)

commit v2 on v1

v2 whole, which is shorter than its diff:
```python
import math

import jax
import jax.numpy as jnp
from jax import lax
from jax.experimental import pallas as pl
from jax.experimental.pallas import tpu as pltpu
from jax.sharding import Mesh, PartitionSpec as P

VALID = 1370
IMAGES = 2
BF = jnp.bfloat16
F32 = jnp.float32
MEM = ("y", "xh", "c")
G = ("y", "xh")
DP = ("z", "xl")
GROUP = (0, 2, 1, 3, 5, 7, 4, 6)
AT = tuple(GROUP.index(j) for j in range(8))
SWAP = [(0, 1), (1, 0)]
CHUNK = 86
ROWS = 88


def teacher_kernel(s_ref, xa0, xa1, xa2, xa2l, xa3, xb0, xb1, xb2, xb2l, xb3, m_own, m_oth, h_own, h_oth, own_ref, oth_ref, xs, wt, p_sc, vx):
    y, xl, rot, c = s_ref[0], s_ref[1], s_ref[2], s_ref[3]
    half = 8 * ROWS
    total = 2 * half
    for d, (a, b) in enumerate(((xa0, xb0), (xa1, xb1), ((xa2, xa2l), (xb2, xb2l)), (xa3, xb3))):
        col = pl.multiple_of(lax.rem(y + d, 4) * 384, 384)
        if d == 2:
            for k, v in enumerate((*a, *b)):
                xs[k * half // 2 : (k + 1) * half // 2, pl.ds(col, 384)] = v[...]
        else:
            xs[0:half, pl.ds(col, 384)] = a[...]
            xs[half:total, pl.ds(col, 384)] = b[...]
    wt[pl.ds(pl.multiple_of(xl * 384, 384), 192), :] = m_own[...]
    wt[pl.ds(pl.multiple_of((1 - xl) * 384, 384), 192), :] = m_oth[...]
    wt[pl.ds(pl.multiple_of(192 + xl * 96, 96), 96), :] = h_own[...]
    wt[pl.ds(pl.multiple_of(192 + (1 - xl) * 96, 96), 96), :] = h_oth[...]
    blk = 176

    def project(i, carry):
        r0 = pl.multiple_of(i * blk, blk)
        out = lax.dot_general(xs[pl.ds(r0, blk), :], wt[...], (((1,), (1,)), ((), ())), preferred_element_type=F32).astype(BF)
        for t in range(9):
            p_sc[t, pl.ds(r0, blk), :] = out[:, 64 * t : 64 * t + 64]
        return carry

    lax.fori_loop(0, total // blk, project, 0)
    q0 = 3 * rot
    k0 = 3 * lax.rem(rot + 2, 3)
    v0 = 3 * lax.rem(rot + 1, 3)
    row = lax.broadcasted_iota(jnp.int32, (total, 1), 0)
    second = row >= half
    r = lax.rem(row, ROWS)
    zz = lax.rem(row // ROWS, 8)
    parity = jnp.where(second, 1 - c, c)
    real = r < jnp.where((zz == 7) & (parity == 1), VALID - 15 * CHUNK, CHUNK)
    realf = real.astype(F32)
    lane = lax.broadcasted_iota(jnp.int32, (total, 64), 1)
    ones = jnp.where(lane == 0, realf, 0.0).astype(BF)
    for h in range(3):
        vals = p_sc[v0 + h].astype(F32) * realf
        vx[h, :, 0:64] = vals.astype(BF)
        vx[h, :, 64:128] = ones

    def attend(i, out_ref, base, at):
        r0 = pl.multiple_of(i * blk, blk)
        for h in range(3):
            q = p_sc[q0 + h, pl.ds(base + r0, blk), :] * jnp.asarray(0.125, BF)
            s = lax.dot_general(q, p_sc[k0 + h], (((1,), (1,)), ((), ())), preferred_element_type=F32)
            m = jnp.max(s, axis=1, keepdims=True)
            p = jnp.exp(s - m).astype(BF)
            o = jnp.dot(p, vx[h], preferred_element_type=F32)
            out_ref[pl.ds(r0, blk), at + 64 * h : at + 64 * h + 64] = o[:, 0:64] / o[:, 64:65]

    quarter = half // 2
    for k, (out_ref, at) in enumerate(((oth_ref, 0), (oth_ref, 192), (own_ref, 0), (own_ref, 192))):
        base = (half if k < 2 else 0) + (k % 2) * quarter

        @pl.loop(0, quarter // blk)
        def _(i, out_ref=out_ref, base=base, at=at):
            attend(i, out_ref, base, at)


VM = pl.BlockSpec(memory_space=pltpu.VMEM)
SM = pl.BlockSpec(memory_space=pltpu.SMEM)
TN = (((0,), (0,)), ((), ()))
NT = (((1,), (1,)), ((), ()))


def call(kernel, outs, *args, scratch=(), scalar=0, flops=0, vmem=24):
    shapes = [jax.ShapeDtypeStruct(s, d) for s, d in outs]
    moved = sum(math.prod(v.shape) * v.dtype.itemsize for v in args) + sum(math.prod(s.shape) * s.dtype.itemsize for s in shapes)
    return pl.pallas_call(
        kernel,
        out_shape=shapes,
        in_specs=[SM] * scalar + [VM] * (len(args) - scalar),
        out_specs=[VM] * len(shapes),
        scratch_shapes=list(scratch),
        compiler_params=pltpu.CompilerParams(vmem_limit_bytes=vmem * 2**20),
        cost_estimate=pl.CostEstimate(flops=flops, bytes_accessed=moved, transcendentals=flops // 1000),
    )(*args)


def student_kernel(s_ref, own, nb, gain, up, down, normed, pre, hidden, br_own, br_oth, own_in):
    xl, c, g = s_ref[1], s_ref[3], s_ref[5]
    mine = c == xl
    for b in range(2):
        for q in range(8):
            for e in range(2):
                first, second = (own, nb) if b == 0 else (nb, own)
                x = jnp.where(mine, first[e, q].astype(F32), second[e, q].astype(F32))
                mean = jnp.mean(x, axis=-1, keepdims=True)
                dev = x - mean
                var = jnp.mean(dev * dev, axis=-1, keepdims=True)
                at = 256 * b + 32 * q + 16 * e
                normed[at : at + 16, :] = (dev * lax.rsqrt(var + 1e-06) * gain[...]).astype(BF)
    x = jnp.dot(normed[...], up[...], preferred_element_type=F32)
    pre[...] = x
    k0 = math.sqrt(2 / math.pi)
    hid = (x * (0.5 * (1.0 + jnp.tanh(k0 * (x + 0.044715 * (x * x * x)))))).astype(BF)
    hidden[...] = hid
    br_own[...] = lax.dot_general(hid[0:256], down[...], NT, preferred_element_type=F32)
    br_oth[...] = lax.dot_general(hid[256:512], down[...], NT, preferred_element_type=F32)
    own_in[...] = jnp.where(mine, own[xl, g].astype(F32), nb[xl, g].astype(F32)).astype(BF)


def join_kernel(keep, own_in, out, wide):
    total = own_in[...].astype(F32)
    for k in range(16):
        total += keep[k].astype(F32)
    row = total.astype(BF)
    out[...] = row
    for k in range(16):
        wide[k] = row


def pack_kernel(own, got, out, tmp0, tmp1, tmp2, mid):
    total = own[...] + got[...]
    for t, tmp in enumerate((tmp0, tmp1, tmp2)):
        tmp[...] = total[:, 128 * t : 128 * t + 128]
        for k in range(4):
            for q in range(8):
                mid[q, 11 * k : 11 * k + 11, 128 * t : 128 * t + 128] = tmp[pl.ds(ROWS * k + q, 11, stride=8), :]
    out[...] = mid[...].astype(BF)


def add_kernel(got, out, tmp):
    total = got[0].astype(F32)
    for k in range(1, 8):
        total += got[k].astype(F32)
    tmp[...] = total
    out[...] = jnp.zeros_like(out)
    for k in range(4):
        rows = tmp[11 * k : 11 * k + 11, :]
        out[k, 0:11, :] = rows[:, 0:192]
        out[k + 4, 0:11, :] = rows[:, 192:384]


def prep_kernel(s_ref, so, *refs):
    own, far = refs[:4], refs[4:8]
    w_ref, pred_ref = refs[8:]
    y, c = s_ref[0], s_ref[3]
    for d in range(4):
        base = lax.rem(y + d, 4) * 384
        for e in range(2):
            w_ref[pl.ds(pl.multiple_of(base + 192 * e + 96 * c, 96), 96), :] = own[d][e]
            w_ref[pl.ds(pl.multiple_of(base + 192 * e + 96 * (1 - c), 96), 96), :] = far[d][e]
    pred_ref[...] = lax.dot_general(so[...], w_ref[...], NT, preferred_element_type=F32)


def head_kernel(s_ref, sums, pred, w_ref, out):
    g, c, z = s_ref[5], s_ref[3], s_ref[4]
    summed = jnp.concatenate([sums[AT[j]] for j in range(8)], axis=-1)
    row_mean = jnp.mean(summed, axis=-1, keepdims=True)
    mean_square = jnp.mean(summed * summed, axis=-1, keepdims=True)
    target = (summed - row_mean) * lax.rsqrt(mean_square - row_mean * row_mean + 1e-06)
    j = lax.broadcasted_iota(jnp.int32, (16, 1), 0)
    r = 8 * j + g
    real = (j < 11) & (r < CHUNK) & (2 * CHUNK * z + CHUNK * c + r < VALID)
    pred_grad = jnp.where(real, (pred[...] - target) * (1.0 / math.sqrt(IMAGES * VALID)), 0.0).astype(BF)
    out_grad = jnp.dot(pred_grad, w_ref[...], preferred_element_type=F32).astype(BF)
    wide = pred_grad.astype(F32)
    for k in range(8):
        for e in range(2):
            at = 192 * k + 48 * e
            out[2 * k + e, :, 0:1024] = out_grad
            cut = jnp.concatenate([wide[:, at : at + 48], wide[:, at + 96 : at + 144], jnp.zeros((16, 32), F32)], axis=-1)
            out[2 * k + e, :, 1024:1152] = cut.astype(BF)


def back_kernel(s_ref, own, far, so, hidden, pre, normed, down, out):
    c = s_ref[3]
    og = jnp.concatenate([own[:, 0:1024], far[:, 0:1024]])
    pg = jnp.concatenate([own[:, 1024:1152], far[:, 1024:1152]]).astype(F32)
    pg = jnp.where(c == 0, pg, jnp.concatenate([pg[:, 48:], pg[:, :48]], axis=-1)).astype(BF)
    head = lax.dot_general(pg, so[...], TN, preferred_element_type=F32)[0:48]
    dn = lax.dot_general(hidden[...], og, TN, preferred_element_type=F32)
    hidden_grad = jnp.dot(og, down[...], preferred_element_type=F32)
    x = pre[...]
    k0 = math.sqrt(2 / math.pi)
    t = jnp.tanh(k0 * (x + 0.044715 * (x * x * x)))
    slope = 0.5 * (1.0 + t) + 0.5 * x * (1.0 - t * t) * (k0 * (1.0 + 3 * 0.044715 * (x * x)))
    pre_grad = (hidden_grad * slope).astype(BF)
    up = lax.dot_general(pre_grad, normed[...], TN, preferred_element_type=F32)
    a = jnp.concatenate([up, head[0:24]])
    b = jnp.concatenate([dn, head[24:48]])
    low = lax.broadcasted_iota(jnp.int32, (152, 128), 1) < 64
    for k in range(8):
        at = a[:, 128 * k : 128 * k + 128]
        bt = b[:, 128 * k : 128 * k + 128]
        out[2 * k] = jnp.where(low, at, pltpu.roll(bt, 64, 1)).astype(BF)
        out[2 * k + 1] = jnp.where(low, pltpu.roll(at, 64, 1), bt).astype(BF)


def finish_kernel(got, up, down, head):
    for e in range(2):
        total = got[e].astype(F32)
        for k in range(1, 8):
            total += got[2 * k + e].astype(F32)
        t = total.T
        up[:, 128 * e : 128 * e + 128] = t[0:64, 0:128]
        down[:, 128 * e : 128 * e + 128] = t[64:128, 0:128]
        head[:, 48 * e : 48 * e + 24] = t[0:64, 128:152]
        head[:, 48 * e + 24 : 48 * e + 48] = t[64:128, 128:152]


def swap(x, axis):
    return lax.ppermute(x, axis, SWAP)


def turn(x, axis, n, by):
    return lax.ppermute(x, axis, [(k, (k - by) % n) for k in range(n)])


def spread(x, axis, n):
    x = jnp.broadcast_to(x[None], (n,) + x.shape)
    return lax.all_to_all(x, axis, 0, 0, tiled=True)


def after(x, *others):
    return lax.optimization_barrier((x,) + others)[0]


def inner(teacher_tokens, teacher_qkv, student_tokens, student_gain, w_up, w_down, w_head):
    y, xh, c, z, xl = (lax.axis_index(a) for a in ("y", "xh", "c", "z", "xl"))
    g = 2 * y + xh
    group = jnp.take(jnp.asarray(GROUP, jnp.int32), z)
    scalars = jnp.stack([y, xl, group % 3, c, z, g]).astype(jnp.int32)

    tt = lax.dynamic_slice_in_dim(teacher_tokens, y * 384, 384, 1).reshape(CHUNK, IMAGES, 384)
    rows = jnp.arange(ROWS)[:, None]
    reals = jnp.where((z == 7) & (xl == 1), VALID - 15 * CHUNK, CHUNK)

    def padded(v):
        v = jnp.pad(v, ((0, ROWS - CHUNK), (0, 0)))
        return jnp.where(rows < reals, v, v[79:80])

    mine = padded(jnp.where(xl == 0, tt[:, 0], tt[:, 1]))
    other = padded(jnp.where(xl == 0, tt[:, 1], tt[:, 0]))
    got = lax.ppermute(other, ("c", "xl"), [(0, 1), (3, 2)])
    piece = jnp.where(c == xl, mine, got)
    xa0 = spread(piece, "z", 8).reshape(8 * ROWS, 384)
    xa1 = turn(xa0, "y", 4, 1)
    xa3 = turn(xa0, "y", 4, 3)
    xa1, xa3 = lax.optimization_barrier((xa1, xa3))
    xa2 = turn(xa1[: 4 * ROWS], "y", 4, 1)
    xa2l = turn(xa3[4 * ROWS :], "y", 4, 3)
    xa = (xa0, xa1, xa2, xa2l, xa3)
    xb = tuple(swap(v, "c") for v in xa)

    wt = teacher_qkv[0].T
    main = jnp.where(xl == 0, wt[:192], wt[96:])
    part = jnp.where(xl == 0, wt[192:], wt[:96])
    to_main = [(2 * k + e, 2 * AT[(3 * k + 2 * e) % 8] + e) for k in range(8) for e in range(2)]
    to_part = [(2 * k + e, 2 * AT[(3 * k + 1) % 8] + e) for k in range(8) for e in range(2)]
    m_own = lax.ppermute(main, DP, to_main)
    h_own = lax.ppermute(part, DP, to_part)
    m_oth = swap(m_own, "xl")
    h_oth = swap(h_own, "xl")

    def arranged(v):
        v = jnp.pad(v, ((0, (128 - CHUNK) * IMAGES), (0, 0))).reshape(16, 8, IMAGES, -1)
        return v.transpose(2, 1, 0, 3)

    st_own = arranged(student_tokens)
    st_nb = swap(st_own, "xl")
    up = lax.dynamic_slice_in_dim(w_up, xl * 128, 128, 1)
    down = lax.dynamic_slice_in_dim(w_down, xl * 128, 128, 1)
    normed, pre, hidden, br_own, br_oth, own_in = call(
        student_kernel,
        [((512, 1024), BF), ((512, 128), F32), ((512, 128), BF), ((256, 1024), F32), ((256, 1024), F32), ((16, 1024), BF)],
        scalars, st_own, st_nb, student_gain[None], up, down, scalar=1, flops=300_000_000,
    )
    keep = (br_own + swap(br_oth, "c")).astype(BF).reshape(16, 16, -1)
    keep = lax.all_to_all(keep, ("y", "xh", "xl"), 0, 0, tiled=True)
    student_out, wide = call(join_kernel, [((16, 1024), BF), ((16, 16, 1024), BF)], keep, own_in)
    so_own = lax.all_to_all(wide, ("y", "xh", "xl"), 0, 0, tiled=True).reshape(256, -1)
    so_all = jnp.concatenate([so_own, swap(so_own, "c")])

    wh = w_head.T
    wh2 = swap(wh, "xh")
    pair = jnp.where(xh == 0, jnp.stack([wh, wh2]), jnp.stack([wh2, wh]))
    w_own = [pair] + [turn(pair, "y", 4, k) for k in (1, 2, 3)]
    w_far = [swap(v, "c") for v in w_own]

    t_scalars = after(scalars, student_out)
    half = 8 * ROWS
    total = 2 * half
    own, oth = call(
        teacher_kernel, [((half // 2, 384), F32)] * 2, t_scalars, *xa, *xb, m_own, m_oth, h_own, h_oth,
        scratch=[
            pltpu.VMEM((total, 1536), BF),
            pltpu.VMEM((576, 1536), BF),
            pltpu.VMEM((9, total, 64), BF),
            pltpu.VMEM((3, total, 128), BF),
        ],
        scalar=1, flops=6_000_000_000, vmem=34,
    )
    got = swap(oth, "c")
    (both,) = call(
        pack_kernel, [((8, 44, 384), BF)], own, got,
        scratch=[pltpu.VMEM((half // 2, 128), F32)] * 3 + [pltpu.VMEM((8, 44, 384), F32)],
    )
    both = after(both, so_own)
    got = lax.all_to_all(both, G, 0, 0, tiled=True)
    (sums,) = call(add_kernel, [((8, 16, 192), F32)], got, scratch=[pltpu.VMEM((44, 384), F32)])
    sums = lax.all_to_all(sums, "z", 0, 0, tiled=True)

    w_all, pred = call(
        prep_kernel, [((1536, 1024), BF), ((16, 1536), F32)], scalars, student_out, *w_own, *w_far, scalar=1
    )
    (load,) = call(head_kernel, [((16, 16, 1152), BF)], scalars, sums, pred, w_all, scalar=1)
    load = lax.all_to_all(load, ("y", "xh", "xl"), 0, 0, tiled=True).reshape(256, 1152)
    far = swap(load, "c")

    (grads,) = call(
        back_kernel, [((16, 152, 128), BF)], scalars, load, far, so_all, hidden, pre, normed, down, scalar=1
    )
    grads = lax.all_to_all(grads, DP, 0, 0, tiled=True)
    return tuple(call(finish_kernel, [((64, 256), F32), ((64, 256), F32), ((64, 96), F32)], grads))


def solution(mesh):
    fine = Mesh(mesh.devices.reshape(4, 2, 2, 8, 2), ("y", "xh", "c", "z", "xl"))
    in_specs = (
        P(DP, None),
        P(MEM, None, DP),
        P(DP, None),
        P(),
        P(None, MEM),
        P(None, MEM),
        P(None, MEM),
    )
    out_specs = (P(DP, MEM), P(DP, MEM), P(DP, MEM))
    return jax.shard_map(inner, mesh=fine, in_specs=in_specs, out_specs=out_specs, check_vma=False)
```

time: 251 us -> 230 us (0.916)
  waiting for transfers between devices: 73.9 us -> 52.2 us
  other arithmetic: 24.8 us -> 7.72 us
  starting transfers between devices: 67.6 us -> 81 us
  Pallas kernels: 24.3 us -> 36.5 us
  matrix products: 7.53 us -> 0 us
    all_to_all x6, waiting for transfers between devices: 43.2 us -> 25.1 us  [the longest x1 8.46 us: inner(): keep = lax.all_to_all(keep, ('y', 'xh', 'xl'), 0, 0, tiled=True)]
    all_to_all x6, starting transfers between devices: 34.2 us -> 49.4 us  [the longest x1 13.2 us: inner(): got = lax.all_to_all(both, G, 0, 0, tiled=True)]
    ppermute x18 -> x17, waiting for transfers between devices: 14.9 us -> 2.12 us  [swap(): return lax.ppermute(x, axis, SWAP)]
    pallas_call x1 -> x9, Pallas kernels: 24.3 us -> 36.5 us  [call(): pl.pallas_call(kernel, out_shape=shapes, in_specs=[SM] * scalar + [VM] *...]
    unnamed x46 -> x48, local copies, waits for them, and re-layouts: 5.03 us -> 14.8 us
    ppermute x10, waiting for transfers between devices: 15.9 us -> 25 us  [the longest x1 8.75 us: inner(): got = lax.ppermute(other, ('c', 'xl'), [(0, 1), (3, 2)])]
    select_n x18 -> x5, other arithmetic: 12.8 us -> 4.38 us  [the longest x1 1.8 us: inner(): part = jnp.where(xl == 0, wt[192:], wt[:96])]
    another operation x12 -> x2, local copies, waits for them, and re-layouts: 8.81 us -> 1.17 us  [the longest x1 0.59 us: inner(): scalars = jnp.stack([y, xl, group % 3, c, z, g]).astype(jnp.int32)]
  transfers between devices with their start and end apart: 34 -> 33, of which waited for: 11 -> 12; matrix products, arithmetic and copies ran while one was open for 18% -> 6% of each run, Pallas kernels for 10% -> 14%
where the time goes in v2:
time: 230 us; the launch traced here: 227 us
  starting transfers between devices  81 us (35%)
  waiting for transfers between devices  52.2 us (23%)
  Pallas kernels  36.5 us (16%)
  blocking collectives  25 us (11%)
  local copies, waits for them, and re-layouts  23 us (10%)
  other arithmetic  7.72 us (3%)
    pallas_call x9, Pallas kernels, call(): pl.pallas_call(kernel, out_shape=shapes, in_specs=[SM] * scalar + [VM] *...  36.5 us
    all_to_all x1, blocking collectives, inner(): grads = lax.all_to_all(grads, DP, 0, 0, tiled=True)  25 us
    unnamed x48, local copies, waits for them, and re-layouts  14.8 us
    all_to_all x1, starting transfers between devices, inner(): got = lax.all_to_all(both, G, 0, 0, tiled=True)  13.2 us
    ppermute x17, starting transfers between devices, swap(): return lax.ppermute(x, axis, SWAP)  11.1 us
    ppermute x7, starting transfers between devices, turn(): return lax.ppermute(x, axis, [(k, (k - by) % n) for k in range(n)])  9.04 us
    ppermute x1, waiting for transfers between devices, inner(): got = lax.ppermute(other, ('c', 'xl'), [(0, 1), (3, 2)])  8.75 us
    all_to_all x1, starting transfers between devices, inner(): sums = lax.all_to_all(sums, 'z', 0, 0, tiled=True)  8.57 us
  transfers between devices with their start and end apart: 33, of which 12 were waited for; matrix products, arithmetic and copies ran while one was open for 6% of the time, Pallas kernels for 14%

profile of v2, /device:TPU:8, one launch (start us, length us, event | category | flops | bytes accessed | tf_op | source)
XLA Modules:
  0.0 227.0 jit_solution(294556481661358139)
XLA Ops:
  4.5 2.4 %collective-permute-start.2 = (bf16[88,384]{1,0:T(8,128)(2,1)S(1)}, bf16[88,384]{1,0:T(8,128)(2,1)S(1)}, u32[]{:S(2)}, u32[]{:S(2)}) collective-permute-start(bf16[88,384]{1,0:T(8,128)(2,1)S(1)} %pad_select_fusion), channel_id=1, source_target_pairs={{0,1},{17,16},{2,3},{19,18},{4,5},{21,20},{6,7},{23,22},{8,9},{25,... | collective-permute-start | bytes 202760 | tf_op jit(solution)/shard_map/ppermute | solution.py:262
  7.0 8.8 %collective-permute-done.2 = bf16[88,384]{1,0:T(8,128)(2,1)S(1)} collective-permute-done((bf16[88,384]{1,0:T(8,128)(2,1)S(1)}, bf16[88,384]{1,0:T(8,128)(2,1)S(1)}, u32[]{:S(2)}, u32[]{:S(2)}) %collective-permute-start.2) | collective-permute-done | bytes 67616 | tf_op jit(solution)/shard_map/ppermute | solution.py:262
  16.7 8.5 %all-to-all-start.1 = ((bf16[8,88,384]{2,1,0:T(8,128)(2,1)}), bf16[8,88,384]{2,1,0:T(8,128)(2,1)}, u32[]{:S(2)}, u32[]{:S(2)}) async-start(bf16[8,88,384]{2,1,0:T(8,128)(2,1)} %broadcast_in_dim.49), calls=%async_computation.1 | async-start | bytes 1081344 | tf_op jit(solution)/shard_map/all_to_all | solution.py:239
  26.0 6.0 %collective-permute-start.12 = (bf16[192,1536]{1,0:T(8,128)(2,1)}, bf16[192,1536]{1,0:T(8,128)(2,1)}, u32[]{:S(2)}, u32[]{:S(2)}) collective-permute-start(bf16[192,1536]{1,0:T(8,128)(2,1)} %slice_select_fusion), channel_id=1, source_target_pairs={{0,0},{1,3},{2,6},{3,9},{4,14},{5,1},{6,4},{7,7},{8,12},{9,15},{10... | collective-permute-start | bytes 1769480 | tf_op jit(solution)/shard_map/ppermute | solution.py:278
  38.0 3.3 %shard_map.103 = (bf16[512,1024]{1,0:T(8,128)(2,1)S(1)}, f32[512,128]{1,0:T(8,128)S(1)}, bf16[512,128]{1,0:T(8,128)(2,1)S(1)}, f32[256,1024]{1,0:T(8,128)S(1)}, ...) custom-call(s32[6]{0:T(128)S(1)} %copy-done.12, bf16[2,8,16,1024]{3,2,1,0:T(8,128)(2,1)S(1)} %bitcast.32, ...), custom_call_target="tpu_custom_call" | custom-call | flops 300000000 | bytes 5148696 | tf_op jit(solution)/shard_map/pallas_call | solution.py:95
  43.0 1.8 slice_select_fusion.1
  44.8 3.0 %collective-permute-start.14 = (bf16[96,1536]{1,0:T(8,128)(2,1)}, bf16[96,1536]{1,0:T(8,128)(2,1)S(1)}, u32[]{:S(2)}, u32[]{:S(2)}) collective-permute-start(bf16[96,1536]{1,0:T(8,128)(2,1)} %slice_select_fusion.1), channel_id=1, source_target_pairs={{0,4},{1,5},{2,12},{3,13},{4,10},{5,11},{6,2},{7,3},{8,8},{9,9},{1... | collective-permute-start | bytes 884744 | tf_op jit(solution)/shard_map/ppermute | solution.py:279
  47.9 5.3 %collective-permute-start.13 = (bf16[192,1536]{1,0:T(8,128)(2,1)}, bf16[192,1536]{1,0:T(8,128)(2,1)}, u32[]{:S(2)}, u32[]{:S(2)}) collective-permute-start(bf16[192,1536]{1,0:T(8,128)(2,1)} %collective-permute-done.12.m_own), channel_id=1, source_target_pairs={{0,1},{1,0},{2,3},{3,2},{4,5},{5,4},{6,7},{7,6},{8,9},{9,8},{10,11... | collective-permute-start | bytes 1769480 | tf_op jit(solution)/shard_map/ppermute | solution.py:230
  55.2 7.7 %collective-permute-done.14.h_own = bf16[96,1536]{1,0:T(8,128)(2,1)S(1)} collective-permute-done((bf16[96,1536]{1,0:T(8,128)(2,1)}, bf16[96,1536]{1,0:T(8,128)(2,1)S(1)}, u32[]{:S(2)}, u32[]{:S(2)}) %collective-permute-start.14) | collective-permute-done | bytes 294944 | tf_op jit(solution)/shard_map/ppermute | solution.py:279
  62.9 2.9 %collective-permute-done.3.xa1 = bf16[704,384]{1,0:T(8,128)(2,1)} collective-permute-done((bf16[704,384]{1,0:T(8,128)(2,1)}, bf16[704,384]{1,0:T(8,128)(2,1)}, u32[]{:S(2)}, u32[]{:S(2)}) %collective-permute-start.3) | collective-permute-done | bytes 540704 | tf_op jit(solution)/shard_map/ppermute | solution.py:234
  72.6 2.2 collective-permute-start.5
  74.8 2.1 add_convert_fusion
  77.0 8.2 %all-to-all-start = ((bf16[16,16,1024]{2,1,0:T(8,128)(2,1)}), bf16[16,16,1024]{2,1,0:T(8,128)(2,1)S(1)}, u32[]{:S(2)}, u32[]{:S(2)}) async-start(bf16[16,16,1024]{2,1,0:T(8,128)(2,1)} %bitcast.36), calls=%async_computation | async-start | bytes 1048576 | tf_op jit(solution)/shard_map/all_to_all | solution.py:297
  85.8 8.5 %all-to-all-done.keep = bf16[16,16,1024]{2,1,0:T(8,128)(2,1)S(1)} async-done(((bf16[16,16,1024]{2,1,0:T(8,128)(2,1)}), bf16[16,16,1024]{2,1,0:T(8,128)(2,1)S(1)}, u32[]{:S(2)}, u32[]{:S(2)}) %all-to-all-start) | async-done | bytes 524320 | tf_op jit(solution)/shard_map/all_to_all | solution.py:297
  96.6 2.1 collective-permute-start.17
  101.2 23.9 %shard_map.105 = (f32[352,384]{1,0:T(8,128)S(1)}, f32[352,384]{1,0:T(8,128)}) custom-call(s32[6]{0:T(128)S(1)} %copy-done.13, bf16[704,384]{1,0:T(8,128)(2,1)} %bitcast.11.xa0, bf16[704,384]{1,0:T(8,128)(2,1)} %collective-permute-done.3.xa1, bf16[352,384]{1,0:T(8,128)(2,1)} %collective-permute-done.5.xa2, bf16[352,384]{1,0:T(8,128)(2,1)} %collective-permute-done.6.xa2l, ...), custom_call_target="tpu_custom_call" | custom-call | flops 6000000000 | bytes 7176216 | tf_op jit(solution)/shard_map/pallas_call | solution.py:95
  125.2 5.7 %all-to-all-start.2 = ((bf16[16,16,1024]{2,1,0:T(8,128)(2,1)}), bf16[16,16,1024]{2,1,0:T(8,128)(2,1)}, u32[]{:S(2)}, u32[]{:S(2)}) async-start(bf16[16,16,1024]{2,1,0:T(8,128)(2,1)} %copy-done.5), calls=%async_computation.2 | async-start | bytes 1048576 | tf_op jit(solution)/shard_map/all_to_all | solution.py:299
  132.5 2.8 %collective-permute-start.19 = (bf16[2,96,1024]{2,1,0:T(8,128)(2,1)S(1)}, bf16[2,96,1024]{2,1,0:T(8,128)(2,1)}, u32[]{:S(2)}, u32[]{:S(2)}) collective-permute-start(bf16[2,96,1024]{2,1,0:T(8,128)(2,1)S(1)} %maximum_select_fusion.refs_0_), channel_id=1, source_target_pairs={{0,128},{64,192},{128,0},{192,64},{1,129},{65,193},{129,1},{193,65... | collective-permute-start | bytes 1179656 | tf_op jit(solution)/shard_map/ppermute | solution.py:234
  135.2 1.8 collective-permute-start.20
  138.0 2.8 %all-to-all-done.2 = bf16[16,16,1024]{2,1,0:T(8,128)(2,1)} async-done(((bf16[16,16,1024]{2,1,0:T(8,128)(2,1)}), bf16[16,16,1024]{2,1,0:T(8,128)(2,1)}, u32[]{:S(2)}, u32[]{:S(2)}) %all-to-all-start.2) | async-done | bytes 524320 | tf_op jit(solution)/shard_map/all_to_all | solution.py:299
  140.7 13.2 %all-to-all-start.3 = ((bf16[8,44,384]{2,1,0:T(8,128)(2,1)}), bf16[8,44,384]{2,1,0:T(8,128)(2,1)S(1)}, u32[]{:S(2)}, u32[]{:S(2)}) async-start(bf16[8,44,384]{2,1,0:T(8,128)(2,1)} %shard_map.106), calls=%async_computation.3 | async-start | bytes 589824 | tf_op jit(solution)/shard_map/all_to_all | solution.py:327
  154.4 4.2 %collective-permute-done.19.refs_2_ = bf16[2,96,1024]{2,1,0:T(8,128)(2,1)} collective-permute-done((bf16[2,96,1024]{2,1,0:T(8,128)(2,1)S(1)}, bf16[2,96,1024]{2,1,0:T(8,128)(2,1)}, u32[]{:S(2)}, u32[]{:S(2)}) %collective-permute-start.19) | collective-permute-done | bytes 393248 | tf_op jit(solution)/shard_map/ppermute | solution.py:234
  159.1 2.0 all-to-all-done.3.got
  161.9 8.6 %all-to-all-start.4 = ((f32[8,16,192]{2,1,0:T(8,128)}), f32[8,16,192]{2,1,0:T(8,128)S(1)}, u32[]{:S(2)}, u32[]{:S(2)}) async-start(f32[8,16,192]{2,1,0:T(8,128)} %shard_map.107), calls=%async_computation.4 | async-start | bytes 262144 | tf_op jit(solution)/shard_map/all_to_all | solution.py:329
  171.8 2.6 %shard_map.108 = (bf16[1536,1024]{1,0:T(8,128)(2,1)S(1)}, f32[16,1536]{1,0:T(8,128)S(1)}) custom-call(s32[6]{0:T(128)S(1)} %copy-done.14, bf16[16,1024]{1,0:T(8,128)(2,1)S(1)} %copy-done.9, bf16[2,96,1024]{2,1,0:T(8,128)(2,1)S(1)} %maximum_select_fusion.refs_0_, bf16[2,96,1024]{2,1,0:T(8,128)(2,1)} %collective-permute-done.18.refs_1_, ...), custom_call_target="tpu_custom_call" | custom-call | bytes 6422552 | tf_op jit(solution)/shard_map/pallas_call | solution.py:95
  176.1 3.5 %all-to-all-done.4.sums = f32[8,16,192]{2,1,0:T(8,128)S(1)} async-done(((f32[8,16,192]{2,1,0:T(8,128)}), f32[8,16,192]{2,1,0:T(8,128)S(1)}, u32[]{:S(2)}, u32[]{:S(2)}) %all-to-all-start.4) | async-done | bytes 98336 | tf_op jit(solution)/shard_map/all_to_all | solution.py:329
  179.5 1.9 copy-done.2
  181.4 2.0 shard_map.109
  183.5 5.3 %all-to-all-start.5 = ((bf16[16,16,1152]{2,1,0:T(8,128)(2,1)}), bf16[16,16,1152]{2,1,0:T(8,128)(2,1)S(1)}, u32[]{:S(2)}, u32[]{:S(2)}) async-start(bf16[16,16,1152]{2,1,0:T(8,128)(2,1)} %shard_map.109), calls=%async_computation.5 | async-start | bytes 1179648 | tf_op jit(solution)/shard_map/all_to_all | solution.py:335
  188.8 8.4 %all-to-all-done.5 = bf16[16,16,1152]{2,1,0:T(8,128)(2,1)S(1)} async-done(((bf16[16,16,1152]{2,1,0:T(8,128)(2,1)}), bf16[16,16,1152]{2,1,0:T(8,128)(2,1)S(1)}, u32[]{:S(2)}, u32[]{:S(2)}) %all-to-all-start.5) | async-done | bytes 589856 | tf_op jit(solution)/shard_map/all_to_all | solution.py:335
  199.2 2.0 shard_map.110
  201.2 25.0 %all_to_all.35.got = bf16[16,152,128]{2,1,0:T(8,128)(2,1)S(1)} all-to-all(bf16[16,152,128]{2,1,0:T(8,128)(2,1)S(1)} %shard_map.110), channel_id=1, replica_groups=mesh['y'=4,'xh'=2,'c'=2,'z'=8,'xl'=2] {'z','xl'}, dimensions={0} | all-to-all | bytes 1245184 | tf_op jit(solution)/shard_map/all_to_all | solution.py:341
  (114 shorter events, 37.1 us)
Async XLA Ops:
  2.3 32.6 %collective-permute-start = (bf16[2,8,16,1024]{3,2,1,0:T(8,128)(2,1)S(1)}, bf16[2,8,16,1024]{3,2,1,0:T(8,128)(2,1)S(1)}, u32[]{:S(2)}, u32[]{:S(2)}) collective-permute-start(bf16[2,8,16,1024]{3,2,1,0:T(8,128)(2,1)S(1)} %bitcast.31), channel_id=1, source_target_pairs={{0,1},{1,0},{2,3},{3,2},{4,5},{5,4},{6,7},{7,6},{8,9},{9,8},{10,11... | collective-permute-start | bytes 1572872 | tf_op jit(solution)/shard_map/ppermute | solution.py:230
  4.5 11.3 %collective-permute-start.2 = (bf16[88,384]{1,0:T(8,128)(2,1)S(1)}, bf16[88,384]{1,0:T(8,128)(2,1)S(1)}, u32[]{:S(2)}, u32[]{:S(2)}) collective-permute-start(bf16[88,384]{1,0:T(8,128)(2,1)S(1)} %pad_select_fusion), channel_id=1, source_target_pairs={{0,1},{17,16},{2,3},{19,18},{4,5},{21,20},{6,7},{23,22},{8,9},{25,... | collective-permute-start | bytes 202760 | tf_op jit(solution)/shard_map/ppermute | solution.py:262
  16.7 36.5 %all-to-all-start.1 = ((bf16[8,88,384]{2,1,0:T(8,128)(2,1)}), bf16[8,88,384]{2,1,0:T(8,128)(2,1)}, u32[]{:S(2)}, u32[]{:S(2)}) async-start(bf16[8,88,384]{2,1,0:T(8,128)(2,1)} %broadcast_in_dim.49), calls=%async_computation.1 | async-start | bytes 1081344 | tf_op jit(solution)/shard_map/all_to_all | solution.py:239
  26.0 21.8 %collective-permute-start.12 = (bf16[192,1536]{1,0:T(8,128)(2,1)}, bf16[192,1536]{1,0:T(8,128)(2,1)}, u32[]{:S(2)}, u32[]{:S(2)}) collective-permute-start(bf16[192,1536]{1,0:T(8,128)(2,1)} %slice_select_fusion), channel_id=1, source_target_pairs={{0,0},{1,3},{2,6},{3,9},{4,14},{5,1},{6,4},{7,7},{8,12},{9,15},{10... | collective-permute-start | bytes 1769480 | tf_op jit(solution)/shard_map/ppermute | solution.py:278
  42.6 32.2 %collective-permute-start.1 = (f32[256,1024]{1,0:T(8,128)}, f32[256,1024]{1,0:T(8,128)}, u32[]{:S(2)}, u32[]{:S(2)}) collective-permute-start(f32[256,1024]{1,0:T(8,128)} %get-tuple-element.20), channel_id=1, source_target_pairs={{0,16},{16,0},{1,17},{17,1},{2,18},{18,2},{3,19},{19,3},{4,20},{20... | collective-permute-start | bytes 3145736 | tf_op jit(solution)/shard_map/ppermute | solution.py:230
  44.8 18.0 %collective-permute-start.14 = (bf16[96,1536]{1,0:T(8,128)(2,1)}, bf16[96,1536]{1,0:T(8,128)(2,1)S(1)}, u32[]{:S(2)}, u32[]{:S(2)}) collective-permute-start(bf16[96,1536]{1,0:T(8,128)(2,1)} %slice_select_fusion.1), channel_id=1, source_target_pairs={{0,4},{1,5},{2,12},{3,13},{4,10},{5,11},{6,2},{7,3},{8,8},{9,9},{1... | collective-permute-start | bytes 884744 | tf_op jit(solution)/shard_map/ppermute | solution.py:279
  47.9 24.7 %collective-permute-start.13 = (bf16[192,1536]{1,0:T(8,128)(2,1)}, bf16[192,1536]{1,0:T(8,128)(2,1)}, u32[]{:S(2)}, u32[]{:S(2)}) collective-permute-start(bf16[192,1536]{1,0:T(8,128)(2,1)} %collective-permute-done.12.m_own), channel_id=1, source_target_pairs={{0,1},{1,0},{2,3},{3,2},{4,5},{5,4},{6,7},{7,6},{8,9},{9,8},{10,11... | collective-permute-start | bytes 1769480 | tf_op jit(solution)/shard_map/ppermute | solution.py:230
  53.2 12.6 %collective-permute-start.3 = (bf16[704,384]{1,0:T(8,128)(2,1)}, bf16[704,384]{1,0:T(8,128)(2,1)}, u32[]{:S(2)}, u32[]{:S(2)}) collective-permute-start(bf16[704,384]{1,0:T(8,128)(2,1)} %bitcast.11.xa0), channel_id=1, source_target_pairs={{0,192},{64,0},{128,64},{192,128},{1,193},{65,1},{129,65},{193,129... | collective-permute-start | bytes 1622024 | tf_op jit(solution)/shard_map/ppermute | solution.py:234
  53.6 13.6 %collective-permute-start.4 = (bf16[704,384]{1,0:T(8,128)(2,1)}, bf16[704,384]{1,0:T(8,128)(2,1)}, u32[]{:S(2)}, u32[]{:S(2)}) collective-permute-start(bf16[704,384]{1,0:T(8,128)(2,1)} %bitcast.11.xa0), channel_id=1, source_target_pairs={{0,64},{64,128},{128,192},{192,0},{1,65},{65,129},{129,193},{193,1... | collective-permute-start | bytes 1622024 | tf_op jit(solution)/shard_map/ppermute | solution.py:234
  62.9 9.0 %collective-permute-start.15 = (bf16[96,1536]{1,0:T(8,128)(2,1)S(1)}, bf16[96,1536]{1,0:T(8,128)(2,1)S(1)}, u32[]{:S(2)}, u32[]{:S(2)}) collective-permute-start(bf16[96,1536]{1,0:T(8,128)(2,1)S(1)} %collective-permute-done.14.h_own), channel_id=1, source_target_pairs={{0,1},{1,0},{2,3},{3,2},{4,5},{5,4},{6,7},{7,6},{8,9},{9,8},{10,11... | collective-permute-start | bytes 884744 | tf_op jit(solution)/shard_map/ppermute | solution.py:230
  65.8 30.8 %collective-permute-start.7 = (bf16[704,384]{1,0:T(8,128)(2,1)}, bf16[704,384]{1,0:T(8,128)(2,1)}, u32[]{:S(2)}, u32[]{:S(2)}) collective-permute-start(bf16[704,384]{1,0:T(8,128)(2,1)} %bitcast.11.xa0), channel_id=1, source_target_pairs={{0,16},{16,0},{1,17},{17,1},{2,18},{18,2},{3,19},{19,3},{4,20},{20... | collective-permute-start | bytes 1622024 | tf_op jit(solution)/shard_map/ppermute | solution.py:230
  69.0 29.7 %collective-permute-start.8 = (bf16[704,384]{1,0:T(8,128)(2,1)}, bf16[704,384]{1,0:T(8,128)(2,1)}, u32[]{:S(2)}, u32[]{:S(2)}) collective-permute-start(bf16[704,384]{1,0:T(8,128)(2,1)} %collective-permute-done.3.xa1), channel_id=1, source_target_pairs={{0,16},{16,0},{1,17},{17,1},{2,18},{18,2},{3,19},{19,3},{4,20},{20... | collective-permute-start | bytes 1622024 | tf_op jit(solution)/shard_map/ppermute | solution.py:230
  72.6 26.1 %collective-permute-start.11 = (bf16[704,384]{1,0:T(8,128)(2,1)}, bf16[704,384]{1,0:T(8,128)(2,1)}, u32[]{:S(2)}, u32[]{:S(2)}) collective-permute-start(bf16[704,384]{1,0:T(8,128)(2,1)} %collective-permute-done.4.xa3), channel_id=1, source_target_pairs={{0,16},{16,0},{1,17},{17,1},{2,18},{18,2},{3,19},{19,3},{4,20},{20... | collective-permute-start | bytes 1622024 | tf_op jit(solution)/shard_map/ppermute | solution.py:230
  72.6 12.6 %collective-permute-start.5 = (bf16[352,384]{1,0:T(8,128)(2,1)}, bf16[352,384]{1,0:T(8,128)(2,1)}, u32[]{:S(2)}, u32[]{:S(2)}) collective-permute-start(bf16[352,384]{1,0:T(8,128)(2,1)} %slice.40), channel_id=1, source_target_pairs={{0,192},{64,0},{128,64},{192,128},{1,193},{65,1},{129,65},{193,129... | collective-permute-start | bytes 811016 | tf_op jit(solution)/shard_map/ppermute | solution.py:234
  74.8 10.5 %collective-permute-start.6 = (bf16[352,384]{1,0:T(8,128)(2,1)}, bf16[352,384]{1,0:T(8,128)(2,1)}, u32[]{:S(2)}, u32[]{:S(2)}) collective-permute-start(bf16[352,384]{1,0:T(8,128)(2,1)} %slice.41), channel_id=1, source_target_pairs={{0,64},{64,128},{128,192},{192,0},{1,65},{65,129},{129,193},{193,1... | collective-permute-start | bytes 811016 | tf_op jit(solution)/shard_map/ppermute | solution.py:234
  77.0 17.3 %all-to-all-start = ((bf16[16,16,1024]{2,1,0:T(8,128)(2,1)}), bf16[16,16,1024]{2,1,0:T(8,128)(2,1)S(1)}, u32[]{:S(2)}, u32[]{:S(2)}) async-start(bf16[16,16,1024]{2,1,0:T(8,128)(2,1)} %bitcast.36), calls=%async_computation | async-start | bytes 1048576 | tf_op jit(solution)/shard_map/all_to_all | solution.py:297
  85.2 13.4 %collective-permute-start.9 = (bf16[352,384]{1,0:T(8,128)(2,1)}, bf16[352,384]{1,0:T(8,128)(2,1)S(1)}, u32[]{:S(2)}, u32[]{:S(2)}) collective-permute-start(bf16[352,384]{1,0:T(8,128)(2,1)} %collective-permute-done.5.xa2), channel_id=1, source_target_pairs={{0,16},{16,0},{1,17},{17,1},{2,18},{18,2},{3,19},{19,3},{4,20},{20... | collective-permute-start | bytes 811016 | tf_op jit(solution)/shard_map/ppermute | solution.py:230
  85.3 13.3 %collective-permute-start.10 = (bf16[352,384]{1,0:T(8,128)(2,1)}, bf16[352,384]{1,0:T(8,128)(2,1)S(1)}, u32[]{:S(2)}, u32[]{:S(2)}) collective-permute-start(bf16[352,384]{1,0:T(8,128)(2,1)} %collective-permute-done.6.xa2l), channel_id=1, source_target_pairs={{0,16},{16,0},{1,17},{17,1},{2,18},{18,2},{3,19},{19,3},{4,20},{20... | collective-permute-start | bytes 811016 | tf_op jit(solution)/shard_map/ppermute | solution.py:230
  96.6 34.4 %collective-permute-start.17 = (bf16[96,1024]{1,0:T(8,128)(2,1)}, bf16[96,1024]{1,0:T(8,128)(2,1)}, u32[]{:S(2)}, u32[]{:S(2)}) collective-permute-start(bf16[96,1024]{1,0:T(8,128)(2,1)} %bitcast.39), channel_id=1, source_target_pairs={{0,32},{32,0},{1,33},{33,1},{2,34},{34,2},{3,35},{35,3},{4,36},{36... | collective-permute-start | bytes 589832 | tf_op jit(solution)/shard_map/ppermute | solution.py:230
  125.1 11.9 %collective-permute-start.16 = (f32[352,384]{1,0:T(8,128)}, f32[352,384]{1,0:T(8,128)S(1)}, u32[]{:S(2)}, u32[]{:S(2)}) collective-permute-start(f32[352,384]{1,0:T(8,128)} %get-tuple-element.27), channel_id=1, source_target_pairs={{0,16},{16,0},{1,17},{17,1},{2,18},{18,2},{3,19},{19,3},{4,20},{20... | collective-permute-start | bytes 1622024 | tf_op jit(solution)/shard_map/ppermute | solution.py:230
  125.2 15.5 %all-to-all-start.2 = ((bf16[16,16,1024]{2,1,0:T(8,128)(2,1)}), bf16[16,16,1024]{2,1,0:T(8,128)(2,1)}, u32[]{:S(2)}, u32[]{:S(2)}) async-start(bf16[16,16,1024]{2,1,0:T(8,128)(2,1)} %copy-done.5), calls=%async_computation.2 | async-start | bytes 1048576 | tf_op jit(solution)/shard_map/all_to_all | solution.py:299
  132.2 21.7 %collective-permute-start.18 = (bf16[2,96,1024]{2,1,0:T(8,128)(2,1)S(1)}, bf16[2,96,1024]{2,1,0:T(8,128)(2,1)}, u32[]{:S(2)}, u32[]{:S(2)}) collective-permute-start(bf16[2,96,1024]{2,1,0:T(8,128)(2,1)S(1)} %maximum_select_fusion.refs_0_), channel_id=1, source_target_pairs={{0,192},{64,0},{128,64},{192,128},{1,193},{65,1},{129,65},{193,129... | collective-permute-start | bytes 1179656 | tf_op jit(solution)/shard_map/ppermute | solution.py:234
  132.5 26.1 %collective-permute-start.19 = (bf16[2,96,1024]{2,1,0:T(8,128)(2,1)S(1)}, bf16[2,96,1024]{2,1,0:T(8,128)(2,1)}, u32[]{:S(2)}, u32[]{:S(2)}) collective-permute-start(bf16[2,96,1024]{2,1,0:T(8,128)(2,1)S(1)} %maximum_select_fusion.refs_0_), channel_id=1, source_target_pairs={{0,128},{64,192},{128,0},{192,64},{1,129},{65,193},{129,1},{193,65... | collective-permute-start | bytes 1179656 | tf_op jit(solution)/shard_map/ppermute | solution.py:234
  135.2 23.3 %collective-permute-start.20 = (bf16[2,96,1024]{2,1,0:T(8,128)(2,1)S(1)}, bf16[2,96,1024]{2,1,0:T(8,128)(2,1)}, u32[]{:S(2)}, u32[]{:S(2)}) collective-permute-start(bf16[2,96,1024]{2,1,0:T(8,128)(2,1)S(1)} %maximum_select_fusion.refs_0_), channel_id=1, source_target_pairs={{0,64},{64,128},{128,192},{192,0},{1,65},{65,129},{129,193},{193,1... | collective-permute-start | bytes 1179656 | tf_op jit(solution)/shard_map/ppermute | solution.py:234
  140.7 20.3 %all-to-all-start.3 = ((bf16[8,44,384]{2,1,0:T(8,128)(2,1)}), bf16[8,44,384]{2,1,0:T(8,128)(2,1)S(1)}, u32[]{:S(2)}, u32[]{:S(2)}) async-start(bf16[8,44,384]{2,1,0:T(8,128)(2,1)} %shard_map.106), calls=%async_computation.3 | async-start | bytes 589824 | tf_op jit(solution)/shard_map/all_to_all | solution.py:327
  153.9 16.6 %collective-permute-start.21 = (bf16[2,96,1024]{2,1,0:T(8,128)(2,1)S(1)}, bf16[2,96,1024]{2,1,0:T(8,128)(2,1)S(1)}, u32[]{:S(2)}, u32[]{:S(2)}) collective-permute-start(bf16[2,96,1024]{2,1,0:T(8,128)(2,1)S(1)} %maximum_select_fusion.refs_0_), channel_id=1, source_target_pairs={{0,16},{16,0},{1,17},{17,1},{2,18},{18,2},{3,19},{19,3},{4,20},{20... | collective-permute-start | bytes 1179656 | tf_op jit(solution)/shard_map/ppermute | solution.py:230
  153.9 16.6 %collective-permute-start.22 = (bf16[2,96,1024]{2,1,0:T(8,128)(2,1)}, bf16[2,96,1024]{2,1,0:T(8,128)(2,1)S(1)}, u32[]{:S(2)}, u32[]{:S(2)}) collective-permute-start(bf16[2,96,1024]{2,1,0:T(8,128)(2,1)} %collective-permute-done.18.refs_1_), channel_id=1, source_target_pairs={{0,16},{16,0},{1,17},{17,1},{2,18},{18,2},{3,19},{19,3},{4,20},{20... | collective-permute-start | bytes 1179656 | tf_op jit(solution)/shard_map/ppermute | solution.py:230
  158.6 11.9 %collective-permute-start.23 = (bf16[2,96,1024]{2,1,0:T(8,128)(2,1)}, bf16[2,96,1024]{2,1,0:T(8,128)(2,1)}, u32[]{:S(2)}, u32[]{:S(2)}) collective-permute-start(bf16[2,96,1024]{2,1,0:T(8,128)(2,1)} %collective-permute-done.19.refs_2_), channel_id=1, source_target_pairs={{0,16},{16,0},{1,17},{17,1},{2,18},{18,2},{3,19},{19,3},{4,20},{20... | collective-permute-start | bytes 1179656 | tf_op jit(solution)/shard_map/ppermute | solution.py:230
  158.6 11.9 %collective-permute-start.24 = (bf16[2,96,1024]{2,1,0:T(8,128)(2,1)}, bf16[2,96,1024]{2,1,0:T(8,128)(2,1)}, u32[]{:S(2)}, u32[]{:S(2)}) collective-permute-start(bf16[2,96,1024]{2,1,0:T(8,128)(2,1)} %collective-permute-done.20.refs_3_), channel_id=1, source_target_pairs={{0,16},{16,0},{1,17},{17,1},{2,18},{18,2},{3,19},{19,3},{4,20},{20... | collective-permute-start | bytes 1179656 | tf_op jit(solution)/shard_map/ppermute | solution.py:230
  161.9 17.6 %all-to-all-start.4 = ((f32[8,16,192]{2,1,0:T(8,128)}), f32[8,16,192]{2,1,0:T(8,128)S(1)}, u32[]{:S(2)}, u32[]{:S(2)}) async-start(f32[8,16,192]{2,1,0:T(8,128)} %shard_map.107), calls=%async_computation.4 | async-start | bytes 262144 | tf_op jit(solution)/shard_map/all_to_all | solution.py:329
  183.5 13.7 %all-to-all-start.5 = ((bf16[16,16,1152]{2,1,0:T(8,128)(2,1)}), bf16[16,16,1152]{2,1,0:T(8,128)(2,1)S(1)}, u32[]{:S(2)}, u32[]{:S(2)}) async-start(bf16[16,16,1152]{2,1,0:T(8,128)(2,1)} %shard_map.109), calls=%async_computation.5 | async-start | bytes 1179648 | tf_op jit(solution)/shard_map/all_to_all | solution.py:335
  188.8 8.4 %collective-permute-start.26 = (bf16[256,1024]{1,0:T(8,128)(2,1)}, bf16[256,1024]{1,0:T(8,128)(2,1)S(1)}, u32[]{:S(2)}, u32[]{:S(2)}) collective-permute-start(bf16[256,1024]{1,0:T(8,128)(2,1)} %bitcast.15), channel_id=1, source_target_pairs={{0,16},{16,0},{1,17},{17,1},{2,18},{18,2},{3,19},{19,3},{4,20},{20... | collective-permute-start | bytes 1572872 | tf_op jit(solution)/shard_map/ppermute | solution.py:230
  (24 other events, 116.4 us)

commit v3 on v2

--- a/solution.py
+++ b/solution.py
@@ -12,7 +12,6 @@
 BF = jnp.bfloat16
 F32 = jnp.float32
 MEM = ("y", "xh", "c")
-G = ("y", "xh")
 DP = ("z", "xl")
 GROUP = (0, 2, 1, 3, 5, 7, 4, 6)
 AT = tuple(GROUP.index(j) for j in range(8))
@@ -37,7 +36,7 @@
     wt[pl.ds(pl.multiple_of((1 - xl) * 384, 384), 192), :] = m_oth[...]
     wt[pl.ds(pl.multiple_of(192 + xl * 96, 96), 96), :] = h_own[...]
     wt[pl.ds(pl.multiple_of(192 + (1 - xl) * 96, 96), 96), :] = h_oth[...]
-    blk = 176
+    blk = 352
 
     def project(i, carry):
         r0 = pl.multiple_of(i * blk, blk)
@@ -64,23 +63,16 @@
         vx[h, :, 0:64] = vals.astype(BF)
         vx[h, :, 64:128] = ones
 
-    def attend(i, out_ref, base, at):
-        r0 = pl.multiple_of(i * blk, blk)
+    for out_ref, base in ((oth_ref, half), (own_ref, 0)):
         for h in range(3):
-            q = p_sc[q0 + h, pl.ds(base + r0, blk), :] * jnp.asarray(0.125, BF)
+            q = p_sc[q0 + h, pl.ds(base, half), :] * jnp.asarray(0.125, BF)
             s = lax.dot_general(q, p_sc[k0 + h], (((1,), (1,)), ((), ())), preferred_element_type=F32)
             m = jnp.max(s, axis=1, keepdims=True)
             p = jnp.exp(s - m).astype(BF)
             o = jnp.dot(p, vx[h], preferred_element_type=F32)
-            out_ref[pl.ds(r0, blk), at + 64 * h : at + 64 * h + 64] = o[:, 0:64] / o[:, 64:65]
-
-    quarter = half // 2
-    for k, (out_ref, at) in enumerate(((oth_ref, 0), (oth_ref, 192), (own_ref, 0), (own_ref, 192))):
-        base = (half if k < 2 else 0) + (k % 2) * quarter
-
-        @pl.loop(0, quarter // blk)
-        def _(i, out_ref=out_ref, base=base, at=at):
-            attend(i, out_ref, base, at)
+            context = o[:, 0:64] / o[:, 64:65]
+            out_ref[:, 64 * h : 64 * h + 64] = context[0 : half // 2]
+            out_ref[:, 192 + 64 * h : 256 + 64 * h] = context[half // 2 :]
 
 
 VM = pl.BlockSpec(memory_space=pltpu.VMEM)
@@ -89,13 +81,13 @@
 NT = (((1,), (1,)), ((), ()))
 
 
-def call(kernel, outs, *args, scratch=(), scalar=0, flops=0, vmem=24):
+def call(kernel, outs, *args, scratch=(), scalar=0, away=0, flops=0, vmem=24):
     shapes = [jax.ShapeDtypeStruct(s, d) for s, d in outs]
     moved = sum(math.prod(v.shape) * v.dtype.itemsize for v in args) + sum(math.prod(s.shape) * s.dtype.itemsize for s in shapes)
     return pl.pallas_call(
         kernel,
         out_shape=shapes,
-        in_specs=[SM] * scalar + [VM] * (len(args) - scalar),
+        in_specs=[SM] * scalar + [pl.BlockSpec(memory_space=pltpu.HBM)] * away + [VM] * (len(args) - scalar - away),
         out_specs=[VM] * len(shapes),
         scratch_shapes=list(scratch),
         compiler_params=pltpu.CompilerParams(vmem_limit_bytes=vmem * 2**20),
@@ -106,23 +98,26 @@
 def student_kernel(s_ref, own, nb, gain, up, down, normed, pre, hidden, br_own, br_oth, own_in):
     xl, c, g = s_ref[1], s_ref[3], s_ref[5]
     mine = c == xl
-    for b in range(2):
-        for q in range(8):
+
+    @pl.loop(0, 8)
+    def _(q):
+        for b in range(2):
             for e in range(2):
                 first, second = (own, nb) if b == 0 else (nb, own)
                 x = jnp.where(mine, first[e, q].astype(F32), second[e, q].astype(F32))
                 mean = jnp.mean(x, axis=-1, keepdims=True)
                 dev = x - mean
                 var = jnp.mean(dev * dev, axis=-1, keepdims=True)
-                at = 256 * b + 32 * q + 16 * e
-                normed[at : at + 16, :] = (dev * lax.rsqrt(var + 1e-06) * gain[...]).astype(BF)
+                at = pl.multiple_of(256 * b + 32 * q + 16 * e, 16)
+                normed[pl.ds(at, 16), :] = (dev * lax.rsqrt(var + 1e-06) * gain[...]).astype(BF)
+
     x = jnp.dot(normed[...], up[...], preferred_element_type=F32)
     pre[...] = x
     k0 = math.sqrt(2 / math.pi)
     hid = (x * (0.5 * (1.0 + jnp.tanh(k0 * (x + 0.044715 * (x * x * x)))))).astype(BF)
     hidden[...] = hid
     br_own[...] = lax.dot_general(hid[0:256], down[...], NT, preferred_element_type=F32)
-    br_oth[...] = lax.dot_general(hid[256:512], down[...], NT, preferred_element_type=F32)
+    br_oth[...] = lax.dot_general(hid[256:512], down[...], NT, preferred_element_type=F32).astype(BF)
     own_in[...] = jnp.where(mine, own[xl, g].astype(F32), nb[xl, g].astype(F32)).astype(BF)
 
 
@@ -136,26 +131,36 @@
         wide[k] = row
 
 
-def pack_kernel(own, got, out, tmp0, tmp1, tmp2, mid):
+def pair_kernel(s_ref, own, other, out):
+    xh = lax.rem(s_ref[5], 2)
+    out[xh] = own[...]
+    out[1 - xh] = other[...]
+
+
+def branch_kernel(own, got, out):
+    out[...] = (own[...] + got[...].astype(F32)).astype(BF)
+
+
+def pack_kernel(own, got, out, a0, a1, b0, b1, mid):
     total = own[...] + got[...]
-    for t, tmp in enumerate((tmp0, tmp1, tmp2)):
-        tmp[...] = total[:, 128 * t : 128 * t + 128]
-        for k in range(4):
-            for q in range(8):
-                mid[q, 11 * k : 11 * k + 11, 128 * t : 128 * t + 128] = tmp[pl.ds(ROWS * k + q, 11, stride=8), :]
+    a0[...] = total[:, 0:128]
+    a1[:, 0:64] = total[:, 128:192]
+    b0[...] = total[:, 192:320]
+    b1[:, 0:64] = total[:, 320:384]
+    mid[...] = jnp.zeros_like(mid)
+
+    @pl.loop(0, 8)
+    def _(q):
+        for k in range(8):
+            first, second = (a0, a1) if k < 4 else (b0, b1)
+            at = ROWS * (k % 4) + q
+            to = 8 * q + k
+            mid[to, :, 0:128] = first[pl.ds(at, 8, stride=8), :]
+            mid[to, :, 128:192] = second[pl.ds(at, 8, stride=8), :][:, 0:64]
+            mid[to, 0:3, 192:320] = first[pl.ds(at + 64, 3, stride=8), :]
+            mid[to, 0:3, 320:384] = second[pl.ds(at + 64, 3, stride=8), :][:, 0:64]
+
     out[...] = mid[...].astype(BF)
-
-
-def add_kernel(got, out, tmp):
-    total = got[0].astype(F32)
-    for k in range(1, 8):
-        total += got[k].astype(F32)
-    tmp[...] = total
-    out[...] = jnp.zeros_like(out)
-    for k in range(4):
-        rows = tmp[11 * k : 11 * k + 11, :]
-        out[k, 0:11, :] = rows[:, 0:192]
-        out[k + 4, 0:11, :] = rows[:, 192:384]
 
 
 def prep_kernel(s_ref, so, *refs):
@@ -170,9 +175,17 @@
     pred_ref[...] = lax.dot_general(so[...], w_ref[...], NT, preferred_element_type=F32)
 
 
-def head_kernel(s_ref, sums, pred, w_ref, out):
+def head_kernel(s_ref, w_hbm, sums, pred, out, w_ref, sem):
+    copy = pltpu.make_async_copy(w_hbm, w_ref, sem)
+    copy.start()
     g, c, z = s_ref[5], s_ref[3], s_ref[4]
-    summed = jnp.concatenate([sums[AT[j]] for j in range(8)], axis=-1)
+    parts = []
+    for k in range(8):
+        total = sums[k].astype(F32)
+        for m in range(1, 8):
+            total += sums[8 * m + k].astype(F32)
+        parts.append(jnp.concatenate([total[:, 0:192], total[:, 192:384]]))
+    summed = jnp.concatenate([parts[AT[j]] for j in range(8)], axis=-1)
     row_mean = jnp.mean(summed, axis=-1, keepdims=True)
     mean_square = jnp.mean(summed * summed, axis=-1, keepdims=True)
     target = (summed - row_mean) * lax.rsqrt(mean_square - row_mean * row_mean + 1e-06)
@@ -180,6 +193,7 @@
     r = 8 * j + g
     real = (j < 11) & (r < CHUNK) & (2 * CHUNK * z + CHUNK * c + r < VALID)
     pred_grad = jnp.where(real, (pred[...] - target) * (1.0 / math.sqrt(IMAGES * VALID)), 0.0).astype(BF)
+    copy.wait()
     out_grad = jnp.dot(pred_grad, w_ref[...], preferred_element_type=F32).astype(BF)
     wide = pred_grad.astype(F32)
     for k in range(8):
@@ -190,12 +204,12 @@
             out[2 * k + e, :, 1024:1152] = cut.astype(BF)
 
 
-def back_kernel(s_ref, own, far, so, hidden, pre, normed, down, out):
+def back_kernel(s_ref, own, far, so, so_far, hidden, pre, normed, down, out):
     c = s_ref[3]
     og = jnp.concatenate([own[:, 0:1024], far[:, 0:1024]])
     pg = jnp.concatenate([own[:, 1024:1152], far[:, 1024:1152]]).astype(F32)
     pg = jnp.where(c == 0, pg, jnp.concatenate([pg[:, 48:], pg[:, :48]], axis=-1)).astype(BF)
-    head = lax.dot_general(pg, so[...], TN, preferred_element_type=F32)[0:48]
+    head = lax.dot_general(pg, jnp.concatenate([so[...], so_far[...]]), TN, preferred_element_type=F32)[0:48]
     dn = lax.dot_general(hidden[...], og, TN, preferred_element_type=F32)
     hidden_grad = jnp.dot(og, down[...], preferred_element_type=F32)
     x = pre[...]
@@ -290,18 +304,19 @@
     down = lax.dynamic_slice_in_dim(w_down, xl * 128, 128, 1)
     normed, pre, hidden, br_own, br_oth, own_in = call(
         student_kernel,
-        [((512, 1024), BF), ((512, 128), F32), ((512, 128), BF), ((256, 1024), F32), ((256, 1024), F32), ((16, 1024), BF)],
+        [((512, 1024), BF), ((512, 128), F32), ((512, 128), BF), ((256, 1024), F32), ((256, 1024), BF), ((16, 1024), BF)],
         scalars, st_own, st_nb, student_gain[None], up, down, scalar=1, flops=300_000_000,
     )
-    keep = (br_own + swap(br_oth, "c")).astype(BF).reshape(16, 16, -1)
+    (keep,) = call(branch_kernel, [((256, 1024), BF)], br_own, swap(br_oth, "c"))
+    keep = keep.reshape(16, 16, -1)
     keep = lax.all_to_all(keep, ("y", "xh", "xl"), 0, 0, tiled=True)
     student_out, wide = call(join_kernel, [((16, 1024), BF), ((16, 16, 1024), BF)], keep, own_in)
     so_own = lax.all_to_all(wide, ("y", "xh", "xl"), 0, 0, tiled=True).reshape(256, -1)
-    so_all = jnp.concatenate([so_own, swap(so_own, "c")])
+    so_far = swap(so_own, "c")
 
     wh = w_head.T
     wh2 = swap(wh, "xh")
-    pair = jnp.where(xh == 0, jnp.stack([wh, wh2]), jnp.stack([wh2, wh]))
+    (pair,) = call(pair_kernel, [((2, 96, 1024), BF)], scalars, wh, wh2, scalar=1)
     w_own = [pair] + [turn(pair, "y", 4, k) for k in (1, 2, 3)]
     w_far = [swap(v, "c") for v in w_own]
 
@@ -320,23 +335,24 @@
     )
     got = swap(oth, "c")
     (both,) = call(
-        pack_kernel, [((8, 44, 384), BF)], own, got,
-        scratch=[pltpu.VMEM((half // 2, 128), F32)] * 3 + [pltpu.VMEM((8, 44, 384), F32)],
+        pack_kernel, [((64, 8, 384), BF)], own, got,
+        scratch=[pltpu.VMEM((half // 2, 128), F32)] * 4 + [pltpu.VMEM((64, 8, 384), F32)],
     )
     both = after(both, so_own)
-    got = lax.all_to_all(both, G, 0, 0, tiled=True)
-    (sums,) = call(add_kernel, [((8, 16, 192), F32)], got, scratch=[pltpu.VMEM((44, 384), F32)])
-    sums = lax.all_to_all(sums, "z", 0, 0, tiled=True)
+    sums = lax.all_to_all(both, ("y", "xh", "z"), 0, 0, tiled=True)
 
     w_all, pred = call(
         prep_kernel, [((1536, 1024), BF), ((16, 1536), F32)], scalars, student_out, *w_own, *w_far, scalar=1
     )
-    (load,) = call(head_kernel, [((16, 16, 1152), BF)], scalars, sums, pred, w_all, scalar=1)
+    (load,) = call(
+        head_kernel, [((16, 16, 1152), BF)], scalars, w_all, sums, pred,
+        scratch=[pltpu.VMEM((1536, 1024), BF), pltpu.SemaphoreType.DMA], scalar=1, away=1, vmem=58,
+    )
     load = lax.all_to_all(load, ("y", "xh", "xl"), 0, 0, tiled=True).reshape(256, 1152)
     far = swap(load, "c")
 
     (grads,) = call(
-        back_kernel, [((16, 152, 128), BF)], scalars, load, far, so_all, hidden, pre, normed, down, scalar=1
+        back_kernel, [((16, 152, 128), BF)], scalars, load, far, so_own, so_far, hidden, pre, normed, down, scalar=1
     )
     grads = lax.all_to_all(grads, DP, 0, 0, tiled=True)
     return tuple(call(finish_kernel, [((64, 256), F32), ((64, 256), F32), ((64, 96), F32)], grads))

time: 230 us -> 221 us (0.961)
  blocking collectives: 25 us -> 43.3 us
  waiting for transfers between devices: 52.2 us -> 38.2 us
  other arithmetic: 7.72 us -> 3.15 us
  Pallas kernels: 36.5 us -> 32.1 us
  local copies, waits for them, and re-layouts: 23 us -> 20.1 us
    all_to_all x3 -> x1, starting transfers between devices: 27 us -> 7.37 us  [inner(): sums = lax.all_to_all(both, ('y', 'xh', 'z'), 0, 0, tiled=True)]
    all_to_all x0 -> x1, blocking collectives: none -> 17.3 us  [inner(): lax.all_to_all(load, ('y', 'xh', 'xl'), 0, 0, tiled=True).reshape(256, 1152)]
    ppermute x17, starting transfers between devices: 11.1 us -> 26.6 us  [swap(): return lax.ppermute(x, axis, SWAP)]
    all_to_all x3 -> x1, waiting for transfers between devices: 13.9 us -> 0.01 us  [inner(): sums = lax.all_to_all(both, ('y', 'xh', 'z'), 0, 0, tiled=True)]
    ppermute x17, waiting for transfers between devices: 2.12 us -> 15.3 us  [swap(): return lax.ppermute(x, axis, SWAP)]
    ppermute x1, waiting for transfers between devices: 7.67 us -> 0.01 us  [inner(): h_own = lax.ppermute(part, DP, to_part)]
    ppermute x1, waiting for transfers between devices: 8.75 us -> 1.85 us  [inner(): got = lax.ppermute(other, ('c', 'xl'), [(0, 1), (3, 2)])]
    pallas_call x9 -> x10, Pallas kernels: 36.5 us -> 32.1 us  [call(): pl.pallas_call(kernel, out_shape=shapes, in_specs=[SM] * scalar + [pl.Blo...]
  transfers between devices with their start and end apart: 33 -> 31, of which waited for: 12 -> 9; matrix products, arithmetic and copies ran while one was open for 6% -> 4% of each run, Pallas kernels for 14% -> 4%
where the time goes in v3:
time: 221 us; the launch traced here: 219 us
  starting transfers between devices  80.1 us (36%)
  blocking collectives  43.3 us (20%)
  waiting for transfers between devices  38.2 us (17%)
  Pallas kernels  32.1 us (15%)
  local copies, waits for them, and re-layouts  20.1 us (9%)
  other arithmetic  3.15 us (1%)
    pallas_call x10, Pallas kernels, call(): pl.pallas_call(kernel, out_shape=shapes, in_specs=[SM] * scalar + [pl.Blo...  32.1 us
    ppermute x17, starting transfers between devices, swap(): return lax.ppermute(x, axis, SWAP)  26.6 us
    all_to_all x1, blocking collectives, inner(): grads = lax.all_to_all(grads, DP, 0, 0, tiled=True)  26 us
    all_to_all x1, blocking collectives, inner(): lax.all_to_all(load, ('y', 'xh', 'xl'), 0, 0, tiled=True).reshape(256, 1152)  17.3 us
    ppermute x17, waiting for transfers between devices, swap(): return lax.ppermute(x, axis, SWAP)  15.3 us
    unnamed x52, local copies, waits for them, and re-layouts  13.3 us
    ppermute x7, waiting for transfers between devices, turn(): return lax.ppermute(x, axis, [(k, (k - by) % n) for k in range(n)])  12.5 us
    ppermute x7, starting transfers between devices, turn(): return lax.ppermute(x, axis, [(k, (k - by) % n) for k in range(n)])  10.8 us
  transfers between devices with their start and end apart: 31, of which 9 were waited for; matrix products, arithmetic and copies ran while one was open for 4% of the time, Pallas kernels for 4%

profile of v3, /device:TPU:8, one launch (start us, length us, event | category | flops | bytes accessed | tf_op | source)
XLA Modules:
  0.0 218.8 jit_solution(3089126074815348714)
XLA Ops:
  2.3 3.4 %collective-permute-start.10 = (bf16[88,384]{1,0:T(8,128)(2,1)S(1)}, bf16[88,384]{1,0:T(8,128)(2,1)S(1)}, u32[]{:S(2)}, u32[]{:S(2)}) collective-permute-start(bf16[88,384]{1,0:T(8,128)(2,1)S(1)} %pad_select_fusion), channel_id=1, source_target_pairs={{0,1},{17,16},{2,3},{19,18},{4,5},{21,20},{6,7},{23,22},{8,9},{25,... | collective-permute-start | bytes 202760 | tf_op jit(solution)/shard_map/ppermute | solution.py:276
  5.8 1.9 collective-permute-done.10
  8.6 8.5 %all-to-all-start.1 = ((bf16[8,88,384]{2,1,0:T(8,128)(2,1)}), bf16[8,88,384]{2,1,0:T(8,128)(2,1)S(1)}, u32[]{:S(2)}, u32[]{:S(2)}) async-start(bf16[8,88,384]{2,1,0:T(8,128)(2,1)} %broadcast_in_dim.49), calls=%async_computation.1 | async-start | bytes 1081344 | tf_op jit(solution)/shard_map/all_to_all | solution.py:253
  17.9 6.0 %collective-permute-start.20 = (bf16[192,1536]{1,0:T(8,128)(2,1)}, bf16[192,1536]{1,0:T(8,128)(2,1)}, u32[]{:S(2)}, u32[]{:S(2)}) collective-permute-start(bf16[192,1536]{1,0:T(8,128)(2,1)} %slice_select_fusion), channel_id=1, source_target_pairs={{0,0},{1,3},{2,6},{3,9},{4,14},{5,1},{6,4},{7,7},{8,12},{9,15},{10... | collective-permute-start | bytes 1769480 | tf_op jit(solution)/shard_map/ppermute | solution.py:292
  24.9 1.8 slice_select_fusion.1
  26.7 3.1 %collective-permute-start.22 = (bf16[96,1536]{1,0:T(8,128)(2,1)}, bf16[96,1536]{1,0:T(8,128)(2,1)S(1)}, u32[]{:S(2)}, u32[]{:S(2)}) collective-permute-start(bf16[96,1536]{1,0:T(8,128)(2,1)} %slice_select_fusion.1), channel_id=1, source_target_pairs={{0,4},{1,5},{2,12},{3,13},{4,10},{5,11},{6,2},{7,3},{8,8},{9,9},{1... | collective-permute-start | bytes 884744 | tf_op jit(solution)/shard_map/ppermute | solution.py:293
  29.8 20.9 %collective-permute-start.21 = (bf16[192,1536]{1,0:T(8,128)(2,1)}, bf16[192,1536]{1,0:T(8,128)(2,1)}, u32[]{:S(2)}, u32[]{:S(2)}) collective-permute-start(bf16[192,1536]{1,0:T(8,128)(2,1)} %collective-permute-done.20.m_own), channel_id=1, source_target_pairs={{0,1},{1,0},{2,3},{3,2},{4,5},{5,4},{6,7},{7,6},{8,9},{9,8},{10,11... | collective-permute-start | bytes 1769480 | tf_op jit(solution)/shard_map/ppermute | solution.py:244
  57.1 3.5 %shard_map.103 = (bf16[512,1024]{1,0:T(8,128)(2,1)S(1)}, f32[512,128]{1,0:T(8,128)S(1)}, bf16[512,128]{1,0:T(8,128)(2,1)S(1)}, f32[256,1024]{1,0:T(8,128)S(1)}, ...) custom-call(s32[6]{0:T(128)S(1)} %stack.27.s_ref, bf16[2,8,16,1024]{3,2,1,0:T(8,128)(2,1)S(1)} %bitcast.31, ...), custom_call_target="tpu_custom_call" | custom-call | flops 300000000 | bytes 4624408 | tf_op jit(solution)/shard_map/pallas_call | solution.py:87
  62.1 2.2 %collective-permute-done.11.xa1 = bf16[704,384]{1,0:T(8,128)(2,1)} collective-permute-done((bf16[704,384]{1,0:T(8,128)(2,1)S(1)}, bf16[704,384]{1,0:T(8,128)(2,1)}, u32[]{:S(2)}, u32[]{:S(2)}) %collective-permute-start.11) | collective-permute-done | bytes 540704 | tf_op jit(solution)/shard_map/ppermute | solution.py:248
  65.8 1.7 slice.40
  67.5 3.0 %collective-permute-start.13 = (bf16[352,384]{1,0:T(8,128)(2,1)}, bf16[352,384]{1,0:T(8,128)(2,1)}, u32[]{:S(2)}, u32[]{:S(2)}) collective-permute-start(bf16[352,384]{1,0:T(8,128)(2,1)} %slice.40), channel_id=1, source_target_pairs={{0,192},{64,0},{128,64},{192,128},{1,193},{65,1},{129,65},{193,129... | collective-permute-start | bytes 811016 | tf_op jit(solution)/shard_map/ppermute | solution.py:248
  70.5 1.7 slice.41
  75.1 8.3 %all-to-all-start = ((bf16[16,16,1024]{2,1,0:T(8,128)(2,1)}), bf16[16,16,1024]{2,1,0:T(8,128)(2,1)S(1)}, u32[]{:S(2)}, u32[]{:S(2)}) async-start(bf16[16,16,1024]{2,1,0:T(8,128)(2,1)} %bitcast.10), calls=%async_computation | async-start | bytes 1048576 | tf_op jit(solution)/shard_map/all_to_all | solution.py:312
  84.1 8.6 %all-to-all-done.keep = bf16[16,16,1024]{2,1,0:T(8,128)(2,1)S(1)} async-done(((bf16[16,16,1024]{2,1,0:T(8,128)(2,1)}), bf16[16,16,1024]{2,1,0:T(8,128)(2,1)S(1)}, u32[]{:S(2)}, u32[]{:S(2)}) %all-to-all-start) | async-done | bytes 524320 | tf_op jit(solution)/shard_map/all_to_all | solution.py:312
  95.6 15.9 %shard_map.108 = (f32[352,384]{1,0:T(8,128)S(1)}, f32[352,384]{1,0:T(8,128)}) custom-call(s32[6]{0:T(128)S(1)} %stack.27.s_ref, bf16[704,384]{1,0:T(8,128)(2,1)S(1)} %bitcast.35, bf16[704,384]{1,0:T(8,128)(2,1)} %collective-permute-done.11.xa1, bf16[352,384]{1,0:T(8,128)(2,1)} %collective-permute-done.13.xa2, bf16[352,384]{1,0:T(8,128)(2,1)} %collective-permute-done.14.xa2l, ...), custom_call_target="tpu_custom_call" | custom-call | flops 6000000000 | bytes 7176216 | tf_op jit(solution)/shard_map/pallas_call | solution.py:87
  112.4 6.1 %all-to-all-start.2 = ((bf16[16,16,1024]{2,1,0:T(8,128)(2,1)}), bf16[16,16,1024]{2,1,0:T(8,128)(2,1)S(1)}, u32[]{:S(2)}, u32[]{:S(2)}) async-start(bf16[16,16,1024]{2,1,0:T(8,128)(2,1)} %copy-done.6), calls=%async_computation.2 | async-start | bytes 1048576 | tf_op jit(solution)/shard_map/all_to_all | solution.py:314
  118.4 3.1 %collective-permute-start.2 = (bf16[96,1024]{1,0:T(8,128)(2,1)S(1)}, bf16[96,1024]{1,0:T(8,128)(2,1)S(1)}, u32[]{:S(2)}, u32[]{:S(2)}) collective-permute-start(bf16[96,1024]{1,0:T(8,128)(2,1)S(1)} %bitcast.36), channel_id=1, source_target_pairs={{0,32},{32,0},{1,33},{33,1},{2,34},{34,2},{3,35},{35,3},{4,36},{36... | collective-permute-start | bytes 589832 | tf_op jit(solution)/shard_map/ppermute | solution.py:244
  121.5 11.1 %collective-permute-done.2.other = bf16[96,1024]{1,0:T(8,128)(2,1)S(1)} collective-permute-done((bf16[96,1024]{1,0:T(8,128)(2,1)S(1)}, bf16[96,1024]{1,0:T(8,128)(2,1)S(1)}, u32[]{:S(2)}, u32[]{:S(2)}) %collective-permute-start.2) | collective-permute-done | bytes 196640 | tf_op jit(solution)/shard_map/ppermute | solution.py:244
  134.4 2.4 %collective-permute-start.4 = (bf16[2,96,1024]{2,1,0:T(8,128)(2,1)S(1)}, bf16[2,96,1024]{2,1,0:T(8,128)(2,1)}, u32[]{:S(2)}, u32[]{:S(2)}) collective-permute-start(bf16[2,96,1024]{2,1,0:T(8,128)(2,1)S(1)} %shard_map.106.refs_0_), channel_id=1, source_target_pairs={{0,128},{64,192},{128,0},{192,64},{1,129},{65,193},{129,1},{193,65... | collective-permute-start | bytes 1179656 | tf_op jit(solution)/shard_map/ppermute | solution.py:248
  136.8 1.8 collective-permute-start.5
  139.7 1.7 shard_map.109
  141.4 7.4 %all-to-all-start.3 = ((bf16[64,8,384]{2,1,0:T(8,128)(2,1)}), bf16[64,8,384]{2,1,0:T(8,128)(2,1)S(1)}, u32[]{:S(2)}, u32[]{:S(2)}) async-start(bf16[64,8,384]{2,1,0:T(8,128)(2,1)} %shard_map.109), calls=%async_computation.3 | async-start | bytes 786432 | tf_op jit(solution)/shard_map/all_to_all | solution.py:342
  149.4 6.0 %collective-permute-done.4.refs_2_ = bf16[2,96,1024]{2,1,0:T(8,128)(2,1)} collective-permute-done((bf16[2,96,1024]{2,1,0:T(8,128)(2,1)S(1)}, bf16[2,96,1024]{2,1,0:T(8,128)(2,1)}, u32[]{:S(2)}, u32[]{:S(2)}) %collective-permute-start.4) | collective-permute-done | bytes 393248 | tf_op jit(solution)/shard_map/ppermute | solution.py:248
  155.4 2.8 %collective-permute-done.5.refs_3_ = bf16[2,96,1024]{2,1,0:T(8,128)(2,1)} collective-permute-done((bf16[2,96,1024]{2,1,0:T(8,128)(2,1)S(1)}, bf16[2,96,1024]{2,1,0:T(8,128)(2,1)}, u32[]{:S(2)}, u32[]{:S(2)}) %collective-permute-start.5) | collective-permute-done | bytes 393248 | tf_op jit(solution)/shard_map/ppermute | solution.py:248
  158.3 1.9 collective-permute-done.9.refs_7_
  160.2 2.4 %shard_map.107 = (bf16[1536,1024]{1,0:T(8,128)(2,1)S(1)}, f32[16,1536]{1,0:T(8,128)S(1)}) custom-call(s32[6]{0:T(128)S(1)} %copy-done.14, bf16[16,1024]{1,0:T(8,128)(2,1)S(1)} %get-tuple-element.22.so, bf16[2,96,1024]{2,1,0:T(8,128)(2,1)S(1)} %shard_map.106.refs_0_, bf16[2,96,1024]{2,1,0:T(8,128)(2,1)} %collective-permute-done.3.refs_1_, ...), custom_call_target="tpu_custom_call" | custom-call | bytes 6422552 | tf_op jit(solution)/shard_map/pallas_call | solution.py:87
  162.6 1.6 copy-done.1
  165.6 4.3 %shard_map.110 = bf16[16,16,1152]{2,1,0:T(8,128)(2,1)} custom-call(s32[6]{0:T(128)} %copy-done.13, bf16[1536,1024]{1,0:T(8,128)(2,1)} %copy-done.1, bf16[64,8,384]{2,1,0:T(8,128)(2,1)} %copy-done.22, f32[16,1536]{1,0:T(8,128)} %copy-done.12), custom_call_target="tpu_custom_call" | custom-call | bytes 4227096 | tf_op jit(solution)/shard_map/pallas_call | solution.py:87
  169.9 17.3 %all_to_all.30 = bf16[16,16,1152]{2,1,0:T(8,128)(2,1)S(1)} all-to-all(bf16[16,16,1152]{2,1,0:T(8,128)(2,1)} %shard_map.110), channel_id=1, replica_groups=mesh['y'=4,'xh'=2,'c'=2,'z'=8,'xl'=2] {'y','xh','xl'}, dimensions={0} | all-to-all | bytes 1179648 | tf_op jit(solution)/shard_map/all_to_all | solution.py:351
  187.7 2.2 %collective-permute-done.26.so_far = bf16[256,1024]{1,0:T(8,128)(2,1)S(1)} collective-permute-done((bf16[256,1024]{1,0:T(8,128)(2,1)S(1)}, bf16[256,1024]{1,0:T(8,128)(2,1)S(1)}, u32[]{:S(2)}, u32[]{:S(2)}) %collective-permute-start.26) | collective-permute-done | bytes 524320 | tf_op jit(solution)/shard_map/ppermute | solution.py:244
  190.0 2.0 shard_map.111
  191.9 26.0 %all_to_all.31.got = bf16[16,152,128]{2,1,0:T(8,128)(2,1)S(1)} all-to-all(bf16[16,152,128]{2,1,0:T(8,128)(2,1)S(1)} %shard_map.111), channel_id=1, replica_groups=mesh['y'=4,'xh'=2,'c'=2,'z'=8,'xl'=2] {'z','xl'}, dimensions={0} | all-to-all | bytes 1245184 | tf_op jit(solution)/shard_map/all_to_all | solution.py:357
  (113 shorter events, 26.6 us)
Async XLA Ops:
  2.3 5.3 %collective-permute-start.10 = (bf16[88,384]{1,0:T(8,128)(2,1)S(1)}, bf16[88,384]{1,0:T(8,128)(2,1)S(1)}, u32[]{:S(2)}, u32[]{:S(2)}) collective-permute-start(bf16[88,384]{1,0:T(8,128)(2,1)S(1)} %pad_select_fusion), channel_id=1, source_target_pairs={{0,1},{17,16},{2,3},{19,18},{4,5},{21,20},{6,7},{23,22},{8,9},{25,... | collective-permute-start | bytes 202760 | tf_op jit(solution)/shard_map/ppermute | solution.py:276
  8.6 44.6 %all-to-all-start.1 = ((bf16[8,88,384]{2,1,0:T(8,128)(2,1)}), bf16[8,88,384]{2,1,0:T(8,128)(2,1)S(1)}, u32[]{:S(2)}, u32[]{:S(2)}) async-start(bf16[8,88,384]{2,1,0:T(8,128)(2,1)} %broadcast_in_dim.49), calls=%async_computation.1 | async-start | bytes 1081344 | tf_op jit(solution)/shard_map/all_to_all | solution.py:253
  17.9 11.9 %collective-permute-start.20 = (bf16[192,1536]{1,0:T(8,128)(2,1)}, bf16[192,1536]{1,0:T(8,128)(2,1)}, u32[]{:S(2)}, u32[]{:S(2)}) collective-permute-start(bf16[192,1536]{1,0:T(8,128)(2,1)} %slice_select_fusion), channel_id=1, source_target_pairs={{0,0},{1,3},{2,6},{3,9},{4,14},{5,1},{6,4},{7,7},{8,12},{9,15},{10... | collective-permute-start | bytes 1769480 | tf_op jit(solution)/shard_map/ppermute | solution.py:292
  24.5 30.8 %collective-permute-start = (bf16[2,8,16,1024]{3,2,1,0:T(8,128)(2,1)S(1)}, bf16[2,8,16,1024]{3,2,1,0:T(8,128)(2,1)S(1)}, u32[]{:S(2)}, u32[]{:S(2)}) collective-permute-start(bf16[2,8,16,1024]{3,2,1,0:T(8,128)(2,1)S(1)} %bitcast.30), channel_id=1, source_target_pairs={{0,1},{1,0},{2,3},{3,2},{4,5},{5,4},{6,7},{7,6},{8,9},{9,8},{10,11... | collective-permute-start | bytes 1572872 | tf_op jit(solution)/shard_map/ppermute | solution.py:244
  26.7 35.4 %collective-permute-start.22 = (bf16[96,1536]{1,0:T(8,128)(2,1)}, bf16[96,1536]{1,0:T(8,128)(2,1)S(1)}, u32[]{:S(2)}, u32[]{:S(2)}) collective-permute-start(bf16[96,1536]{1,0:T(8,128)(2,1)} %slice_select_fusion.1), channel_id=1, source_target_pairs={{0,4},{1,5},{2,12},{3,13},{4,10},{5,11},{6,2},{7,3},{8,8},{9,9},{1... | collective-permute-start | bytes 884744 | tf_op jit(solution)/shard_map/ppermute | solution.py:293
  29.8 43.9 %collective-permute-start.21 = (bf16[192,1536]{1,0:T(8,128)(2,1)}, bf16[192,1536]{1,0:T(8,128)(2,1)}, u32[]{:S(2)}, u32[]{:S(2)}) collective-permute-start(bf16[192,1536]{1,0:T(8,128)(2,1)} %collective-permute-done.20.m_own), channel_id=1, source_target_pairs={{0,1},{1,0},{2,3},{3,2},{4,5},{5,4},{6,7},{7,6},{8,9},{9,8},{10,11... | collective-permute-start | bytes 1769480 | tf_op jit(solution)/shard_map/ppermute | solution.py:244
  53.2 40.5 %copy-start.13 = (s32[6]{0:T(128)}, s32[6]{0:T(128)S(1)}, u32[]{:S(2)}) copy-start(s32[6]{0:T(128)S(1)} %stack.27.s_ref) | copy-start | bytes 76
  53.2 11.2 %collective-permute-start.11 = (bf16[704,384]{1,0:T(8,128)(2,1)S(1)}, bf16[704,384]{1,0:T(8,128)(2,1)}, u32[]{:S(2)}, u32[]{:S(2)}) collective-permute-start(bf16[704,384]{1,0:T(8,128)(2,1)S(1)} %bitcast.32), channel_id=1, source_target_pairs={{0,192},{64,0},{128,64},{192,128},{1,193},{65,1},{129,65},{193,129... | collective-permute-start | bytes 1622024 | tf_op jit(solution)/shard_map/ppermute | solution.py:248
  53.7 12.1 %collective-permute-start.12 = (bf16[704,384]{1,0:T(8,128)(2,1)S(1)}, bf16[704,384]{1,0:T(8,128)(2,1)}, u32[]{:S(2)}, u32[]{:S(2)}) collective-permute-start(bf16[704,384]{1,0:T(8,128)(2,1)S(1)} %bitcast.33), channel_id=1, source_target_pairs={{0,64},{64,128},{128,192},{192,0},{1,65},{65,129},{129,193},{193,1... | collective-permute-start | bytes 1622024 | tf_op jit(solution)/shard_map/ppermute | solution.py:248
  62.0 11.7 %collective-permute-start.1 = (bf16[256,1024]{1,0:T(8,128)(2,1)S(1)}, bf16[256,1024]{1,0:T(8,128)(2,1)S(1)}, u32[]{:S(2)}, u32[]{:S(2)}) collective-permute-start(bf16[256,1024]{1,0:T(8,128)(2,1)S(1)} %get-tuple-element.20), channel_id=1, source_target_pairs={{0,16},{16,0},{1,17},{17,1},{2,18},{18,2},{3,19},{19,3},{4,20},{20... | collective-permute-start | bytes 1572872 | tf_op jit(solution)/shard_map/ppermute | solution.py:244
  62.0 10.1 %collective-permute-start.23 = (bf16[96,1536]{1,0:T(8,128)(2,1)S(1)}, bf16[96,1536]{1,0:T(8,128)(2,1)S(1)}, u32[]{:S(2)}, u32[]{:S(2)}) collective-permute-start(bf16[96,1536]{1,0:T(8,128)(2,1)S(1)} %collective-permute-done.22.h_own), channel_id=1, source_target_pairs={{0,1},{1,0},{2,3},{3,2},{4,5},{5,4},{6,7},{7,6},{8,9},{9,8},{10,11... | collective-permute-start | bytes 884744 | tf_op jit(solution)/shard_map/ppermute | solution.py:244
  64.4 29.3 %collective-permute-start.15 = (bf16[704,384]{1,0:T(8,128)(2,1)S(1)}, bf16[704,384]{1,0:T(8,128)(2,1)}, u32[]{:S(2)}, u32[]{:S(2)}) collective-permute-start(bf16[704,384]{1,0:T(8,128)(2,1)S(1)} %bitcast.34), channel_id=1, source_target_pairs={{0,16},{16,0},{1,17},{17,1},{2,18},{18,2},{3,19},{19,3},{4,20},{20... | collective-permute-start | bytes 1622024 | tf_op jit(solution)/shard_map/ppermute | solution.py:244
  67.5 16.0 %collective-permute-start.13 = (bf16[352,384]{1,0:T(8,128)(2,1)}, bf16[352,384]{1,0:T(8,128)(2,1)}, u32[]{:S(2)}, u32[]{:S(2)}) collective-permute-start(bf16[352,384]{1,0:T(8,128)(2,1)} %slice.40), channel_id=1, source_target_pairs={{0,192},{64,0},{128,64},{192,128},{1,193},{65,1},{129,65},{193,129... | collective-permute-start | bytes 811016 | tf_op jit(solution)/shard_map/ppermute | solution.py:248
  72.9 10.7 %collective-permute-start.14 = (bf16[352,384]{1,0:T(8,128)(2,1)}, bf16[352,384]{1,0:T(8,128)(2,1)}, u32[]{:S(2)}, u32[]{:S(2)}) collective-permute-start(bf16[352,384]{1,0:T(8,128)(2,1)} %slice.41), channel_id=1, source_target_pairs={{0,64},{64,128},{128,192},{192,0},{1,65},{65,129},{129,193},{193,1... | collective-permute-start | bytes 811016 | tf_op jit(solution)/shard_map/ppermute | solution.py:248
  73.7 19.9 %collective-permute-start.16 = (bf16[704,384]{1,0:T(8,128)(2,1)}, bf16[704,384]{1,0:T(8,128)(2,1)}, u32[]{:S(2)}, u32[]{:S(2)}) collective-permute-start(bf16[704,384]{1,0:T(8,128)(2,1)} %collective-permute-done.11.xa1), channel_id=1, source_target_pairs={{0,16},{16,0},{1,17},{17,1},{2,18},{18,2},{3,19},{19,3},{4,20},{20... | collective-permute-start | bytes 1622024 | tf_op jit(solution)/shard_map/ppermute | solution.py:244
  73.8 19.9 %collective-permute-start.19 = (bf16[704,384]{1,0:T(8,128)(2,1)}, bf16[704,384]{1,0:T(8,128)(2,1)}, u32[]{:S(2)}, u32[]{:S(2)}) collective-permute-start(bf16[704,384]{1,0:T(8,128)(2,1)} %collective-permute-done.12.xa3), channel_id=1, source_target_pairs={{0,16},{16,0},{1,17},{17,1},{2,18},{18,2},{3,19},{19,3},{4,20},{20... | collective-permute-start | bytes 1622024 | tf_op jit(solution)/shard_map/ppermute | solution.py:244
  75.1 17.5 %all-to-all-start = ((bf16[16,16,1024]{2,1,0:T(8,128)(2,1)}), bf16[16,16,1024]{2,1,0:T(8,128)(2,1)S(1)}, u32[]{:S(2)}, u32[]{:S(2)}) async-start(bf16[16,16,1024]{2,1,0:T(8,128)(2,1)} %bitcast.10), calls=%async_computation | async-start | bytes 1048576 | tf_op jit(solution)/shard_map/all_to_all | solution.py:312
  83.5 10.2 %collective-permute-start.17 = (bf16[352,384]{1,0:T(8,128)(2,1)}, bf16[352,384]{1,0:T(8,128)(2,1)}, u32[]{:S(2)}, u32[]{:S(2)}) collective-permute-start(bf16[352,384]{1,0:T(8,128)(2,1)} %collective-permute-done.13.xa2), channel_id=1, source_target_pairs={{0,16},{16,0},{1,17},{17,1},{2,18},{18,2},{3,19},{19,3},{4,20},{20... | collective-permute-start | bytes 811016 | tf_op jit(solution)/shard_map/ppermute | solution.py:244
  83.6 10.1 %collective-permute-start.18 = (bf16[352,384]{1,0:T(8,128)(2,1)}, bf16[352,384]{1,0:T(8,128)(2,1)}, u32[]{:S(2)}, u32[]{:S(2)}) collective-permute-start(bf16[352,384]{1,0:T(8,128)(2,1)} %collective-permute-done.14.xa2l), channel_id=1, source_target_pairs={{0,16},{16,0},{1,17},{17,1},{2,18},{18,2},{3,19},{19,3},{4,20},{20... | collective-permute-start | bytes 811016 | tf_op jit(solution)/shard_map/ppermute | solution.py:244
  112.4 26.3 %collective-permute-start.24 = (f32[352,384]{1,0:T(8,128)}, f32[352,384]{1,0:T(8,128)S(1)}, u32[]{:S(2)}, u32[]{:S(2)}) collective-permute-start(f32[352,384]{1,0:T(8,128)} %get-tuple-element.28), channel_id=1, source_target_pairs={{0,16},{16,0},{1,17},{17,1},{2,18},{18,2},{3,19},{19,3},{4,20},{20... | collective-permute-start | bytes 1622024 | tf_op jit(solution)/shard_map/ppermute | solution.py:244
  112.4 29.1 %all-to-all-start.2 = ((bf16[16,16,1024]{2,1,0:T(8,128)(2,1)}), bf16[16,16,1024]{2,1,0:T(8,128)(2,1)S(1)}, u32[]{:S(2)}, u32[]{:S(2)}) async-start(bf16[16,16,1024]{2,1,0:T(8,128)(2,1)} %copy-done.6), calls=%async_computation.2 | async-start | bytes 1048576 | tf_op jit(solution)/shard_map/all_to_all | solution.py:314
  118.4 14.1 %collective-permute-start.2 = (bf16[96,1024]{1,0:T(8,128)(2,1)S(1)}, bf16[96,1024]{1,0:T(8,128)(2,1)S(1)}, u32[]{:S(2)}, u32[]{:S(2)}) collective-permute-start(bf16[96,1024]{1,0:T(8,128)(2,1)S(1)} %bitcast.36), channel_id=1, source_target_pairs={{0,32},{32,0},{1,33},{33,1},{2,34},{34,2},{3,35},{35,3},{4,36},{36... | collective-permute-start | bytes 589832 | tf_op jit(solution)/shard_map/ppermute | solution.py:244
  133.8 15.1 %collective-permute-start.3 = (bf16[2,96,1024]{2,1,0:T(8,128)(2,1)S(1)}, bf16[2,96,1024]{2,1,0:T(8,128)(2,1)}, u32[]{:S(2)}, u32[]{:S(2)}) collective-permute-start(bf16[2,96,1024]{2,1,0:T(8,128)(2,1)S(1)} %shard_map.106.refs_0_), channel_id=1, source_target_pairs={{0,192},{64,0},{128,64},{192,128},{1,193},{65,1},{129,65},{193,129... | collective-permute-start | bytes 1179656 | tf_op jit(solution)/shard_map/ppermute | solution.py:248
  134.4 21.0 %collective-permute-start.4 = (bf16[2,96,1024]{2,1,0:T(8,128)(2,1)S(1)}, bf16[2,96,1024]{2,1,0:T(8,128)(2,1)}, u32[]{:S(2)}, u32[]{:S(2)}) collective-permute-start(bf16[2,96,1024]{2,1,0:T(8,128)(2,1)S(1)} %shard_map.106.refs_0_), channel_id=1, source_target_pairs={{0,128},{64,192},{128,0},{192,64},{1,129},{65,193},{129,1},{193,65... | collective-permute-start | bytes 1179656 | tf_op jit(solution)/shard_map/ppermute | solution.py:248
  136.8 21.4 %collective-permute-start.5 = (bf16[2,96,1024]{2,1,0:T(8,128)(2,1)S(1)}, bf16[2,96,1024]{2,1,0:T(8,128)(2,1)}, u32[]{:S(2)}, u32[]{:S(2)}) collective-permute-start(bf16[2,96,1024]{2,1,0:T(8,128)(2,1)S(1)} %shard_map.106.refs_0_), channel_id=1, source_target_pairs={{0,64},{64,128},{128,192},{192,0},{1,65},{65,129},{129,193},{193,1... | collective-permute-start | bytes 1179656 | tf_op jit(solution)/shard_map/ppermute | solution.py:248
  141.4 23.4 %all-to-all-start.3 = ((bf16[64,8,384]{2,1,0:T(8,128)(2,1)}), bf16[64,8,384]{2,1,0:T(8,128)(2,1)S(1)}, u32[]{:S(2)}, u32[]{:S(2)}) async-start(bf16[64,8,384]{2,1,0:T(8,128)(2,1)} %shard_map.109), calls=%async_computation.3 | async-start | bytes 786432 | tf_op jit(solution)/shard_map/all_to_all | solution.py:342
  148.8 9.5 %collective-permute-start.6 = (bf16[2,96,1024]{2,1,0:T(8,128)(2,1)S(1)}, bf16[2,96,1024]{2,1,0:T(8,128)(2,1)S(1)}, u32[]{:S(2)}, u32[]{:S(2)}) collective-permute-start(bf16[2,96,1024]{2,1,0:T(8,128)(2,1)S(1)} %shard_map.106.refs_0_), channel_id=1, source_target_pairs={{0,16},{16,0},{1,17},{17,1},{2,18},{18,2},{3,19},{19,3},{4,20},{20... | collective-permute-start | bytes 1179656 | tf_op jit(solution)/shard_map/ppermute | solution.py:244
  148.9 9.3 %collective-permute-start.7 = (bf16[2,96,1024]{2,1,0:T(8,128)(2,1)}, bf16[2,96,1024]{2,1,0:T(8,128)(2,1)S(1)}, u32[]{:S(2)}, u32[]{:S(2)}) collective-permute-start(bf16[2,96,1024]{2,1,0:T(8,128)(2,1)} %collective-permute-done.3.refs_1_), channel_id=1, source_target_pairs={{0,16},{16,0},{1,17},{17,1},{2,18},{18,2},{3,19},{19,3},{4,20},{20... | collective-permute-start | bytes 1179656 | tf_op jit(solution)/shard_map/ppermute | solution.py:244
  155.4 2.9 %collective-permute-start.8 = (bf16[2,96,1024]{2,1,0:T(8,128)(2,1)}, bf16[2,96,1024]{2,1,0:T(8,128)(2,1)S(1)}, u32[]{:S(2)}, u32[]{:S(2)}) collective-permute-start(bf16[2,96,1024]{2,1,0:T(8,128)(2,1)} %collective-permute-done.4.refs_2_), channel_id=1, source_target_pairs={{0,16},{16,0},{1,17},{17,1},{2,18},{18,2},{3,19},{19,3},{4,20},{20... | collective-permute-start | bytes 1179656 | tf_op jit(solution)/shard_map/ppermute | solution.py:244
  158.3 1.9 collective-permute-start.9
  187.2 2.8 %collective-permute-start.25 = (bf16[256,1152]{1,0:T(8,128)(2,1)S(1)}, bf16[256,1152]{1,0:T(8,128)(2,1)S(1)}, u32[]{:S(2)}, u32[]{:S(2)}) collective-permute-start(bf16[256,1152]{1,0:T(8,128)(2,1)S(1)} %bitcast.26), channel_id=1, source_target_pairs={{0,16},{16,0},{1,17},{17,1},{2,18},{18,2},{3,19},{19,3},{4,20},{20... | collective-permute-start | bytes 1769480 | tf_op jit(solution)/shard_map/ppermute | solution.py:244
  187.2 2.8 %collective-permute-start.26 = (bf16[256,1024]{1,0:T(8,128)(2,1)S(1)}, bf16[256,1024]{1,0:T(8,128)(2,1)S(1)}, u32[]{:S(2)}, u32[]{:S(2)}) collective-permute-start(bf16[256,1024]{1,0:T(8,128)(2,1)S(1)} %bitcast.28), channel_id=1, source_target_pairs={{0,16},{16,0},{1,17},{17,1},{2,18},{18,2},{3,19},{19,3},{4,20},{20... | collective-permute-start | bytes 1572872 | tf_op jit(solution)/shard_map/ppermute | solution.py:244
  (24 other events, 257.6 us)

commit v4 on v3

--- a/solution.py
+++ b/solution.py
@@ -240,6 +240,24 @@
         head[:, 48 * e + 24 : 48 * e + 48] = t[64:128, 128:152]
 
 
+def halves_kernel(a, b, top, low):
+    top[...] = a[...]
+    low[...] = b[...]
+
+
+def halves(a, b):
+    shape = (a.shape[0] // 2, a.shape[1])
+    first = pl.BlockSpec(shape, lambda i: (0, 0))
+    return pl.pallas_call(
+        halves_kernel,
+        grid=(1,),
+        out_shape=[jax.ShapeDtypeStruct(shape, a.dtype)] * 2,
+        in_specs=[first, pl.BlockSpec(shape, lambda i: (1, 0))],
+        out_specs=[first, first],
+        name="halves",
+    )(a, b)
+
+
 def swap(x, axis):
     return lax.ppermute(x, axis, SWAP)
 
@@ -278,9 +296,9 @@
     xa0 = spread(piece, "z", 8).reshape(8 * ROWS, 384)
     xa1 = turn(xa0, "y", 4, 1)
     xa3 = turn(xa0, "y", 4, 3)
-    xa1, xa3 = lax.optimization_barrier((xa1, xa3))
-    xa2 = turn(xa1[: 4 * ROWS], "y", 4, 1)
-    xa2l = turn(xa3[4 * ROWS :], "y", 4, 3)
+    top, low = halves(xa1, xa3)
+    xa2 = turn(top, "y", 4, 1)
+    xa2l = turn(low, "y", 4, 3)
     xa = (xa0, xa1, xa2, xa2l, xa3)
     xb = tuple(swap(v, "c") for v in xa)
 

time: 221 us -> 223 us (level)
  Pallas kernels: 32.1 us -> 34.8 us
    ppermute x7, waiting for transfers between devices: 12.5 us -> 8.85 us  [turn(): return lax.ppermute(x, axis, [(k, (k - by) % n) for k in range(n)])]
    slice x2 -> x0, local copies, waits for them, and re-layouts: 3.38 us -> none  [the longest x1 1.7 us: inner(): xa2 = turn(xa1[:4 * ROWS], 'y', 4, 1)]
    unnamed x52 -> x56, local copies, waits for them, and re-layouts: 13.3 us -> 16.4 us
    ppermute x17, waiting for transfers between devices: 15.3 us -> 18.1 us  [swap(): return lax.ppermute(x, axis, SWAP)]
  transfers between devices with their start and end apart: 31 -> 31, of which waited for: 9 -> 8; matrix products, arithmetic and copies ran while one was open for 4% -> 2% of each run, Pallas kernels for 4% -> 5%
where the time goes in v4:
time: 223 us; the launch traced here: 221 us
  starting transfers between devices  81 us (36%)
  blocking collectives  43.3 us (19%)
  waiting for transfers between devices  37.4 us (17%)
  Pallas kernels  34.8 us (16%)
  local copies, waits for them, and re-layouts  19.8 us (9%)
  other arithmetic  3.19 us (1%)
    pallas_call x10, Pallas kernels, call(): pl.pallas_call(kernel, out_shape=shapes, in_specs=[SM] * scalar + [pl.Blo...  32.9 us
    ppermute x17, starting transfers between devices, swap(): return lax.ppermute(x, axis, SWAP)  27 us
    all_to_all x1, blocking collectives, inner(): grads = lax.all_to_all(grads, DP, 0, 0, tiled=True)  26 us
    ppermute x17, waiting for transfers between devices, swap(): return lax.ppermute(x, axis, SWAP)  18.1 us
    all_to_all x1, blocking collectives, inner(): lax.all_to_all(load, ('y', 'xh', 'xl'), 0, 0, tiled=True).reshape(256, 1152)  17.3 us
    unnamed x56, local copies, waits for them, and re-layouts  16.4 us
    ppermute x7, starting transfers between devices, turn(): return lax.ppermute(x, axis, [(k, (k - by) % n) for k in range(n)])  11.3 us
    ppermute x7, waiting for transfers between devices, turn(): return lax.ppermute(x, axis, [(k, (k - by) % n) for k in range(n)])  8.85 us
  transfers between devices with their start and end apart: 31, of which 8 were waited for; matrix products, arithmetic and copies ran while one was open for 2% of the time, Pallas kernels for 5%

profile of v4, /device:TPU:8, one launch (start us, length us, event | category | flops | bytes accessed | tf_op | source)
XLA Modules:
  0.0 221.1 jit_solution(5218630852969542980)
XLA Ops:
  2.3 3.4 %collective-permute-start.10 = (bf16[88,384]{1,0:T(8,128)(2,1)S(1)}, bf16[88,384]{1,0:T(8,128)(2,1)S(1)}, u32[]{:S(2)}, u32[]{:S(2)}) collective-permute-start(bf16[88,384]{1,0:T(8,128)(2,1)S(1)} %pad_select_fusion), channel_id=1, source_target_pairs={{0,1},{17,16},{2,3},{19,18},{4,5},{21,20},{6,7},{23,22},{8,9},{25,... | collective-permute-start | bytes 202760 | tf_op jit(solution)/shard_map/ppermute | solution.py:294
  5.8 1.9 collective-permute-done.10
  8.6 8.5 %all-to-all-start.1 = ((bf16[8,88,384]{2,1,0:T(8,128)(2,1)}), bf16[8,88,384]{2,1,0:T(8,128)(2,1)S(1)}, u32[]{:S(2)}, u32[]{:S(2)}) async-start(bf16[8,88,384]{2,1,0:T(8,128)(2,1)} %broadcast_in_dim.49), calls=%async_computation.1 | async-start | bytes 1081344 | tf_op jit(solution)/shard_map/all_to_all | solution.py:271
  18.0 5.9 %collective-permute-start.20 = (bf16[192,1536]{1,0:T(8,128)(2,1)}, bf16[192,1536]{1,0:T(8,128)(2,1)}, u32[]{:S(2)}, u32[]{:S(2)}) collective-permute-start(bf16[192,1536]{1,0:T(8,128)(2,1)} %slice_select_fusion), channel_id=1, source_target_pairs={{0,0},{1,3},{2,6},{3,9},{4,14},{5,1},{6,4},{7,7},{8,12},{9,15},{10... | collective-permute-start | bytes 1769480 | tf_op jit(solution)/shard_map/ppermute | solution.py:310
  24.9 1.8 slice_select_fusion.1
  26.7 3.1 %collective-permute-start.22 = (bf16[96,1536]{1,0:T(8,128)(2,1)}, bf16[96,1536]{1,0:T(8,128)(2,1)S(1)}, u32[]{:S(2)}, u32[]{:S(2)}) collective-permute-start(bf16[96,1536]{1,0:T(8,128)(2,1)} %slice_select_fusion.1), channel_id=1, source_target_pairs={{0,4},{1,5},{2,12},{3,13},{4,10},{5,11},{6,2},{7,3},{8,8},{9,9},{1... | collective-permute-start | bytes 884744 | tf_op jit(solution)/shard_map/ppermute | solution.py:311
  29.9 20.8 %collective-permute-start.21 = (bf16[192,1536]{1,0:T(8,128)(2,1)}, bf16[192,1536]{1,0:T(8,128)(2,1)}, u32[]{:S(2)}, u32[]{:S(2)}) collective-permute-start(bf16[192,1536]{1,0:T(8,128)(2,1)} %collective-permute-done.20.m_own), channel_id=1, source_target_pairs={{0,1},{1,0},{2,3},{3,2},{4,5},{5,4},{6,7},{7,6},{8,9},{9,8},{10,11... | collective-permute-start | bytes 1769480 | tf_op jit(solution)/shard_map/ppermute | solution.py:262
  53.6 1.6 collective-permute-start.12
  57.1 4.3 %shard_map.103 = (bf16[512,1024]{1,0:T(8,128)(2,1)S(1)}, f32[512,128]{1,0:T(8,128)S(1)}, bf16[512,128]{1,0:T(8,128)(2,1)S(1)}, f32[256,1024]{1,0:T(8,128)S(1)}, ...) custom-call(s32[6]{0:T(128)S(1)} %stack.27.s_ref, bf16[2,8,16,1024]{3,2,1,0:T(8,128)(2,1)S(1)} %bitcast.31, ...), custom_call_target="tpu_custom_call" | custom-call | flops 300000000 | bytes 4624408 | tf_op jit(solution)/shard_map/pallas_call | solution.py:87
  65.9 1.9 halves.1
  67.8 2.7 %collective-permute-start.13 = (bf16[352,384]{1,0:T(8,128)(2,1)}, bf16[352,384]{1,0:T(8,128)(2,1)}, u32[]{:S(2)}, u32[]{:S(2)}) collective-permute-start(bf16[352,384]{1,0:T(8,128)(2,1)} %get-tuple-element.25), channel_id=1, source_target_pairs={{0,192},{64,0},{128,64},{192,128},{1,193},{65,1},{129,65},{193,129... | collective-permute-start | bytes 811016 | tf_op jit(solution)/shard_map/ppermute | solution.py:266
  70.5 2.8 %collective-permute-done.23.h_oth = bf16[96,1536]{1,0:T(8,128)(2,1)} collective-permute-done((bf16[96,1536]{1,0:T(8,128)(2,1)S(1)}, bf16[96,1536]{1,0:T(8,128)(2,1)}, u32[]{:S(2)}, u32[]{:S(2)}) %collective-permute-start.23) | collective-permute-done | bytes 294944 | tf_op jit(solution)/shard_map/ppermute | solution.py:262
  77.5 8.3 %all-to-all-start = ((bf16[16,16,1024]{2,1,0:T(8,128)(2,1)}), bf16[16,16,1024]{2,1,0:T(8,128)(2,1)S(1)}, u32[]{:S(2)}, u32[]{:S(2)}) async-start(bf16[16,16,1024]{2,1,0:T(8,128)(2,1)} %bitcast.10), calls=%async_computation | async-start | bytes 1048576 | tf_op jit(solution)/shard_map/all_to_all | solution.py:330
  86.5 8.6 %all-to-all-done.keep = bf16[16,16,1024]{2,1,0:T(8,128)(2,1)S(1)} async-done(((bf16[16,16,1024]{2,1,0:T(8,128)(2,1)}), bf16[16,16,1024]{2,1,0:T(8,128)(2,1)S(1)}, u32[]{:S(2)}, u32[]{:S(2)}) %all-to-all-start) | async-done | bytes 524320 | tf_op jit(solution)/shard_map/all_to_all | solution.py:330
  98.0 15.8 %shard_map.108 = (f32[352,384]{1,0:T(8,128)S(1)}, f32[352,384]{1,0:T(8,128)}) custom-call(s32[6]{0:T(128)S(1)} %stack.27.s_ref, bf16[704,384]{1,0:T(8,128)(2,1)S(1)} %bitcast.35, bf16[704,384]{1,0:T(8,128)(2,1)S(1)} %copy-done.5, bf16[352,384]{1,0:T(8,128)(2,1)} %collective-permute-done.13.xa2, bf16[352,384]{1,0:T(8,128)(2,1)} %collective-permute-done.14.xa2l, ...), custom_call_target="tpu_custom_call" | custom-call | flops 6000000000 | bytes 7176216 | tf_op jit(solution)/shard_map/pallas_call | solution.py:87
  114.7 6.1 %all-to-all-start.2 = ((bf16[16,16,1024]{2,1,0:T(8,128)(2,1)}), bf16[16,16,1024]{2,1,0:T(8,128)(2,1)S(1)}, u32[]{:S(2)}, u32[]{:S(2)}) async-start(bf16[16,16,1024]{2,1,0:T(8,128)(2,1)} %copy-done.10), calls=%async_computation.2 | async-start | bytes 1048576 | tf_op jit(solution)/shard_map/all_to_all | solution.py:332
  120.7 3.1 %collective-permute-start.2 = (bf16[96,1024]{1,0:T(8,128)(2,1)S(1)}, bf16[96,1024]{1,0:T(8,128)(2,1)S(1)}, u32[]{:S(2)}, u32[]{:S(2)}) collective-permute-start(bf16[96,1024]{1,0:T(8,128)(2,1)S(1)} %bitcast.36), channel_id=1, source_target_pairs={{0,32},{32,0},{1,33},{33,1},{2,34},{34,2},{3,35},{35,3},{4,36},{36... | collective-permute-start | bytes 589832 | tf_op jit(solution)/shard_map/ppermute | solution.py:262
  123.8 11.1 %collective-permute-done.2.other = bf16[96,1024]{1,0:T(8,128)(2,1)S(1)} collective-permute-done((bf16[96,1024]{1,0:T(8,128)(2,1)S(1)}, bf16[96,1024]{1,0:T(8,128)(2,1)S(1)}, u32[]{:S(2)}, u32[]{:S(2)}) %collective-permute-start.2) | collective-permute-done | bytes 196640 | tf_op jit(solution)/shard_map/ppermute | solution.py:262
  136.7 2.4 %collective-permute-start.4 = (bf16[2,96,1024]{2,1,0:T(8,128)(2,1)S(1)}, bf16[2,96,1024]{2,1,0:T(8,128)(2,1)}, u32[]{:S(2)}, u32[]{:S(2)}) collective-permute-start(bf16[2,96,1024]{2,1,0:T(8,128)(2,1)S(1)} %shard_map.106.refs_0_), channel_id=1, source_target_pairs={{0,128},{64,192},{128,0},{192,64},{1,129},{65,193},{129,1},{193,65... | collective-permute-start | bytes 1179656 | tf_op jit(solution)/shard_map/ppermute | solution.py:266
  139.1 1.8 collective-permute-start.5
  142.0 1.7 shard_map.109
  143.7 7.4 %all-to-all-start.3 = ((bf16[64,8,384]{2,1,0:T(8,128)(2,1)}), bf16[64,8,384]{2,1,0:T(8,128)(2,1)S(1)}, u32[]{:S(2)}, u32[]{:S(2)}) async-start(bf16[64,8,384]{2,1,0:T(8,128)(2,1)} %shard_map.109), calls=%async_computation.3 | async-start | bytes 786432 | tf_op jit(solution)/shard_map/all_to_all | solution.py:360
  151.7 5.8 %collective-permute-done.4.refs_2_ = bf16[2,96,1024]{2,1,0:T(8,128)(2,1)} collective-permute-done((bf16[2,96,1024]{2,1,0:T(8,128)(2,1)S(1)}, bf16[2,96,1024]{2,1,0:T(8,128)(2,1)}, u32[]{:S(2)}, u32[]{:S(2)}) %collective-permute-start.4) | collective-permute-done | bytes 393248 | tf_op jit(solution)/shard_map/ppermute | solution.py:266
  157.6 3.0 %collective-permute-done.5.refs_3_ = bf16[2,96,1024]{2,1,0:T(8,128)(2,1)} collective-permute-done((bf16[2,96,1024]{2,1,0:T(8,128)(2,1)S(1)}, bf16[2,96,1024]{2,1,0:T(8,128)(2,1)}, u32[]{:S(2)}, u32[]{:S(2)}) %collective-permute-start.5) | collective-permute-done | bytes 393248 | tf_op jit(solution)/shard_map/ppermute | solution.py:266
  160.6 1.9 collective-permute-done.9.refs_7_
  162.5 2.4 %shard_map.107 = (bf16[1536,1024]{1,0:T(8,128)(2,1)S(1)}, f32[16,1536]{1,0:T(8,128)S(1)}) custom-call(s32[6]{0:T(128)S(1)} %copy-done.18, bf16[16,1024]{1,0:T(8,128)(2,1)S(1)} %get-tuple-element.22.so, bf16[2,96,1024]{2,1,0:T(8,128)(2,1)S(1)} %shard_map.106.refs_0_, bf16[2,96,1024]{2,1,0:T(8,128)(2,1)} %collective-permute-done.3.refs_1_, ...), custom_call_target="tpu_custom_call" | custom-call | bytes 6422552 | tf_op jit(solution)/shard_map/pallas_call | solution.py:87
  164.9 1.6 copy-done.1
  167.9 4.3 %shard_map.110 = bf16[16,16,1152]{2,1,0:T(8,128)(2,1)} custom-call(s32[6]{0:T(128)} %copy-done.17, bf16[1536,1024]{1,0:T(8,128)(2,1)} %copy-done.1, bf16[64,8,384]{2,1,0:T(8,128)(2,1)} %copy-done.24, f32[16,1536]{1,0:T(8,128)} %copy-done.16), custom_call_target="tpu_custom_call" | custom-call | bytes 4227096 | tf_op jit(solution)/shard_map/pallas_call | solution.py:87
  172.2 17.3 %all_to_all.30 = bf16[16,16,1152]{2,1,0:T(8,128)(2,1)S(1)} all-to-all(bf16[16,16,1152]{2,1,0:T(8,128)(2,1)} %shard_map.110), channel_id=1, replica_groups=mesh['y'=4,'xh'=2,'c'=2,'z'=8,'xl'=2] {'y','xh','xl'}, dimensions={0} | all-to-all | bytes 1179648 | tf_op jit(solution)/shard_map/all_to_all | solution.py:369
  190.0 2.2 %collective-permute-done.26.so_far = bf16[256,1024]{1,0:T(8,128)(2,1)S(1)} collective-permute-done((bf16[256,1024]{1,0:T(8,128)(2,1)S(1)}, bf16[256,1024]{1,0:T(8,128)(2,1)S(1)}, u32[]{:S(2)}, u32[]{:S(2)}) %collective-permute-start.26) | collective-permute-done | bytes 524320 | tf_op jit(solution)/shard_map/ppermute | solution.py:262
  192.3 2.0 shard_map.111
  194.2 26.0 %all_to_all.31.got = bf16[16,152,128]{2,1,0:T(8,128)(2,1)S(1)} all-to-all(bf16[16,152,128]{2,1,0:T(8,128)(2,1)S(1)} %shard_map.111), channel_id=1, replica_groups=mesh['y'=4,'xh'=2,'c'=2,'z'=8,'xl'=2] {'z','xl'}, dimensions={0} | all-to-all | bytes 1245184 | tf_op jit(solution)/shard_map/all_to_all | solution.py:375
  (116 shorter events, 27.8 us)
Async XLA Ops:
  2.3 5.3 %collective-permute-start.10 = (bf16[88,384]{1,0:T(8,128)(2,1)S(1)}, bf16[88,384]{1,0:T(8,128)(2,1)S(1)}, u32[]{:S(2)}, u32[]{:S(2)}) collective-permute-start(bf16[88,384]{1,0:T(8,128)(2,1)S(1)} %pad_select_fusion), channel_id=1, source_target_pairs={{0,1},{17,16},{2,3},{19,18},{4,5},{21,20},{6,7},{23,22},{8,9},{25,... | collective-permute-start | bytes 202760 | tf_op jit(solution)/shard_map/ppermute | solution.py:294
  8.6 44.5 %all-to-all-start.1 = ((bf16[8,88,384]{2,1,0:T(8,128)(2,1)}), bf16[8,88,384]{2,1,0:T(8,128)(2,1)S(1)}, u32[]{:S(2)}, u32[]{:S(2)}) async-start(bf16[8,88,384]{2,1,0:T(8,128)(2,1)} %broadcast_in_dim.49), calls=%async_computation.1 | async-start | bytes 1081344 | tf_op jit(solution)/shard_map/all_to_all | solution.py:271
  18.0 11.9 %collective-permute-start.20 = (bf16[192,1536]{1,0:T(8,128)(2,1)}, bf16[192,1536]{1,0:T(8,128)(2,1)}, u32[]{:S(2)}, u32[]{:S(2)}) collective-permute-start(bf16[192,1536]{1,0:T(8,128)(2,1)} %slice_select_fusion), channel_id=1, source_target_pairs={{0,0},{1,3},{2,6},{3,9},{4,14},{5,1},{6,4},{7,7},{8,12},{9,15},{10... | collective-permute-start | bytes 1769480 | tf_op jit(solution)/shard_map/ppermute | solution.py:310
  24.5 30.7 %collective-permute-start = (bf16[2,8,16,1024]{3,2,1,0:T(8,128)(2,1)S(1)}, bf16[2,8,16,1024]{3,2,1,0:T(8,128)(2,1)S(1)}, u32[]{:S(2)}, u32[]{:S(2)}) collective-permute-start(bf16[2,8,16,1024]{3,2,1,0:T(8,128)(2,1)S(1)} %bitcast.30), channel_id=1, source_target_pairs={{0,1},{1,0},{2,3},{3,2},{4,5},{5,4},{6,7},{7,6},{8,9},{9,8},{10,11... | collective-permute-start | bytes 1572872 | tf_op jit(solution)/shard_map/ppermute | solution.py:262
  26.7 37.1 %collective-permute-start.22 = (bf16[96,1536]{1,0:T(8,128)(2,1)}, bf16[96,1536]{1,0:T(8,128)(2,1)S(1)}, u32[]{:S(2)}, u32[]{:S(2)}) collective-permute-start(bf16[96,1536]{1,0:T(8,128)(2,1)} %slice_select_fusion.1), channel_id=1, source_target_pairs={{0,4},{1,5},{2,12},{3,13},{4,10},{5,11},{6,2},{7,3},{8,8},{9,9},{1... | collective-permute-start | bytes 884744 | tf_op jit(solution)/shard_map/ppermute | solution.py:311
  29.9 45.0 %collective-permute-start.21 = (bf16[192,1536]{1,0:T(8,128)(2,1)}, bf16[192,1536]{1,0:T(8,128)(2,1)}, u32[]{:S(2)}, u32[]{:S(2)}) collective-permute-start(bf16[192,1536]{1,0:T(8,128)(2,1)} %collective-permute-done.20.m_own), channel_id=1, source_target_pairs={{0,1},{1,0},{2,3},{3,2},{4,5},{5,4},{6,7},{7,6},{8,9},{9,8},{10,11... | collective-permute-start | bytes 1769480 | tf_op jit(solution)/shard_map/ppermute | solution.py:262
  53.1 42.9 %copy-start.17 = (s32[6]{0:T(128)}, s32[6]{0:T(128)S(1)}, u32[]{:S(2)}) copy-start(s32[6]{0:T(128)S(1)} %stack.27.s_ref) | copy-start | bytes 76
  53.1 11.4 %collective-permute-start.11 = (bf16[704,384]{1,0:T(8,128)(2,1)S(1)}, bf16[704,384]{1,0:T(8,128)(2,1)S(1)}, u32[]{:S(2)}, u32[]{:S(2)}) collective-permute-start(bf16[704,384]{1,0:T(8,128)(2,1)S(1)} %bitcast.32), channel_id=1, source_target_pairs={{0,192},{64,0},{128,64},{192,128},{1,193},{65,1},{129,65},{193,129... | collective-permute-start | bytes 1622024 | tf_op jit(solution)/shard_map/ppermute | solution.py:266
  53.6 12.3 %collective-permute-start.12 = (bf16[704,384]{1,0:T(8,128)(2,1)S(1)}, bf16[704,384]{1,0:T(8,128)(2,1)}, u32[]{:S(2)}, u32[]{:S(2)}) collective-permute-start(bf16[704,384]{1,0:T(8,128)(2,1)S(1)} %bitcast.33), channel_id=1, source_target_pairs={{0,64},{64,128},{128,192},{192,0},{1,65},{65,129},{129,193},{193,1... | collective-permute-start | bytes 1622024 | tf_op jit(solution)/shard_map/ppermute | solution.py:266
  63.8 11.1 %collective-permute-start.1 = (bf16[256,1024]{1,0:T(8,128)(2,1)}, bf16[256,1024]{1,0:T(8,128)(2,1)S(1)}, u32[]{:S(2)}, u32[]{:S(2)}) collective-permute-start(bf16[256,1024]{1,0:T(8,128)(2,1)} %get-tuple-element.20), channel_id=1, source_target_pairs={{0,16},{16,0},{1,17},{17,1},{2,18},{18,2},{3,19},{19,3},{4,20},{20... | collective-permute-start | bytes 1572872 | tf_op jit(solution)/shard_map/ppermute | solution.py:262
  63.8 9.5 %collective-permute-start.23 = (bf16[96,1536]{1,0:T(8,128)(2,1)S(1)}, bf16[96,1536]{1,0:T(8,128)(2,1)}, u32[]{:S(2)}, u32[]{:S(2)}) collective-permute-start(bf16[96,1536]{1,0:T(8,128)(2,1)S(1)} %collective-permute-done.22.h_own), channel_id=1, source_target_pairs={{0,1},{1,0},{2,3},{3,2},{4,5},{5,4},{6,7},{7,6},{8,9},{9,8},{10,11... | collective-permute-start | bytes 884744 | tf_op jit(solution)/shard_map/ppermute | solution.py:262
  65.4 30.6 %collective-permute-start.15 = (bf16[704,384]{1,0:T(8,128)(2,1)S(1)}, bf16[704,384]{1,0:T(8,128)(2,1)}, u32[]{:S(2)}, u32[]{:S(2)}) collective-permute-start(bf16[704,384]{1,0:T(8,128)(2,1)S(1)} %bitcast.34), channel_id=1, source_target_pairs={{0,16},{16,0},{1,17},{17,1},{2,18},{18,2},{3,19},{19,3},{4,20},{20... | collective-permute-start | bytes 1622024 | tf_op jit(solution)/shard_map/ppermute | solution.py:262
  67.8 18.1 %collective-permute-start.13 = (bf16[352,384]{1,0:T(8,128)(2,1)}, bf16[352,384]{1,0:T(8,128)(2,1)}, u32[]{:S(2)}, u32[]{:S(2)}) collective-permute-start(bf16[352,384]{1,0:T(8,128)(2,1)} %get-tuple-element.25), channel_id=1, source_target_pairs={{0,192},{64,0},{128,64},{192,128},{1,193},{65,1},{129,65},{193,129... | collective-permute-start | bytes 811016 | tf_op jit(solution)/shard_map/ppermute | solution.py:266
  73.3 12.6 %collective-permute-start.14 = (bf16[352,384]{1,0:T(8,128)(2,1)}, bf16[352,384]{1,0:T(8,128)(2,1)}, u32[]{:S(2)}, u32[]{:S(2)}) collective-permute-start(bf16[352,384]{1,0:T(8,128)(2,1)} %get-tuple-element.26), channel_id=1, source_target_pairs={{0,64},{64,128},{128,192},{192,0},{1,65},{65,129},{129,193},{193,1... | collective-permute-start | bytes 811016 | tf_op jit(solution)/shard_map/ppermute | solution.py:266
  74.9 21.1 %collective-permute-start.16 = (bf16[704,384]{1,0:T(8,128)(2,1)}, bf16[704,384]{1,0:T(8,128)(2,1)}, u32[]{:S(2)}, u32[]{:S(2)}) collective-permute-start(bf16[704,384]{1,0:T(8,128)(2,1)} %copy-done.4), channel_id=1, source_target_pairs={{0,16},{16,0},{1,17},{17,1},{2,18},{18,2},{3,19},{19,3},{4,20},{20... | collective-permute-start | bytes 1622024 | tf_op jit(solution)/shard_map/ppermute | solution.py:262
  74.9 21.1 %collective-permute-start.19 = (bf16[704,384]{1,0:T(8,128)(2,1)}, bf16[704,384]{1,0:T(8,128)(2,1)}, u32[]{:S(2)}, u32[]{:S(2)}) collective-permute-start(bf16[704,384]{1,0:T(8,128)(2,1)} %collective-permute-done.12.b.xa3), channel_id=1, source_target_pairs={{0,16},{16,0},{1,17},{17,1},{2,18},{18,2},{3,19},{19,3},{4,20},{20... | collective-permute-start | bytes 1622024 | tf_op jit(solution)/shard_map/ppermute | solution.py:262
  77.5 17.5 %all-to-all-start = ((bf16[16,16,1024]{2,1,0:T(8,128)(2,1)}), bf16[16,16,1024]{2,1,0:T(8,128)(2,1)S(1)}, u32[]{:S(2)}, u32[]{:S(2)}) async-start(bf16[16,16,1024]{2,1,0:T(8,128)(2,1)} %bitcast.10), calls=%async_computation | async-start | bytes 1048576 | tf_op jit(solution)/shard_map/all_to_all | solution.py:330
  85.9 10.1 %collective-permute-start.17 = (bf16[352,384]{1,0:T(8,128)(2,1)}, bf16[352,384]{1,0:T(8,128)(2,1)}, u32[]{:S(2)}, u32[]{:S(2)}) collective-permute-start(bf16[352,384]{1,0:T(8,128)(2,1)} %collective-permute-done.13.xa2), channel_id=1, source_target_pairs={{0,16},{16,0},{1,17},{17,1},{2,18},{18,2},{3,19},{19,3},{4,20},{20... | collective-permute-start | bytes 811016 | tf_op jit(solution)/shard_map/ppermute | solution.py:262
  86.0 10.0 %collective-permute-start.18 = (bf16[352,384]{1,0:T(8,128)(2,1)}, bf16[352,384]{1,0:T(8,128)(2,1)}, u32[]{:S(2)}, u32[]{:S(2)}) collective-permute-start(bf16[352,384]{1,0:T(8,128)(2,1)} %collective-permute-done.14.xa2l), channel_id=1, source_target_pairs={{0,16},{16,0},{1,17},{17,1},{2,18},{18,2},{3,19},{19,3},{4,20},{20... | collective-permute-start | bytes 811016 | tf_op jit(solution)/shard_map/ppermute | solution.py:262
  114.7 26.3 %collective-permute-start.24 = (f32[352,384]{1,0:T(8,128)}, f32[352,384]{1,0:T(8,128)S(1)}, u32[]{:S(2)}, u32[]{:S(2)}) collective-permute-start(f32[352,384]{1,0:T(8,128)} %get-tuple-element.28), channel_id=1, source_target_pairs={{0,16},{16,0},{1,17},{17,1},{2,18},{18,2},{3,19},{19,3},{4,20},{20... | collective-permute-start | bytes 1622024 | tf_op jit(solution)/shard_map/ppermute | solution.py:262
  114.7 29.1 %all-to-all-start.2 = ((bf16[16,16,1024]{2,1,0:T(8,128)(2,1)}), bf16[16,16,1024]{2,1,0:T(8,128)(2,1)S(1)}, u32[]{:S(2)}, u32[]{:S(2)}) async-start(bf16[16,16,1024]{2,1,0:T(8,128)(2,1)} %copy-done.10), calls=%async_computation.2 | async-start | bytes 1048576 | tf_op jit(solution)/shard_map/all_to_all | solution.py:332
  120.7 14.1 %collective-permute-start.2 = (bf16[96,1024]{1,0:T(8,128)(2,1)S(1)}, bf16[96,1024]{1,0:T(8,128)(2,1)S(1)}, u32[]{:S(2)}, u32[]{:S(2)}) collective-permute-start(bf16[96,1024]{1,0:T(8,128)(2,1)S(1)} %bitcast.36), channel_id=1, source_target_pairs={{0,32},{32,0},{1,33},{33,1},{2,34},{34,2},{3,35},{35,3},{4,36},{36... | collective-permute-start | bytes 589832 | tf_op jit(solution)/shard_map/ppermute | solution.py:262
  136.1 15.1 %collective-permute-start.3 = (bf16[2,96,1024]{2,1,0:T(8,128)(2,1)S(1)}, bf16[2,96,1024]{2,1,0:T(8,128)(2,1)}, u32[]{:S(2)}, u32[]{:S(2)}) collective-permute-start(bf16[2,96,1024]{2,1,0:T(8,128)(2,1)S(1)} %shard_map.106.refs_0_), channel_id=1, source_target_pairs={{0,192},{64,0},{128,64},{192,128},{1,193},{65,1},{129,65},{193,129... | collective-permute-start | bytes 1179656 | tf_op jit(solution)/shard_map/ppermute | solution.py:266
  136.7 20.8 %collective-permute-start.4 = (bf16[2,96,1024]{2,1,0:T(8,128)(2,1)S(1)}, bf16[2,96,1024]{2,1,0:T(8,128)(2,1)}, u32[]{:S(2)}, u32[]{:S(2)}) collective-permute-start(bf16[2,96,1024]{2,1,0:T(8,128)(2,1)S(1)} %shard_map.106.refs_0_), channel_id=1, source_target_pairs={{0,128},{64,192},{128,0},{192,64},{1,129},{65,193},{129,1},{193,65... | collective-permute-start | bytes 1179656 | tf_op jit(solution)/shard_map/ppermute | solution.py:266
  139.1 21.4 %collective-permute-start.5 = (bf16[2,96,1024]{2,1,0:T(8,128)(2,1)S(1)}, bf16[2,96,1024]{2,1,0:T(8,128)(2,1)}, u32[]{:S(2)}, u32[]{:S(2)}) collective-permute-start(bf16[2,96,1024]{2,1,0:T(8,128)(2,1)S(1)} %shard_map.106.refs_0_), channel_id=1, source_target_pairs={{0,64},{64,128},{128,192},{192,0},{1,65},{65,129},{129,193},{193,1... | collective-permute-start | bytes 1179656 | tf_op jit(solution)/shard_map/ppermute | solution.py:266
  143.7 23.4 %all-to-all-start.3 = ((bf16[64,8,384]{2,1,0:T(8,128)(2,1)}), bf16[64,8,384]{2,1,0:T(8,128)(2,1)S(1)}, u32[]{:S(2)}, u32[]{:S(2)}) async-start(bf16[64,8,384]{2,1,0:T(8,128)(2,1)} %shard_map.109), calls=%async_computation.3 | async-start | bytes 786432 | tf_op jit(solution)/shard_map/all_to_all | solution.py:360
  151.1 9.4 %collective-permute-start.6 = (bf16[2,96,1024]{2,1,0:T(8,128)(2,1)S(1)}, bf16[2,96,1024]{2,1,0:T(8,128)(2,1)S(1)}, u32[]{:S(2)}, u32[]{:S(2)}) collective-permute-start(bf16[2,96,1024]{2,1,0:T(8,128)(2,1)S(1)} %shard_map.106.refs_0_), channel_id=1, source_target_pairs={{0,16},{16,0},{1,17},{17,1},{2,18},{18,2},{3,19},{19,3},{4,20},{20... | collective-permute-start | bytes 1179656 | tf_op jit(solution)/shard_map/ppermute | solution.py:262
  151.2 9.3 %collective-permute-start.7 = (bf16[2,96,1024]{2,1,0:T(8,128)(2,1)}, bf16[2,96,1024]{2,1,0:T(8,128)(2,1)S(1)}, u32[]{:S(2)}, u32[]{:S(2)}) collective-permute-start(bf16[2,96,1024]{2,1,0:T(8,128)(2,1)} %collective-permute-done.3.refs_1_), channel_id=1, source_target_pairs={{0,16},{16,0},{1,17},{17,1},{2,18},{18,2},{3,19},{19,3},{4,20},{20... | collective-permute-start | bytes 1179656 | tf_op jit(solution)/shard_map/ppermute | solution.py:262
  157.6 3.0 %collective-permute-start.8 = (bf16[2,96,1024]{2,1,0:T(8,128)(2,1)}, bf16[2,96,1024]{2,1,0:T(8,128)(2,1)S(1)}, u32[]{:S(2)}, u32[]{:S(2)}) collective-permute-start(bf16[2,96,1024]{2,1,0:T(8,128)(2,1)} %collective-permute-done.4.refs_2_), channel_id=1, source_target_pairs={{0,16},{16,0},{1,17},{17,1},{2,18},{18,2},{3,19},{19,3},{4,20},{20... | collective-permute-start | bytes 1179656 | tf_op jit(solution)/shard_map/ppermute | solution.py:262
  160.6 1.9 collective-permute-start.9
  189.5 2.8 %collective-permute-start.25 = (bf16[256,1152]{1,0:T(8,128)(2,1)S(1)}, bf16[256,1152]{1,0:T(8,128)(2,1)S(1)}, u32[]{:S(2)}, u32[]{:S(2)}) collective-permute-start(bf16[256,1152]{1,0:T(8,128)(2,1)S(1)} %bitcast.26), channel_id=1, source_target_pairs={{0,16},{16,0},{1,17},{17,1},{2,18},{18,2},{3,19},{19,3},{4,20},{20... | collective-permute-start | bytes 1769480 | tf_op jit(solution)/shard_map/ppermute | solution.py:262
  189.5 2.8 %collective-permute-start.26 = (bf16[256,1024]{1,0:T(8,128)(2,1)S(1)}, bf16[256,1024]{1,0:T(8,128)(2,1)S(1)}, u32[]{:S(2)}, u32[]{:S(2)}) collective-permute-start(bf16[256,1024]{1,0:T(8,128)(2,1)S(1)} %bitcast.28), channel_id=1, source_target_pairs={{0,16},{16,0},{1,17},{17,1},{2,18},{18,2},{3,19},{19,3},{4,20},{20... | collective-permute-start | bytes 1572872 | tf_op jit(solution)/shard_map/ppermute | solution.py:262
  (26 other events, 230.8 us)

commit v5 on v4

--- a/solution.py
+++ b/solution.py
@@ -143,10 +143,11 @@
 
 def pack_kernel(own, got, out, a0, a1, b0, b1, mid):
     total = own[...] + got[...]
-    a0[...] = total[:, 0:128]
-    a1[:, 0:64] = total[:, 128:192]
-    b0[...] = total[:, 192:320]
-    b1[:, 0:64] = total[:, 320:384]
+    n = total.shape[0]
+    a0[0:n, :] = total[:, 0:128]
+    a1[0:n, 0:64] = total[:, 128:192]
+    b0[0:n, :] = total[:, 192:320]
+    b1[0:n, 0:64] = total[:, 320:384]
     mid[...] = jnp.zeros_like(mid)
 
     @pl.loop(0, 8)
@@ -354,7 +355,7 @@
     got = swap(oth, "c")
     (both,) = call(
         pack_kernel, [((64, 8, 384), BF)], own, got,
-        scratch=[pltpu.VMEM((half // 2, 128), F32)] * 4 + [pltpu.VMEM((64, 8, 384), F32)],
+        scratch=[pltpu.VMEM((half // 2 + 48, 128), F32)] * 4 + [pltpu.VMEM((64, 8, 384), F32)],
     )
     both = after(both, so_own)
     sums = lax.all_to_all(both, ("y", "xh", "z"), 0, 0, tiled=True)

time: 223 us -> 223 us (level)
  no operation moved by 1% of the time
where the time goes in v5:
time: 223 us; the launch traced here: 221 us
  starting transfers between devices  81 us (36%)
  blocking collectives  43.3 us (19%)
  waiting for transfers between devices  37.4 us (17%)
  Pallas kernels  34.8 us (16%)
  local copies, waits for them, and re-layouts  19.8 us (9%)
  other arithmetic  3.19 us (1%)
    pallas_call x10, Pallas kernels, call(): pl.pallas_call(kernel, out_shape=shapes, in_specs=[SM] * scalar + [pl.Blo...  32.9 us
    ppermute x17, starting transfers between devices, swap(): return lax.ppermute(x, axis, SWAP)  27 us
    all_to_all x1, blocking collectives, inner(): grads = lax.all_to_all(grads, DP, 0, 0, tiled=True)  26 us
    ppermute x17, waiting for transfers between devices, swap(): return lax.ppermute(x, axis, SWAP)  18.1 us
    all_to_all x1, blocking collectives, inner(): lax.all_to_all(load, ('y', 'xh', 'xl'), 0, 0, tiled=True).reshape(256, 1152)  17.3 us
    unnamed x56, local copies, waits for them, and re-layouts  16.4 us
    ppermute x7, starting transfers between devices, turn(): return lax.ppermute(x, axis, [(k, (k - by) % n) for k in range(n)])  11.3 us
    ppermute x7, waiting for transfers between devices, turn(): return lax.ppermute(x, axis, [(k, (k - by) % n) for k in range(n)])  8.85 us
  transfers between devices with their start and end apart: 31, of which 8 were waited for; matrix products, arithmetic and copies ran while one was open for 2% of the time, Pallas kernels for 5%

profile of v5, /device:TPU:8, one launch (start us, length us, event | category | flops | bytes accessed | tf_op | source)
XLA Modules:
  0.0 221.1 jit_solution(3406501202645907442)
XLA Ops:
  2.3 3.4 %collective-permute-start.10 = (bf16[88,384]{1,0:T(8,128)(2,1)S(1)}, bf16[88,384]{1,0:T(8,128)(2,1)S(1)}, u32[]{:S(2)}, u32[]{:S(2)}) collective-permute-start(bf16[88,384]{1,0:T(8,128)(2,1)S(1)} %pad_select_fusion), channel_id=1, source_target_pairs={{0,1},{17,16},{2,3},{19,18},{4,5},{21,20},{6,7},{23,22},{8,9},{25,... | collective-permute-start | bytes 202760 | tf_op jit(solution)/shard_map/ppermute | solution.py:295
  5.8 1.9 collective-permute-done.10
  8.6 8.5 %all-to-all-start.1 = ((bf16[8,88,384]{2,1,0:T(8,128)(2,1)}), bf16[8,88,384]{2,1,0:T(8,128)(2,1)S(1)}, u32[]{:S(2)}, u32[]{:S(2)}) async-start(bf16[8,88,384]{2,1,0:T(8,128)(2,1)} %broadcast_in_dim.49), calls=%async_computation.1 | async-start | bytes 1081344 | tf_op jit(solution)/shard_map/all_to_all | solution.py:272
  18.0 5.9 %collective-permute-start.20 = (bf16[192,1536]{1,0:T(8,128)(2,1)}, bf16[192,1536]{1,0:T(8,128)(2,1)}, u32[]{:S(2)}, u32[]{:S(2)}) collective-permute-start(bf16[192,1536]{1,0:T(8,128)(2,1)} %slice_select_fusion), channel_id=1, source_target_pairs={{0,0},{1,3},{2,6},{3,9},{4,14},{5,1},{6,4},{7,7},{8,12},{9,15},{10... | collective-permute-start | bytes 1769480 | tf_op jit(solution)/shard_map/ppermute | solution.py:311
  24.9 1.8 slice_select_fusion.1
  26.7 3.1 %collective-permute-start.22 = (bf16[96,1536]{1,0:T(8,128)(2,1)}, bf16[96,1536]{1,0:T(8,128)(2,1)S(1)}, u32[]{:S(2)}, u32[]{:S(2)}) collective-permute-start(bf16[96,1536]{1,0:T(8,128)(2,1)} %slice_select_fusion.1), channel_id=1, source_target_pairs={{0,4},{1,5},{2,12},{3,13},{4,10},{5,11},{6,2},{7,3},{8,8},{9,9},{1... | collective-permute-start | bytes 884744 | tf_op jit(solution)/shard_map/ppermute | solution.py:312
  29.9 20.8 %collective-permute-start.21 = (bf16[192,1536]{1,0:T(8,128)(2,1)}, bf16[192,1536]{1,0:T(8,128)(2,1)}, u32[]{:S(2)}, u32[]{:S(2)}) collective-permute-start(bf16[192,1536]{1,0:T(8,128)(2,1)} %collective-permute-done.20.m_own), channel_id=1, source_target_pairs={{0,1},{1,0},{2,3},{3,2},{4,5},{5,4},{6,7},{7,6},{8,9},{9,8},{10,11... | collective-permute-start | bytes 1769480 | tf_op jit(solution)/shard_map/ppermute | solution.py:263
  53.6 1.6 collective-permute-start.12
  57.1 4.3 %shard_map.103 = (bf16[512,1024]{1,0:T(8,128)(2,1)S(1)}, f32[512,128]{1,0:T(8,128)S(1)}, bf16[512,128]{1,0:T(8,128)(2,1)S(1)}, f32[256,1024]{1,0:T(8,128)S(1)}, ...) custom-call(s32[6]{0:T(128)S(1)} %stack.27.s_ref, bf16[2,8,16,1024]{3,2,1,0:T(8,128)(2,1)S(1)} %bitcast.31, ...), custom_call_target="tpu_custom_call" | custom-call | flops 300000000 | bytes 4624408 | tf_op jit(solution)/shard_map/pallas_call | solution.py:87
  65.9 1.9 halves.1
  67.8 2.7 %collective-permute-start.13 = (bf16[352,384]{1,0:T(8,128)(2,1)}, bf16[352,384]{1,0:T(8,128)(2,1)}, u32[]{:S(2)}, u32[]{:S(2)}) collective-permute-start(bf16[352,384]{1,0:T(8,128)(2,1)} %get-tuple-element.25), channel_id=1, source_target_pairs={{0,192},{64,0},{128,64},{192,128},{1,193},{65,1},{129,65},{193,129... | collective-permute-start | bytes 811016 | tf_op jit(solution)/shard_map/ppermute | solution.py:267
  70.5 2.8 %collective-permute-done.23.h_oth = bf16[96,1536]{1,0:T(8,128)(2,1)} collective-permute-done((bf16[96,1536]{1,0:T(8,128)(2,1)S(1)}, bf16[96,1536]{1,0:T(8,128)(2,1)}, u32[]{:S(2)}, u32[]{:S(2)}) %collective-permute-start.23) | collective-permute-done | bytes 294944 | tf_op jit(solution)/shard_map/ppermute | solution.py:263
  77.5 8.3 %all-to-all-start = ((bf16[16,16,1024]{2,1,0:T(8,128)(2,1)}), bf16[16,16,1024]{2,1,0:T(8,128)(2,1)S(1)}, u32[]{:S(2)}, u32[]{:S(2)}) async-start(bf16[16,16,1024]{2,1,0:T(8,128)(2,1)} %bitcast.10), calls=%async_computation | async-start | bytes 1048576 | tf_op jit(solution)/shard_map/all_to_all | solution.py:331
  86.5 8.6 %all-to-all-done.keep = bf16[16,16,1024]{2,1,0:T(8,128)(2,1)S(1)} async-done(((bf16[16,16,1024]{2,1,0:T(8,128)(2,1)}), bf16[16,16,1024]{2,1,0:T(8,128)(2,1)S(1)}, u32[]{:S(2)}, u32[]{:S(2)}) %all-to-all-start) | async-done | bytes 524320 | tf_op jit(solution)/shard_map/all_to_all | solution.py:331
  98.0 15.8 %shard_map.108 = (f32[352,384]{1,0:T(8,128)S(1)}, f32[352,384]{1,0:T(8,128)}) custom-call(s32[6]{0:T(128)S(1)} %stack.27.s_ref, bf16[704,384]{1,0:T(8,128)(2,1)S(1)} %bitcast.35, bf16[704,384]{1,0:T(8,128)(2,1)S(1)} %copy-done.5, bf16[352,384]{1,0:T(8,128)(2,1)} %collective-permute-done.13.xa2, bf16[352,384]{1,0:T(8,128)(2,1)} %collective-permute-done.14.xa2l, ...), custom_call_target="tpu_custom_call" | custom-call | flops 6000000000 | bytes 7176216 | tf_op jit(solution)/shard_map/pallas_call | solution.py:87
  114.7 6.1 %all-to-all-start.2 = ((bf16[16,16,1024]{2,1,0:T(8,128)(2,1)}), bf16[16,16,1024]{2,1,0:T(8,128)(2,1)S(1)}, u32[]{:S(2)}, u32[]{:S(2)}) async-start(bf16[16,16,1024]{2,1,0:T(8,128)(2,1)} %copy-done.10), calls=%async_computation.2 | async-start | bytes 1048576 | tf_op jit(solution)/shard_map/all_to_all | solution.py:333
  120.7 3.1 %collective-permute-start.2 = (bf16[96,1024]{1,0:T(8,128)(2,1)S(1)}, bf16[96,1024]{1,0:T(8,128)(2,1)S(1)}, u32[]{:S(2)}, u32[]{:S(2)}) collective-permute-start(bf16[96,1024]{1,0:T(8,128)(2,1)S(1)} %bitcast.36), channel_id=1, source_target_pairs={{0,32},{32,0},{1,33},{33,1},{2,34},{34,2},{3,35},{35,3},{4,36},{36... | collective-permute-start | bytes 589832 | tf_op jit(solution)/shard_map/ppermute | solution.py:263
  123.8 11.1 %collective-permute-done.2.other = bf16[96,1024]{1,0:T(8,128)(2,1)S(1)} collective-permute-done((bf16[96,1024]{1,0:T(8,128)(2,1)S(1)}, bf16[96,1024]{1,0:T(8,128)(2,1)S(1)}, u32[]{:S(2)}, u32[]{:S(2)}) %collective-permute-start.2) | collective-permute-done | bytes 196640 | tf_op jit(solution)/shard_map/ppermute | solution.py:263
  136.7 2.4 %collective-permute-start.4 = (bf16[2,96,1024]{2,1,0:T(8,128)(2,1)S(1)}, bf16[2,96,1024]{2,1,0:T(8,128)(2,1)}, u32[]{:S(2)}, u32[]{:S(2)}) collective-permute-start(bf16[2,96,1024]{2,1,0:T(8,128)(2,1)S(1)} %shard_map.106.refs_0_), channel_id=1, source_target_pairs={{0,128},{64,192},{128,0},{192,64},{1,129},{65,193},{129,1},{193,65... | collective-permute-start | bytes 1179656 | tf_op jit(solution)/shard_map/ppermute | solution.py:267
  139.1 1.8 collective-permute-start.5
  142.0 1.7 shard_map.109
  143.7 7.4 %all-to-all-start.3 = ((bf16[64,8,384]{2,1,0:T(8,128)(2,1)}), bf16[64,8,384]{2,1,0:T(8,128)(2,1)S(1)}, u32[]{:S(2)}, u32[]{:S(2)}) async-start(bf16[64,8,384]{2,1,0:T(8,128)(2,1)} %shard_map.109), calls=%async_computation.3 | async-start | bytes 786432 | tf_op jit(solution)/shard_map/all_to_all | solution.py:361
  151.7 5.8 %collective-permute-done.4.refs_2_ = bf16[2,96,1024]{2,1,0:T(8,128)(2,1)} collective-permute-done((bf16[2,96,1024]{2,1,0:T(8,128)(2,1)S(1)}, bf16[2,96,1024]{2,1,0:T(8,128)(2,1)}, u32[]{:S(2)}, u32[]{:S(2)}) %collective-permute-start.4) | collective-permute-done | bytes 393248 | tf_op jit(solution)/shard_map/ppermute | solution.py:267
  157.6 3.0 %collective-permute-done.5.refs_3_ = bf16[2,96,1024]{2,1,0:T(8,128)(2,1)} collective-permute-done((bf16[2,96,1024]{2,1,0:T(8,128)(2,1)S(1)}, bf16[2,96,1024]{2,1,0:T(8,128)(2,1)}, u32[]{:S(2)}, u32[]{:S(2)}) %collective-permute-start.5) | collective-permute-done | bytes 393248 | tf_op jit(solution)/shard_map/ppermute | solution.py:267
  160.6 1.9 collective-permute-done.9.refs_7_
  162.5 2.4 %shard_map.107 = (bf16[1536,1024]{1,0:T(8,128)(2,1)S(1)}, f32[16,1536]{1,0:T(8,128)S(1)}) custom-call(s32[6]{0:T(128)S(1)} %copy-done.18, bf16[16,1024]{1,0:T(8,128)(2,1)S(1)} %get-tuple-element.22.so, bf16[2,96,1024]{2,1,0:T(8,128)(2,1)S(1)} %shard_map.106.refs_0_, bf16[2,96,1024]{2,1,0:T(8,128)(2,1)} %collective-permute-done.3.refs_1_, ...), custom_call_target="tpu_custom_call" | custom-call | bytes 6422552 | tf_op jit(solution)/shard_map/pallas_call | solution.py:87
  164.9 1.6 copy-done.1
  167.9 4.3 %shard_map.110 = bf16[16,16,1152]{2,1,0:T(8,128)(2,1)} custom-call(s32[6]{0:T(128)} %copy-done.17, bf16[1536,1024]{1,0:T(8,128)(2,1)} %copy-done.1, bf16[64,8,384]{2,1,0:T(8,128)(2,1)} %copy-done.24, f32[16,1536]{1,0:T(8,128)} %copy-done.16), custom_call_target="tpu_custom_call" | custom-call | bytes 4227096 | tf_op jit(solution)/shard_map/pallas_call | solution.py:87
  172.2 17.3 %all_to_all.30 = bf16[16,16,1152]{2,1,0:T(8,128)(2,1)S(1)} all-to-all(bf16[16,16,1152]{2,1,0:T(8,128)(2,1)} %shard_map.110), channel_id=1, replica_groups=mesh['y'=4,'xh'=2,'c'=2,'z'=8,'xl'=2] {'y','xh','xl'}, dimensions={0} | all-to-all | bytes 1179648 | tf_op jit(solution)/shard_map/all_to_all | solution.py:370
  190.0 2.2 %collective-permute-done.26.so_far = bf16[256,1024]{1,0:T(8,128)(2,1)S(1)} collective-permute-done((bf16[256,1024]{1,0:T(8,128)(2,1)S(1)}, bf16[256,1024]{1,0:T(8,128)(2,1)S(1)}, u32[]{:S(2)}, u32[]{:S(2)}) %collective-permute-start.26) | collective-permute-done | bytes 524320 | tf_op jit(solution)/shard_map/ppermute | solution.py:263
  192.3 2.0 shard_map.111
  194.2 26.0 %all_to_all.31.got = bf16[16,152,128]{2,1,0:T(8,128)(2,1)S(1)} all-to-all(bf16[16,152,128]{2,1,0:T(8,128)(2,1)S(1)} %shard_map.111), channel_id=1, replica_groups=mesh['y'=4,'xh'=2,'c'=2,'z'=8,'xl'=2] {'z','xl'}, dimensions={0} | all-to-all | bytes 1245184 | tf_op jit(solution)/shard_map/all_to_all | solution.py:376
  (116 shorter events, 27.8 us)
Async XLA Ops:
  2.3 5.3 %collective-permute-start.10 = (bf16[88,384]{1,0:T(8,128)(2,1)S(1)}, bf16[88,384]{1,0:T(8,128)(2,1)S(1)}, u32[]{:S(2)}, u32[]{:S(2)}) collective-permute-start(bf16[88,384]{1,0:T(8,128)(2,1)S(1)} %pad_select_fusion), channel_id=1, source_target_pairs={{0,1},{17,16},{2,3},{19,18},{4,5},{21,20},{6,7},{23,22},{8,9},{25,... | collective-permute-start | bytes 202760 | tf_op jit(solution)/shard_map/ppermute | solution.py:295
  8.6 44.5 %all-to-all-start.1 = ((bf16[8,88,384]{2,1,0:T(8,128)(2,1)}), bf16[8,88,384]{2,1,0:T(8,128)(2,1)S(1)}, u32[]{:S(2)}, u32[]{:S(2)}) async-start(bf16[8,88,384]{2,1,0:T(8,128)(2,1)} %broadcast_in_dim.49), calls=%async_computation.1 | async-start | bytes 1081344 | tf_op jit(solution)/shard_map/all_to_all | solution.py:272
  18.0 11.9 %collective-permute-start.20 = (bf16[192,1536]{1,0:T(8,128)(2,1)}, bf16[192,1536]{1,0:T(8,128)(2,1)}, u32[]{:S(2)}, u32[]{:S(2)}) collective-permute-start(bf16[192,1536]{1,0:T(8,128)(2,1)} %slice_select_fusion), channel_id=1, source_target_pairs={{0,0},{1,3},{2,6},{3,9},{4,14},{5,1},{6,4},{7,7},{8,12},{9,15},{10... | collective-permute-start | bytes 1769480 | tf_op jit(solution)/shard_map/ppermute | solution.py:311
  24.5 30.7 %collective-permute-start = (bf16[2,8,16,1024]{3,2,1,0:T(8,128)(2,1)S(1)}, bf16[2,8,16,1024]{3,2,1,0:T(8,128)(2,1)S(1)}, u32[]{:S(2)}, u32[]{:S(2)}) collective-permute-start(bf16[2,8,16,1024]{3,2,1,0:T(8,128)(2,1)S(1)} %bitcast.30), channel_id=1, source_target_pairs={{0,1},{1,0},{2,3},{3,2},{4,5},{5,4},{6,7},{7,6},{8,9},{9,8},{10,11... | collective-permute-start | bytes 1572872 | tf_op jit(solution)/shard_map/ppermute | solution.py:263
  26.7 37.1 %collective-permute-start.22 = (bf16[96,1536]{1,0:T(8,128)(2,1)}, bf16[96,1536]{1,0:T(8,128)(2,1)S(1)}, u32[]{:S(2)}, u32[]{:S(2)}) collective-permute-start(bf16[96,1536]{1,0:T(8,128)(2,1)} %slice_select_fusion.1), channel_id=1, source_target_pairs={{0,4},{1,5},{2,12},{3,13},{4,10},{5,11},{6,2},{7,3},{8,8},{9,9},{1... | collective-permute-start | bytes 884744 | tf_op jit(solution)/shard_map/ppermute | solution.py:312
  29.9 45.0 %collective-permute-start.21 = (bf16[192,1536]{1,0:T(8,128)(2,1)}, bf16[192,1536]{1,0:T(8,128)(2,1)}, u32[]{:S(2)}, u32[]{:S(2)}) collective-permute-start(bf16[192,1536]{1,0:T(8,128)(2,1)} %collective-permute-done.20.m_own), channel_id=1, source_target_pairs={{0,1},{1,0},{2,3},{3,2},{4,5},{5,4},{6,7},{7,6},{8,9},{9,8},{10,11... | collective-permute-start | bytes 1769480 | tf_op jit(solution)/shard_map/ppermute | solution.py:263
  53.1 42.9 %copy-start.17 = (s32[6]{0:T(128)}, s32[6]{0:T(128)S(1)}, u32[]{:S(2)}) copy-start(s32[6]{0:T(128)S(1)} %stack.27.s_ref) | copy-start | bytes 76
  53.1 11.4 %collective-permute-start.11 = (bf16[704,384]{1,0:T(8,128)(2,1)S(1)}, bf16[704,384]{1,0:T(8,128)(2,1)S(1)}, u32[]{:S(2)}, u32[]{:S(2)}) collective-permute-start(bf16[704,384]{1,0:T(8,128)(2,1)S(1)} %bitcast.32), channel_id=1, source_target_pairs={{0,192},{64,0},{128,64},{192,128},{1,193},{65,1},{129,65},{193,129... | collective-permute-start | bytes 1622024 | tf_op jit(solution)/shard_map/ppermute | solution.py:267
  53.6 12.3 %collective-permute-start.12 = (bf16[704,384]{1,0:T(8,128)(2,1)S(1)}, bf16[704,384]{1,0:T(8,128)(2,1)}, u32[]{:S(2)}, u32[]{:S(2)}) collective-permute-start(bf16[704,384]{1,0:T(8,128)(2,1)S(1)} %bitcast.33), channel_id=1, source_target_pairs={{0,64},{64,128},{128,192},{192,0},{1,65},{65,129},{129,193},{193,1... | collective-permute-start | bytes 1622024 | tf_op jit(solution)/shard_map/ppermute | solution.py:267
  63.8 11.1 %collective-permute-start.1 = (bf16[256,1024]{1,0:T(8,128)(2,1)}, bf16[256,1024]{1,0:T(8,128)(2,1)S(1)}, u32[]{:S(2)}, u32[]{:S(2)}) collective-permute-start(bf16[256,1024]{1,0:T(8,128)(2,1)} %get-tuple-element.20), channel_id=1, source_target_pairs={{0,16},{16,0},{1,17},{17,1},{2,18},{18,2},{3,19},{19,3},{4,20},{20... | collective-permute-start | bytes 1572872 | tf_op jit(solution)/shard_map/ppermute | solution.py:263
  63.8 9.5 %collective-permute-start.23 = (bf16[96,1536]{1,0:T(8,128)(2,1)S(1)}, bf16[96,1536]{1,0:T(8,128)(2,1)}, u32[]{:S(2)}, u32[]{:S(2)}) collective-permute-start(bf16[96,1536]{1,0:T(8,128)(2,1)S(1)} %collective-permute-done.22.h_own), channel_id=1, source_target_pairs={{0,1},{1,0},{2,3},{3,2},{4,5},{5,4},{6,7},{7,6},{8,9},{9,8},{10,11... | collective-permute-start | bytes 884744 | tf_op jit(solution)/shard_map/ppermute | solution.py:263
  65.4 30.6 %collective-permute-start.15 = (bf16[704,384]{1,0:T(8,128)(2,1)S(1)}, bf16[704,384]{1,0:T(8,128)(2,1)}, u32[]{:S(2)}, u32[]{:S(2)}) collective-permute-start(bf16[704,384]{1,0:T(8,128)(2,1)S(1)} %bitcast.34), channel_id=1, source_target_pairs={{0,16},{16,0},{1,17},{17,1},{2,18},{18,2},{3,19},{19,3},{4,20},{20... | collective-permute-start | bytes 1622024 | tf_op jit(solution)/shard_map/ppermute | solution.py:263
  67.8 18.1 %collective-permute-start.13 = (bf16[352,384]{1,0:T(8,128)(2,1)}, bf16[352,384]{1,0:T(8,128)(2,1)}, u32[]{:S(2)}, u32[]{:S(2)}) collective-permute-start(bf16[352,384]{1,0:T(8,128)(2,1)} %get-tuple-element.25), channel_id=1, source_target_pairs={{0,192},{64,0},{128,64},{192,128},{1,193},{65,1},{129,65},{193,129... | collective-permute-start | bytes 811016 | tf_op jit(solution)/shard_map/ppermute | solution.py:267
  73.3 12.6 %collective-permute-start.14 = (bf16[352,384]{1,0:T(8,128)(2,1)}, bf16[352,384]{1,0:T(8,128)(2,1)}, u32[]{:S(2)}, u32[]{:S(2)}) collective-permute-start(bf16[352,384]{1,0:T(8,128)(2,1)} %get-tuple-element.26), channel_id=1, source_target_pairs={{0,64},{64,128},{128,192},{192,0},{1,65},{65,129},{129,193},{193,1... | collective-permute-start | bytes 811016 | tf_op jit(solution)/shard_map/ppermute | solution.py:267
  74.9 21.1 %collective-permute-start.16 = (bf16[704,384]{1,0:T(8,128)(2,1)}, bf16[704,384]{1,0:T(8,128)(2,1)}, u32[]{:S(2)}, u32[]{:S(2)}) collective-permute-start(bf16[704,384]{1,0:T(8,128)(2,1)} %copy-done.4), channel_id=1, source_target_pairs={{0,16},{16,0},{1,17},{17,1},{2,18},{18,2},{3,19},{19,3},{4,20},{20... | collective-permute-start | bytes 1622024 | tf_op jit(solution)/shard_map/ppermute | solution.py:263
  74.9 21.1 %collective-permute-start.19 = (bf16[704,384]{1,0:T(8,128)(2,1)}, bf16[704,384]{1,0:T(8,128)(2,1)}, u32[]{:S(2)}, u32[]{:S(2)}) collective-permute-start(bf16[704,384]{1,0:T(8,128)(2,1)} %collective-permute-done.12.b.xa3), channel_id=1, source_target_pairs={{0,16},{16,0},{1,17},{17,1},{2,18},{18,2},{3,19},{19,3},{4,20},{20... | collective-permute-start | bytes 1622024 | tf_op jit(solution)/shard_map/ppermute | solution.py:263
  77.5 17.5 %all-to-all-start = ((bf16[16,16,1024]{2,1,0:T(8,128)(2,1)}), bf16[16,16,1024]{2,1,0:T(8,128)(2,1)S(1)}, u32[]{:S(2)}, u32[]{:S(2)}) async-start(bf16[16,16,1024]{2,1,0:T(8,128)(2,1)} %bitcast.10), calls=%async_computation | async-start | bytes 1048576 | tf_op jit(solution)/shard_map/all_to_all | solution.py:331
  85.9 10.1 %collective-permute-start.17 = (bf16[352,384]{1,0:T(8,128)(2,1)}, bf16[352,384]{1,0:T(8,128)(2,1)}, u32[]{:S(2)}, u32[]{:S(2)}) collective-permute-start(bf16[352,384]{1,0:T(8,128)(2,1)} %collective-permute-done.13.xa2), channel_id=1, source_target_pairs={{0,16},{16,0},{1,17},{17,1},{2,18},{18,2},{3,19},{19,3},{4,20},{20... | collective-permute-start | bytes 811016 | tf_op jit(solution)/shard_map/ppermute | solution.py:263
  86.0 10.0 %collective-permute-start.18 = (bf16[352,384]{1,0:T(8,128)(2,1)}, bf16[352,384]{1,0:T(8,128)(2,1)}, u32[]{:S(2)}, u32[]{:S(2)}) collective-permute-start(bf16[352,384]{1,0:T(8,128)(2,1)} %collective-permute-done.14.xa2l), channel_id=1, source_target_pairs={{0,16},{16,0},{1,17},{17,1},{2,18},{18,2},{3,19},{19,3},{4,20},{20... | collective-permute-start | bytes 811016 | tf_op jit(solution)/shard_map/ppermute | solution.py:263
  114.7 26.3 %collective-permute-start.24 = (f32[352,384]{1,0:T(8,128)}, f32[352,384]{1,0:T(8,128)S(1)}, u32[]{:S(2)}, u32[]{:S(2)}) collective-permute-start(f32[352,384]{1,0:T(8,128)} %get-tuple-element.28), channel_id=1, source_target_pairs={{0,16},{16,0},{1,17},{17,1},{2,18},{18,2},{3,19},{19,3},{4,20},{20... | collective-permute-start | bytes 1622024 | tf_op jit(solution)/shard_map/ppermute | solution.py:263
  114.7 29.1 %all-to-all-start.2 = ((bf16[16,16,1024]{2,1,0:T(8,128)(2,1)}), bf16[16,16,1024]{2,1,0:T(8,128)(2,1)S(1)}, u32[]{:S(2)}, u32[]{:S(2)}) async-start(bf16[16,16,1024]{2,1,0:T(8,128)(2,1)} %copy-done.10), calls=%async_computation.2 | async-start | bytes 1048576 | tf_op jit(solution)/shard_map/all_to_all | solution.py:333
  120.7 14.1 %collective-permute-start.2 = (bf16[96,1024]{1,0:T(8,128)(2,1)S(1)}, bf16[96,1024]{1,0:T(8,128)(2,1)S(1)}, u32[]{:S(2)}, u32[]{:S(2)}) collective-permute-start(bf16[96,1024]{1,0:T(8,128)(2,1)S(1)} %bitcast.36), channel_id=1, source_target_pairs={{0,32},{32,0},{1,33},{33,1},{2,34},{34,2},{3,35},{35,3},{4,36},{36... | collective-permute-start | bytes 589832 | tf_op jit(solution)/shard_map/ppermute | solution.py:263
  136.1 15.1 %collective-permute-start.3 = (bf16[2,96,1024]{2,1,0:T(8,128)(2,1)S(1)}, bf16[2,96,1024]{2,1,0:T(8,128)(2,1)}, u32[]{:S(2)}, u32[]{:S(2)}) collective-permute-start(bf16[2,96,1024]{2,1,0:T(8,128)(2,1)S(1)} %shard_map.106.refs_0_), channel_id=1, source_target_pairs={{0,192},{64,0},{128,64},{192,128},{1,193},{65,1},{129,65},{193,129... | collective-permute-start | bytes 1179656 | tf_op jit(solution)/shard_map/ppermute | solution.py:267
  136.7 20.8 %collective-permute-start.4 = (bf16[2,96,1024]{2,1,0:T(8,128)(2,1)S(1)}, bf16[2,96,1024]{2,1,0:T(8,128)(2,1)}, u32[]{:S(2)}, u32[]{:S(2)}) collective-permute-start(bf16[2,96,1024]{2,1,0:T(8,128)(2,1)S(1)} %shard_map.106.refs_0_), channel_id=1, source_target_pairs={{0,128},{64,192},{128,0},{192,64},{1,129},{65,193},{129,1},{193,65... | collective-permute-start | bytes 1179656 | tf_op jit(solution)/shard_map/ppermute | solution.py:267
  139.1 21.4 %collective-permute-start.5 = (bf16[2,96,1024]{2,1,0:T(8,128)(2,1)S(1)}, bf16[2,96,1024]{2,1,0:T(8,128)(2,1)}, u32[]{:S(2)}, u32[]{:S(2)}) collective-permute-start(bf16[2,96,1024]{2,1,0:T(8,128)(2,1)S(1)} %shard_map.106.refs_0_), channel_id=1, source_target_pairs={{0,64},{64,128},{128,192},{192,0},{1,65},{65,129},{129,193},{193,1... | collective-permute-start | bytes 1179656 | tf_op jit(solution)/shard_map/ppermute | solution.py:267
  143.7 23.4 %all-to-all-start.3 = ((bf16[64,8,384]{2,1,0:T(8,128)(2,1)}), bf16[64,8,384]{2,1,0:T(8,128)(2,1)S(1)}, u32[]{:S(2)}, u32[]{:S(2)}) async-start(bf16[64,8,384]{2,1,0:T(8,128)(2,1)} %shard_map.109), calls=%async_computation.3 | async-start | bytes 786432 | tf_op jit(solution)/shard_map/all_to_all | solution.py:361
  151.1 9.4 %collective-permute-start.6 = (bf16[2,96,1024]{2,1,0:T(8,128)(2,1)S(1)}, bf16[2,96,1024]{2,1,0:T(8,128)(2,1)S(1)}, u32[]{:S(2)}, u32[]{:S(2)}) collective-permute-start(bf16[2,96,1024]{2,1,0:T(8,128)(2,1)S(1)} %shard_map.106.refs_0_), channel_id=1, source_target_pairs={{0,16},{16,0},{1,17},{17,1},{2,18},{18,2},{3,19},{19,3},{4,20},{20... | collective-permute-start | bytes 1179656 | tf_op jit(solution)/shard_map/ppermute | solution.py:263
  151.2 9.3 %collective-permute-start.7 = (bf16[2,96,1024]{2,1,0:T(8,128)(2,1)}, bf16[2,96,1024]{2,1,0:T(8,128)(2,1)S(1)}, u32[]{:S(2)}, u32[]{:S(2)}) collective-permute-start(bf16[2,96,1024]{2,1,0:T(8,128)(2,1)} %collective-permute-done.3.refs_1_), channel_id=1, source_target_pairs={{0,16},{16,0},{1,17},{17,1},{2,18},{18,2},{3,19},{19,3},{4,20},{20... | collective-permute-start | bytes 1179656 | tf_op jit(solution)/shard_map/ppermute | solution.py:263
  157.6 3.0 %collective-permute-start.8 = (bf16[2,96,1024]{2,1,0:T(8,128)(2,1)}, bf16[2,96,1024]{2,1,0:T(8,128)(2,1)S(1)}, u32[]{:S(2)}, u32[]{:S(2)}) collective-permute-start(bf16[2,96,1024]{2,1,0:T(8,128)(2,1)} %collective-permute-done.4.refs_2_), channel_id=1, source_target_pairs={{0,16},{16,0},{1,17},{17,1},{2,18},{18,2},{3,19},{19,3},{4,20},{20... | collective-permute-start | bytes 1179656 | tf_op jit(solution)/shard_map/ppermute | solution.py:263
  160.6 1.9 collective-permute-start.9
  189.5 2.8 %collective-permute-start.25 = (bf16[256,1152]{1,0:T(8,128)(2,1)S(1)}, bf16[256,1152]{1,0:T(8,128)(2,1)S(1)}, u32[]{:S(2)}, u32[]{:S(2)}) collective-permute-start(bf16[256,1152]{1,0:T(8,128)(2,1)S(1)} %bitcast.26), channel_id=1, source_target_pairs={{0,16},{16,0},{1,17},{17,1},{2,18},{18,2},{3,19},{19,3},{4,20},{20... | collective-permute-start | bytes 1769480 | tf_op jit(solution)/shard_map/ppermute | solution.py:263
  189.5 2.8 %collective-permute-start.26 = (bf16[256,1024]{1,0:T(8,128)(2,1)S(1)}, bf16[256,1024]{1,0:T(8,128)(2,1)S(1)}, u32[]{:S(2)}, u32[]{:S(2)}) collective-permute-start(bf16[256,1024]{1,0:T(8,128)(2,1)S(1)} %bitcast.28), channel_id=1, source_target_pairs={{0,16},{16,0},{1,17},{17,1},{2,18},{18,2},{3,19},{19,3},{4,20},{20... | collective-permute-start | bytes 1572872 | tf_op jit(solution)/shard_map/ppermute | solution.py:263
  (26 other events, 230.8 us)
